TPU v7x, 32 devices: a whole 2x2x4 slice. The times are simulated.
32 devices in a mesh: dp: 8 (over z, y), mp: 4 (over x, core).
Axes of the slice: x: 2, y: 2, z: 4, core: 2. Of those that a mesh axis runs over, the one named last changes fastest.
Arguments:
- tokens: bfloat16 [1024, 16384], P('dp', 'mp'), may hold values from -6 to 6
- cotangent: bfloat16 [1024, 16384], P('dp', 'mp'), may hold values from -6 to 6
- up_right: bfloat16 [2, 128, 128, 128], P(None, 'mp'), may hold values from -0.5 to 0.5
- up_left: bfloat16 [2, 128, 128, 128], P(None, 'mp'), may hold values from -0.5 to 0.5
- down_first_factor: bfloat16 [2, 128, 128, 128], P(None, 'mp'), may hold values from -0.5 to 0.5
- down_left: bfloat16 [2, 128, 128, 128], P(None, 'mp'), may hold values from -0.5 to 0.5
Outputs:
- mixed: bfloat16 [1024, 16384], P('dp', 'mp')
- tokens_grad: bfloat16 [1024, 16384], P('dp', 'mp')
- grad_up_right: float32 [2, 128, 128, 128], P(None, 'mp', 'dp')
- grad_up_left: float32 [2, 128, 128, 128], P(None, 'mp', 'dp')
- grad_down_right: float32 [2, 128, 128, 128], P(None, 'mp', 'dp')
- grad_down_left: float32 [2, 128, 128, 128], P(None, 'mp', 'dp')
All inputs are finite; a program needn't handle non-finite values.
Results may differ from a plain program's by a relative error of at most 0.01.
Values may be sent and summed in bfloat16 or wider, within the bound.
A program may use at most 128 MiB of HBM per device.

v0:
```python
import jax
import jax.numpy as jnp
from jax import lax
from jax.sharding import PartitionSpec as P

gelu_root = 0.7978845608
gelu_cube = 0.044715


def gelu_value(pre_values):
    inner_arg = gelu_root * (pre_values + gelu_cube * pre_values * pre_values * pre_values)
    return 0.5 * pre_values * (1.0 + jnp.tanh(inner_arg))


def gelu_slope(pre_values):
    inner_arg = gelu_root * (pre_values + gelu_cube * pre_values * pre_values * pre_values)
    tanh_term = jnp.tanh(inner_arg)
    return 0.5 * (1.0 + tanh_term) + 0.5 * pre_values * (
        1.0 - tanh_term * tanh_term
    ) * gelu_root * (1.0 + 3.0 * gelu_cube * pre_values * pre_values)


def partner_cross(panel_data, split_dim, concat_dim):
    return lax.all_to_all(panel_data, "mp", split_dim, concat_dim, tiled=True)


def forward_cross(panel_data, work_fn):
    return work_fn(partner_cross(panel_data, 2, 1))


def backward_cross(panel_data, work_fn):
    return work_fn(partner_cross(panel_data, 1, 2))


def body(tokens, cotangent, up_right, up_left, down_first_factor, down_left):
    tok_rows = tokens.shape[0]
    blocks_here = up_right.shape[1]
    block_width = up_right.shape[2]
    inputs = tokens.reshape(tok_rows, blocks_here, block_width)
    upstream = cotangent.reshape(tok_rows, blocks_here, block_width)
    right_panel = jnp.einsum(
        "tij,qijc->qict", inputs, up_right, preferred_element_type=jnp.float32
    ).astype(jnp.bfloat16)

    def up_work(crossed):
        return (
            crossed,
            jnp.einsum("qact,qcab->qcbt", crossed, up_left, preferred_element_type=jnp.float32),
        )

    crossed_up, preactivation_values = forward_cross(right_panel, up_work)
    hidden = gelu_value(preactivation_values).astype(jnp.bfloat16)
    down_panel = jnp.einsum(
        "qcat,qcae->qcet", hidden, down_first_factor, preferred_element_type=jnp.float32
    ).astype(jnp.bfloat16)

    def down_work(crossed):
        return (
            crossed,
            jnp.einsum("qcet,qecf->eft", crossed, down_left, preferred_element_type=jnp.float32)[
                None
            ],
        )

    crossed_down, summed = forward_cross(down_panel, down_work)
    mixed = jnp.transpose(summed[0], (2, 0, 1)).reshape(tok_rows, -1).astype(jnp.bfloat16)
    grad_down_left = jnp.einsum(
        "qcet,tef->qecf", crossed_down, upstream, preferred_element_type=jnp.float32
    )
    back_panel = jnp.einsum(
        "tef,qecf->qcet", upstream, down_left, preferred_element_type=jnp.float32
    ).astype(jnp.bfloat16)

    def down_back(crossed):
        return (
            crossed,
            jnp.einsum(
                "qcet,qcae->qcat", crossed, down_first_factor, preferred_element_type=jnp.float32
            ),
        )

    down_grad, hidden_grad = backward_cross(back_panel, down_back)
    grad_down_right = jnp.einsum(
        "qcat,qcet->qcae", hidden, down_grad, preferred_element_type=jnp.float32
    )
    grad_scale = (lax.axis_size("dp") * tok_rows) ** (-0.5)
    preactivation_gradient = (hidden_grad * gelu_slope(preactivation_values)).astype(jnp.bfloat16)
    grad_up_left = jnp.einsum(
        "qact,qcbt->qcab", crossed_up, preactivation_gradient, preferred_element_type=jnp.float32
    )
    up_back_panel = jnp.einsum(
        "qcbt,qcab->qact", preactivation_gradient, up_left, preferred_element_type=jnp.float32
    ).astype(jnp.bfloat16)

    def up_back(crossed):
        return (
            crossed,
            jnp.einsum("qict,qijc->ijt", crossed, up_right, preferred_element_type=jnp.float32)[
                None
            ],
        )

    right_factor_gradient, input_grad = backward_cross(up_back_panel, up_back)
    grad_up_right = jnp.einsum(
        "tij,qict->qijc", inputs, right_factor_gradient, preferred_element_type=jnp.float32
    )
    tokens_grad = jnp.transpose(input_grad[0], (2, 0, 1)).reshape(tok_rows, -1).astype(jnp.bfloat16)
    reduced = (
        lax.psum_scatter(
            grad_up_right.astype(jnp.bfloat16), "dp", scatter_dimension=2, tiled=True
        ).astype(jnp.float32),
        lax.psum_scatter(
            grad_up_left.astype(jnp.bfloat16), "dp", scatter_dimension=2, tiled=True
        ).astype(jnp.float32),
        lax.psum_scatter(
            grad_down_right.astype(jnp.bfloat16), "dp", scatter_dimension=2, tiled=True
        ).astype(jnp.float32),
        lax.psum_scatter(
            grad_down_left.astype(jnp.bfloat16), "dp", scatter_dimension=2, tiled=True
        ).astype(jnp.float32),
    )
    return (
        mixed,
        tokens_grad,
        reduced[0] * grad_scale,
        reduced[1] * grad_scale,
        reduced[2] * grad_scale,
        reduced[3] * grad_scale,
    )


def solution(mesh):
    in_specs = (
        P("dp", "mp"),
        P("dp", "mp"),
        P(None, "mp", None, None),
        P(None, "mp", None, None),
        P(None, "mp", None, None),
        P(None, "mp", None, None),
    )
    out_specs = (
        P("dp", "mp"),
        P("dp", "mp"),
        P(None, "mp", "dp", None),
        P(None, "mp", "dp", None),
        P(None, "mp", "dp", None),
        P(None, "mp", "dp", None),
    )
    return jax.shard_map(body, mesh=mesh, in_specs=in_specs, out_specs=out_specs, check_vma=False)
```

profile of v0, /device:TPU:0, one launch (start us, length us, event | category | flops | bytes accessed | tf_op | source)
XLA Modules:
  0.0 374.9 jit_solution(15483309474980769913)
XLA Ops:
  7.2 1.6 copy.155
  8.8 1.0 copy-done.6
  9.8 0.8 convert_bitcast_fusion.3
  10.6 3.5 copy.108
  14.1 4.5 %all-to-all-start.2 = ((bf16[2,128,32,128]{3,0,2,1:T(2,128)(2,1)}), bf16[2,128,32,128]{3,0,2,1:T(2,128)(2,1)}, u32[]{:S(2)}, u32[]{:S(2)}) async-start(bf16[2,128,32,128]{3,0,2,1:T(2,128)(2,1)} %copy.108), calls=%async_computation.2 | async-start | bytes 4194304 | tf_op jit(solution)/shard_map/all_to_all | solution.py:24
  18.6 1.6 copy.154
  20.5 0.9 convert_bitcast_fusion.5
  21.4 3.5 copy.98
  24.9 20.0 %all-to-all-done.2 = bf16[2,128,32,128]{3,0,2,1:T(2,128)(2,1)} async-done(((bf16[2,128,32,128]{3,0,2,1:T(2,128)(2,1)}), bf16[2,128,32,128]{3,0,2,1:T(2,128)(2,1)}, u32[]{:S(2)}, u32[]{:S(2)}) %all-to-all-start.2) | async-done | bytes 2097184 | tf_op jit(solution)/shard_map/all_to_all | solution.py:24
  44.9 4.5 %all-to-all-start = ((bf16[2,32,128,128]{3,0,1,2:T(2,128)(2,1)}), bf16[2,32,128,128]{3,0,1,2:T(2,128)(2,1)}, u32[]{:S(2)}, u32[]{:S(2)}) async-start(bf16[2,32,128,128]{3,0,1,2:T(2,128)(2,1)} %copy.98), calls=%async_computation | async-start | bytes 4194304 | tf_op jit(solution)/shard_map/all_to_all | solution.py:24
  49.6 1.9 copy.109
  51.6 2.0 copy.110
  53.5 21.6 %all-to-all-done = bf16[2,32,128,128]{3,0,1,2:T(2,128)(2,1)} async-done(((bf16[2,32,128,128]{3,0,1,2:T(2,128)(2,1)}), bf16[2,32,128,128]{3,0,1,2:T(2,128)(2,1)}, u32[]{:S(2)}, u32[]{:S(2)}) %all-to-all-start) | async-done | bytes 2097184 | tf_op jit(solution)/shard_map/all_to_all | solution.py:24
  75.2 2.9 copy.99
  78.5 1.7 copy-done.9
  80.3 0.9 fusion.13
  81.8 1.7 convolution_convert_fusion
  83.6 2.7 copy.122
  86.6 6.2 %fusion.6 = bf16[2,32,128,128]{2,3,1,0:T(8,128)(2,1)S(1)} fusion(f32[2,32,128,128]{3,2,1,0:T(8,128)} %copy-done.12, bf16[2,32,128,128]{3,2,1,0:T(8,128)(2,1)} %bitcast.94, bf16[2,32,128,128]{3,2,1,0:T(8,128)(2,1)S(1)} %copy-done), kind=kOutput, calls=%fused_computation.8 | convolution fusion | flops 288358400 | bytes 10485760 | tf_op jit(solution)/shard_map/qcet,qcae->qcat/dot_general | solution.py:77
  92.9 1.3 convolution_convert_fusion.1
  94.2 2.7 copy.120
  97.0 5.0 %convert_bitcast_fusion.4 = bf16[2,32,128,128]{2,3,1,0:T(8,128)(2,1)} fusion(bf16[2,32,128,128]{3,2,1,0:T(8,128)(2,1)S(1)} %copy-done, f32[2,32,128,128]{3,2,1,0:T(8,128)} %copy-done.12), kind=kOutput, calls=%fused_computation.17 | convolution fusion | flops 278921216 | bytes 8388608 | tf_op jit(solution)/shard_map/qcat,qcae->qcet/dot_general | solution.py:53
  102.0 3.5 copy.102
  105.5 28.2 %all_to_all.72 = bf16[2,32,128,128]{3,1,0,2:T(8,128)(2,1)S(1)} all-to-all(bf16[2,32,128,128]{3,1,0,2:T(8,128)(2,1)S(1)} %copy.102), channel_id=1, replica_groups=mesh['dp'=8,'mp'=4] {'mp'}, dimensions={2} | all-to-all | bytes 4194304 | tf_op jit(solution)/shard_map/all_to_all | solution.py:24
  134.2 0.7 copy-done.7
  134.9 0.9 convert_bitcast_fusion
  135.8 2.7 copy.124
  138.6 5.1 %convert_bitcast_fusion.2 = bf16[2,128,32,128]{1,3,2,0:T(8,128)(2,1)} fusion(bf16[2,32,128,128]{2,3,1,0:T(8,128)(2,1)} %copy-done.8, bf16[2,32,128,128]{3,2,1,0:T(8,128)(2,1)} %param.9), kind=kOutput, calls=%fused_computation.15 | convolution fusion | flops 269484032 | bytes 6291456 | tf_op jit(solution)/shard_map/qcbt,qcab->qact/dot_general | solution.py:91
  143.7 4.6 %copy.112 = bf16[2,128,32,128]{3,2,0,1:T(8,128)(2,1)} copy(bf16[2,128,32,128]{1,3,2,0:T(8,128)(2,1)} %convert_bitcast_fusion.2) | data formatting | bytes 4194304 | tf_op jit(solution)/shard_map/convert_element_type | solution.py:93
  148.3 29.5 %all_to_all.73 = bf16[2,128,32,128]{3,2,0,1:T(8,128)(2,1)S(1)} all-to-all(bf16[2,128,32,128]{3,2,0,1:T(8,128)(2,1)} %copy.112), channel_id=1, replica_groups=mesh['dp'=8,'mp'=4] {'mp'}, dimensions={1} | all-to-all | bytes 4194304 | tf_op jit(solution)/shard_map/all_to_all | solution.py:24
  178.4 1.4 copy-done.4
  179.8 2.2 convert_bitcast_fusion.1
  182.0 4.5 %copy.117 = bf16[2,32,128,128]{3,1,0,2:T(8,128)(2,1)} copy(bf16[2,32,128,128]{2,3,0,1:T(8,128)(2,1)} %convert_bitcast_fusion.1) | data formatting | bytes 4194304 | tf_op jit(solution)/shard_map/convert_element_type | solution.py:110
  186.5 2.4 bitcast_convert_fusion.1
  188.9 1.3 copy.125
  190.9 2.3 bitcast_convert_fusion
  193.2 1.3 copy.126
  194.5 1.0 convert_multiply_fusion.1
  195.6 1.1 copy.129
  196.7 28.9 %reduce-scatter.7.cloned.1.call-done = bf16[2,32,16,128]{3,1,0,2:T(8,128)(2,1)} async-done(((bf16[2,32,128,128]{3,1,0,2:T(8,128)(2,1)}), bf16[2,32,16,128]{3,1,0,2:T(8,128)(2,1)}) %reduce-scatter.7.cloned.1.call-update) | async-done | bytes 262160 | tf_op jit(solution)/shard_map/reduce_scatter | solution.py:112
  225.6 1.0 convert_multiply_fusion.2
  226.6 1.1 copy.128
  227.7 68.1 %reduce-scatter.11.cloned.1.call-done = bf16[2,32,16,128]{3,1,0,2:T(8,128)(2,1)} async-done(((bf16[2,32,128,128]{3,1,0,2:T(8,128)(2,1)}), bf16[2,32,16,128]{3,1,0,2:T(8,128)(2,1)}) %reduce-scatter.11.cloned.1.call-update) | async-done | bytes 262160 | tf_op jit(solution)/shard_map/reduce_scatter | solution.py:118
  295.8 1.0 convert_multiply_fusion
  296.8 1.1 copy.130
  297.9 68.3 %reduce-scatter.5.cloned.1.call-done = bf16[2,32,16,128]{3,1,0,2:T(8,128)(2,1)} async-done(((bf16[2,32,128,128]{3,1,0,2:T(8,128)(2,1)}), bf16[2,32,16,128]{3,1,0,2:T(8,128)(2,1)}) %reduce-scatter.5.cloned.1.call-update) | async-done | bytes 262160 | tf_op jit(solution)/shard_map/reduce_scatter | solution.py:109
  366.2 1.0 convert_multiply_fusion.3
  367.2 1.1 copy.127
  (36 shorter events, 3.8 us)
Async XLA Ops:
  7.2 79.4 %copy-start = (bf16[2,32,128,128]{3,2,1,0:T(8,128)(2,1)S(1)}, bf16[2,32,128,128]{3,2,1,0:T(8,128)(2,1)}, u32[]{:S(2)}) copy-start(bf16[2,32,128,128]{3,2,1,0:T(8,128)(2,1)} %param.10) | copy-start | bytes 6291460
  7.2 2.6 copy-start.10
  8.8 1.0 copy-start.6
  14.1 30.8 %all-to-all-start.2 = ((bf16[2,128,32,128]{3,0,2,1:T(2,128)(2,1)}), bf16[2,128,32,128]{3,0,2,1:T(2,128)(2,1)}, u32[]{:S(2)}, u32[]{:S(2)}) async-start(bf16[2,128,32,128]{3,0,2,1:T(2,128)(2,1)} %copy.108), calls=%async_computation.2 | async-start | bytes 4194304 | tf_op jit(solution)/shard_map/all_to_all | solution.py:24
  18.6 1.9 copy-start.11
  44.9 30.2 %all-to-all-start = ((bf16[2,32,128,128]{3,0,1,2:T(2,128)(2,1)}), bf16[2,32,128,128]{3,0,1,2:T(2,128)(2,1)}, u32[]{:S(2)}, u32[]{:S(2)}) async-start(bf16[2,32,128,128]{3,0,1,2:T(2,128)(2,1)} %copy.98), calls=%async_computation | async-start | bytes 4194304 | tf_op jit(solution)/shard_map/all_to_all | solution.py:24
  49.4 145.1 %reduce-scatter.9.cloned.1.call-start = ((), (), s32[]{:S(2)}) async-start(), calls=%async_computation.10 | async-start | bytes 2359296 | tf_op jit(solution)/shard_map/reduce_scatter | solution.py:115
  78.1 2.1 copy-start.9
  78.5 2.7 copy-start.2
  80.2 1.6 copy-start.13
  81.2 2.4 copy-start.12
  86.3 139.2 %reduce-scatter.7.cloned.1.call-start = ((), (), s32[]{:S(2)}) async-start(), calls=%async_computation.9 | async-start | bytes 2359296 | tf_op jit(solution)/shard_map/reduce_scatter | solution.py:112
  86.6 6.2 %copy-start.3 = (bf16[2,4,32,32,128]{4,3,2,1,0:T(8,128)(2,1)S(1)}, bf16[2,4,32,32,128]{4,3,2,1,0:T(8,128)(2,1)}, u32[]{:S(2)}) copy-start(bf16[2,4,32,32,128]{4,3,2,1,0:T(8,128)(2,1)} %copy-done.2) | copy-start | bytes 6291460
  92.8 1.4 copy-start.8
  97.0 198.8 %reduce-scatter.11.cloned.1.call-start = ((), (), s32[]{:S(2)}) async-start(), calls=%async_computation.11 | async-start | bytes 2359296 | tf_op jit(solution)/shard_map/reduce_scatter | solution.py:118
  133.7 1.2 copy-start.7
  138.5 227.7 %reduce-scatter.5.cloned.1.call-start = ((), (), s32[]{:S(2)}) async-start(), calls=%async_computation.8 | async-start | bytes 2359296 | tf_op jit(solution)/shard_map/reduce_scatter | solution.py:109
  178.4 1.4 copy-start.4
  188.9 2.0 copy-start.5
  226.6 141.8 %copy-start.1 = (bf16[2,32,128,128]{3,2,1,0:T(8,128)(2,1)S(1)}, bf16[2,32,128,128]{3,2,1,0:T(8,128)(2,1)}, u32[]{:S(2)}) copy-start(bf16[2,32,128,128]{3,2,1,0:T(8,128)(2,1)} %param.10) | copy-start | bytes 6291460
Sparse Core Ops, SparseCore 0:
  86.5 68.8 reduce-scatter.8
  158.9 66.6 reduce-scatter.6
  229.1 66.6 reduce-scatter.10
  299.2 66.9 reduce-scatter.4
where the time goes:
time: 376 us; the launch traced here: 375 us
  waiting for transfers between devices  207 us (55%)
  blocking collectives  57.7 us (15%)
  local copies, waits for them, and re-layouts  52.8 us (14%)
  matrix products  29.7 us (8%)
  between operations  14.1 us (4%)
  starting transfers between devices  9.47 us (3%)
  other arithmetic  4.01 us (1%)
    reduce_scatter x1, waiting for transfers between devices, body(): lax.psum_scatter(grad_up_right.astype(jnp.bfloat16), 'dp', scatter_dimens...  68.3 us
    reduce_scatter x1, waiting for transfers between devices, body(): lax.psum_scatter(grad_down_left.astype(jnp.bfloat16), 'dp', scatter_dimen...  68.1 us
    all_to_all x2, blocking collectives, partner_cross(): return lax.all_to_all(panel_data, 'mp', split_dim, concat_dim, tiled=True)  57.7 us
    all_to_all x2, waiting for transfers between devices, partner_cross(): return lax.all_to_all(panel_data, 'mp', split_dim, concat_dim, tiled=True)  41.6 us
    reduce_scatter x1, waiting for transfers between devices, body(): lax.psum_scatter(grad_up_left.astype(jnp.bfloat16), 'dp', scatter_dimensi...  28.9 us
    unnamed x36, local copies, waits for them, and re-layouts  16.9 us
    all_to_all x2, starting transfers between devices, partner_cross(): return lax.all_to_all(panel_data, 'mp', split_dim, concat_dim, tiled=True)  8.91 us
    all_to_all x6, local copies, waits for them, and re-layouts, partner_cross(): return lax.all_to_all(panel_data, 'mp', split_dim, concat_dim, tiled=True)  8.23 us
  transfers between devices with their start and end apart: 6, of which 5 were waited for; matrix products, arithmetic and copies ran while one was open for 17% of the time, Pallas kernels for 0%

commit v1 on v0

v1 whole, which is shorter than its diff:
```python
import functools

import jax
import jax.numpy as jnp
from jax import lax
from jax.experimental import pallas as pl
from jax.experimental.pallas import tpu as pltpu
from jax.sharding import PartitionSpec as P

gelu_root = 0.7978845608
gelu_cube = 0.044715
F32 = jnp.float32
BF16 = jnp.bfloat16


def mm(lhs, rhs, ldim, rdim):
    return lax.dot_general(lhs, rhs, (((ldim,), (rdim,)), ((), ())), preferred_element_type=F32)


def send_panel(outs, scratch, me, blocks):
    span = blocks * blocks
    for k, out in enumerate(outs):
        start = pl.multiple_of((me ^ k) * span, span)
        rows = scratch[pl.ds(start, span), :]
        out[...] = rows.reshape(out.shape).astype(BF16)


def gather_rows(parts, scratch, me, block, blocks):
    for k, part in enumerate(parts):
        start = pl.multiple_of((me ^ k) * blocks, blocks)
        scratch[pl.ds(start, blocks), :] = part[block].astype(F32)
    return scratch[...].astype(BF16)


def store_grad(keep, send, kind, block, value, scratch, me, ways):
    rows = value.shape[0] // ways
    scratch[...] = value
    for p in range(ways // 2):
        k = 2 * p
        for out, rel in ((keep, k), (send, k + 1)):
            start = pl.multiple_of((me ^ rel) * rows, rows)
            out[p, kind, block] = scratch[pl.ds(start, rows), :].astype(BF16)


def panel_kernel(ways, wdim, me_ref, x_ref, w_ref, *rest):
    outs, scratch = rest[:ways], rest[ways]
    blocks, width = w_ref.shape[1], w_ref.shape[2]
    me = me_ref[0]
    for i in range(blocks):
        value = mm(w_ref[0, i], x_ref[:, i * width : (i + 1) * width], wdim, 1)
        scratch[pl.ds(i, width, stride=blocks), :] = value
    send_panel(outs, scratch, me, blocks)


def make_panel(me, x, w, q, ways, wdim):
    tok, width = x.shape[0], w.shape[-1]
    blocks = w.shape[1]
    part = jax.ShapeDtypeStruct((blocks, blocks, tok), BF16)
    return pl.pallas_call(
        functools.partial(panel_kernel, ways, wdim),
        out_shape=[part] * ways,
        grid=(1,),
        in_specs=[
            pl.BlockSpec(memory_space=pltpu.SMEM),
            pl.BlockSpec(x.shape, lambda s: (0, 0)),
            pl.BlockSpec((1,) + w.shape[1:], lambda s: (q, 0, 0, 0)),
        ],
        out_specs=[pl.BlockSpec(part.shape, lambda s: (0, 0, 0))] * ways,
        scratch_shapes=[pltpu.VMEM((width * blocks, tok), F32)],
        compiler_params=pltpu.CompilerParams(vmem_limit_bytes=40 * 2**20),
        cost_estimate=pl.CostEstimate(flops=2 * tok * x.shape[1] * width * 8, bytes_accessed=4 * 2**20, transcendentals=0),
    )(me, x, w)


def middle_kernel(mp_ways, dp_ways, me_ref, ul_ref, df_ref, *rest):
    n = mp_ways
    r_in, b_in = rest[:n], rest[n : 2 * n]
    d_out, u_out = rest[2 * n : 3 * n], rest[3 * n : 4 * n]
    keep, send = rest[4 * n], rest[4 * n + 1]
    scr_d, scr_u, asm_r, asm_b, gr1, gr2 = rest[4 * n + 2 :]
    blocks, width = ul_ref.shape[1], ul_ref.shape[2]
    me_mp, me_dp = me_ref[0], me_ref[1]

    def step(c, carry):
        ul, df = ul_ref[0, c], df_ref[0, c]
        cu = gather_rows(r_in, asm_r, me_mp, c, blocks)
        dg = gather_rows(b_in, asm_b, me_mp, c, blocks)
        pre = mm(ul, cu, 0, 0)
        sq = pre * pre
        th = jnp.tanh(gelu_root * (pre + gelu_cube * sq * pre))
        half = 0.5 * (1.0 + th)
        hidden = (pre * half).astype(BF16)
        slope = half + 0.5 * pre * (1.0 - th * th) * (gelu_root * (1.0 + 3.0 * gelu_cube * sq))
        scr_d[pl.ds(c, width, stride=blocks), :] = mm(df, hidden, 0, 0)
        pg = (mm(df, dg, 1, 0) * slope).astype(BF16)
        scr_u[pl.ds(c, width, stride=blocks), :] = mm(ul, pg, 1, 0)
        store_grad(keep, send, 0, c, mm(hidden, dg, 1, 1), gr1, me_dp, dp_ways)
        store_grad(keep, send, 1, c, mm(cu, pg, 1, 1), gr2, me_dp, dp_ways)
        return carry

    lax.fori_loop(0, blocks, step, 0)
    send_panel(d_out, scr_d, me_mp, blocks)
    send_panel(u_out, scr_u, me_mp, blocks)


def grad_halves(blocks, width, dp_ways):
    return jax.ShapeDtypeStruct((dp_ways // 2, 2, blocks, width // dp_ways, width), BF16)


def full_spec(shape):
    return pl.BlockSpec(shape, lambda s: (0,) * len(shape))


def make_middle(me, r_in, b_in, ul, df, q, dp_ways):
    n = len(r_in)
    part = jax.ShapeDtypeStruct(r_in[0].shape, BF16)
    blocks, width, tok = ul.shape[1], ul.shape[2], part.shape[2]
    half = grad_halves(blocks, width, dp_ways)
    w_spec = pl.BlockSpec((1,) + ul.shape[1:], lambda s: (q, 0, 0, 0))
    res = pl.pallas_call(
        functools.partial(middle_kernel, n, dp_ways),
        out_shape=[part] * (2 * n) + [half] * 2,
        grid=(1,),
        in_specs=[pl.BlockSpec(memory_space=pltpu.SMEM), w_spec, w_spec] + [full_spec(part.shape)] * (2 * n),
        out_specs=[full_spec(part.shape)] * (2 * n) + [full_spec(half.shape)] * 2,
        scratch_shapes=[pltpu.VMEM((width * blocks, tok), F32)] * 2
        + [pltpu.VMEM((width, tok), F32)] * 2
        + [pltpu.VMEM((width, width), F32)] * 2,
        compiler_params=pltpu.CompilerParams(vmem_limit_bytes=40 * 2**20),
        cost_estimate=pl.CostEstimate(flops=6 * 2 * tok * blocks * width * width * 8, bytes_accessed=8 * 2**20, transcendentals=0),
    )(me, ul, df, *r_in, *b_in)
    return res[:n], res[n : 2 * n], res[2 * n], res[2 * n + 1]


def last_grads_kernel(mp_ways, dp_ways, me_ref, x_ref, g_ref, *rest):
    n = mp_ways
    d_in, u_in = rest[:n], rest[n : 2 * n]
    keep, send, asm_d, asm_u, gr1, gr2 = rest[2 * n :]
    blocks = d_in[0].shape[0]
    width = gr1.shape[0]
    me_mp, me_dp = me_ref[0], me_ref[1]

    for e in range(blocks):
        cols = slice(e * width, (e + 1) * width)
        cd = gather_rows(d_in, asm_d, me_mp, e, blocks)
        rg = gather_rows(u_in, asm_u, me_mp, e, blocks)
        store_grad(keep, send, 0, e, mm(cd, g_ref[:, cols], 1, 0), gr1, me_dp, dp_ways)
        store_grad(keep, send, 1, e, mm(rg, x_ref[:, cols], 1, 0).T, gr2, me_dp, dp_ways)


def make_last_grads(me, d_in, u_in, x, g, width, dp_ways):
    n = len(d_in)
    part = d_in[0]
    blocks, tok = part.shape[0], part.shape[2]
    half = grad_halves(blocks, width, dp_ways)
    return pl.pallas_call(
        functools.partial(last_grads_kernel, n, dp_ways),
        out_shape=[half] * 2,
        grid=(1,),
        in_specs=[pl.BlockSpec(memory_space=pltpu.SMEM)] + [full_spec(x.shape)] * 2 + [full_spec(part.shape)] * (2 * n),
        out_specs=[full_spec(half.shape)] * 2,
        scratch_shapes=[pltpu.VMEM((width, tok), F32)] * 2 + [pltpu.VMEM((width, width), F32)] * 2,
        compiler_params=pltpu.CompilerParams(vmem_limit_bytes=40 * 2**20),
        cost_estimate=pl.CostEstimate(flops=2 * 2 * tok * blocks * width * width * 8, bytes_accessed=6 * 2**20, transcendentals=0),
    )(me, x, g, *d_in, *u_in)


def outputs_kernel(mp_ways, me_ref, dl_ref, ur_ref, *rest):
    n = mp_ways
    groups = dl_ref.shape[0]
    count = groups * n
    d_in, u_in = rest[:count], rest[count : 2 * count]
    mixed, tgrad, asm_d, asm_u = rest[2 * count :]
    blocks, width = dl_ref.shape[1], dl_ref.shape[2]
    me_mp = me_ref[0]
    for e in range(blocks):
        cols = slice(e * width, (e + 1) * width)
        out_sum = grad_sum = None
        for q in range(groups):
            cd = gather_rows(d_in[q * n : (q + 1) * n], asm_d, me_mp, e, blocks)
            rg = gather_rows(u_in[q * n : (q + 1) * n], asm_u, me_mp, e, blocks)
            one = mm(cd, dl_ref[q, e], 0, 0)
            two = mm(ur_ref[q, e], rg, 1, 0)
            out_sum = one if q == 0 else out_sum + one
            grad_sum = two if q == 0 else grad_sum + two
        mixed[:, cols] = out_sum.astype(BF16)
        tgrad[:, cols] = grad_sum.T.astype(BF16)


def make_outputs(me, d_in, u_in, dl, ur):
    n = len(d_in[0])
    part = d_in[0][0]
    groups, blocks, width, tok = dl.shape[0], dl.shape[1], dl.shape[2], part.shape[2]
    flat_d = [p for d in d_in for p in d]
    flat_u = [p for u in u_in for p in u]
    out = jax.ShapeDtypeStruct((tok, blocks * width), BF16)
    return pl.pallas_call(
        functools.partial(outputs_kernel, n),
        out_shape=[out] * 2,
        grid=(1,),
        in_specs=[pl.BlockSpec(memory_space=pltpu.SMEM)]
        + [full_spec(dl.shape)] * 2
        + [full_spec(part.shape)] * (2 * n * groups),
        out_specs=[full_spec(out.shape)] * 2,
        scratch_shapes=[pltpu.VMEM((width, tok), F32)] * 2,
        compiler_params=pltpu.CompilerParams(vmem_limit_bytes=40 * 2**20),
        cost_estimate=pl.CostEstimate(flops=4 * 2 * tok * blocks * width * width * 8, bytes_accessed=10 * 2**20, transcendentals=0),
    )(me, dl, ur, *flat_d, *flat_u)


def xor_permute(array, axis, k):
    return lax.ppermute(array, axis, [(i, i ^ k) for i in range(lax.axis_size(axis))])


def exchange(parts):
    return [p if k == 0 else xor_permute(p, "mp", k) for k, p in enumerate(parts)]


def halving_sum(keep, send, scale):
    bit = 1
    while True:
        got = xor_permute(send, "dp", bit)
        total = keep.astype(F32) + got.astype(F32)
        if total.shape[0] == 1:
            return total[0] * scale
        total = total.astype(BF16).reshape((total.shape[0] // 2, 2) + total.shape[1:])
        keep, send = total[:, 0], total[:, 1]
        bit *= 2


def body(tokens, cotangent, up_right, up_left, down_first_factor, down_left):
    groups, width = up_right.shape[0], up_right.shape[2]
    mp_ways, dp_ways = lax.axis_size("mp"), lax.axis_size("dp")
    scale = (dp_ways * tokens.shape[0]) ** (-0.5)
    me = jnp.stack([lax.axis_index("mp"), lax.axis_index("dp")]).astype(jnp.int32)
    rights, backs = [], []
    for q in range(groups):
        rights.append(exchange(make_panel(me, tokens, up_right, q, mp_ways, 0)))
        backs.append(exchange(make_panel(me, cotangent, down_left, q, mp_ways, 1)))
    downs, ups, mid_sums, last_sums = [], [], [], []
    for q in range(groups):
        d, u, keep, send = make_middle(me, rights[q], backs[q], up_left, down_first_factor, q, dp_ways)
        downs.append(exchange(d))
        ups.append(exchange(u))
        mid_sums.append(halving_sum(keep, send, scale))
    for q in range(groups):
        keep, send = make_last_grads(me, downs[q], ups[q], tokens, cotangent, width, dp_ways)
        last_sums.append(halving_sum(keep, send, scale))
    mixed, tokens_grad = make_outputs(me, downs, ups, down_left, up_right)

    def pick(sums, kind):
        return jnp.stack([s[kind] for s in sums])

    return (mixed, tokens_grad, pick(last_sums, 1), pick(mid_sums, 1), pick(mid_sums, 0), pick(last_sums, 0))


def solution(mesh):
    weight = P(None, "mp", None, None)
    in_specs = (P("dp", "mp"), P("dp", "mp"), weight, weight, weight, weight)
    grad = P(None, "mp", "dp", None)
    out_specs = (P("dp", "mp"), P("dp", "mp"), grad, grad, grad, grad)
    return jax.shard_map(body, mesh=mesh, in_specs=in_specs, out_specs=out_specs, check_vma=False)
```

time: 376 us -> 222 us (0.59)
  waiting for transfers between devices: 207 us -> 123 us
  blocking collectives: 57.7 us -> 0 us
  Pallas kernels: 0 us -> 49.8 us
  local copies, waits for them, and re-layouts: 52.8 us -> 3.34 us
  matrix products: 29.7 us -> 0 us
  starting transfers between devices: 9.47 us -> 39.1 us
  between operations: 14.1 us -> 0.96 us
    reduce_scatter x4 -> x0, waiting for transfers between devices: 165 us -> none  [the longest x1 68.3 us: body(): lax.psum_scatter(grad_up_right.astype(jnp.bfloat16), 'dp', scatter_dimens...]
    ppermute x0 -> x36, waiting for transfers between devices: none -> 123 us  [xor_permute(): lax.ppermute(array, axis, [(i, i ^ k) for i in range(lax.axis_size(axis))])]
    all_to_all x2 -> x0, blocking collectives: 57.7 us -> none  [partner_cross(): return lax.all_to_all(panel_data, 'mp', split_dim, concat_dim, tiled=True)]
    pallas_call x0 -> x9, Pallas kernels: none -> 49.8 us  [the longest x2 32.7 us: make_middle(): pl.pallas_call(functools.partial(middle_kernel, n, dp_ways), out_shape=[p...]
    all_to_all x2 -> x0, waiting for transfers between devices: 41.6 us -> none  [partner_cross(): return lax.all_to_all(panel_data, 'mp', split_dim, concat_dim, tiled=True)]
    ppermute x0 -> x36, starting transfers between devices: none -> 39.1 us  [xor_permute(): lax.ppermute(array, axis, [(i, i ^ k) for i in range(lax.axis_size(axis))])]
    dot_general x12 -> x0, matrix products: 29.7 us -> none  [the longest x1 6.21 us: down_back(): jnp.einsum('qcet,qcae->qcat', crossed, down_first_factor, preferred_eleme...]
    convert_element_type x8 -> x0, local copies, waits for them, and re-layouts: 27.7 us -> none  [the longest x1 4.6 us: body(): up_back_panel = jnp.einsum('qcbt,qcab->qact', preactivation_gradient, up_...]
  transfers between devices with their start and end apart: 6 -> 36, of which waited for: 5 -> 16; matrix products, arithmetic and copies ran while one was open for 17% -> 2% of each run, Pallas kernels for 0% -> 21%
where the time goes in v1:
time: 222 us; the launch traced here: 221 us
  waiting for transfers between devices  123 us (55%)
  Pallas kernels  49.8 us (22%)
  starting transfers between devices  39.1 us (18%)
  other arithmetic  5.33 us (2%)
  local copies, waits for them, and re-layouts  3.34 us (2%)
    ppermute x36, waiting for transfers between devices, xor_permute(): lax.ppermute(array, axis, [(i, i ^ k) for i in range(lax.axis_size(axis))])  123 us
    ppermute x36, starting transfers between devices, xor_permute(): lax.ppermute(array, axis, [(i, i ^ k) for i in range(lax.axis_size(axis))])  39.1 us
    pallas_call x2, Pallas kernels, make_middle(): pl.pallas_call(functools.partial(middle_kernel, n, dp_ways), out_shape=[p...  32.7 us
    pallas_call x4, Pallas kernels, make_panel(): pl.pallas_call(functools.partial(panel_kernel, ways, wdim), out_shape=[pa...  9.88 us
  transfers between devices with their start and end apart: 36, of which 16 were waited for; matrix products, arithmetic and copies ran while one was open for 2% of the time, Pallas kernels for 21%

profile of v1, /device:TPU:0, one launch (start us, length us, event | category | flops | bytes accessed | tf_op | source)
XLA Modules:
  0.0 221.5 jit_solution(39872733086074083)
XLA Ops:
  0.7 1.7 copy-done.3
  2.4 1.2 copy-done.5
  3.7 2.5 %shard_map.109 = (bf16[32,32,128]{2,1,0:T(8,128)(2,1)S(1)}, bf16[32,32,128]{2,1,0:T(8,128)(2,1)S(1)}, bf16[32,32,128]{2,1,0:T(8,128)(2,1)S(1)}, bf16[32,32,128]{2,1,0:T(8,128)(2,1)S(1)}) custom-call(s32[2]{0:T(128)S(1)} %pad_add_fusion.me_ref, bf16[128,4096]{1,0:T(8,128)(2,1)S(1)} %copy-done.5, bf16[2,32,128,128]{3,2,1,0:T(8,128)(2,1)S(1)} %copy-done.3), custom_call_target="tpu_custom_call" | custom-call | flops 1073741824 | bytes 4194304 | tf_op jit(solution)/shard_map/pallas_call | solution.py:59
  6.7 2.6 %collective-permute-start.1 = (bf16[32,32,128]{2,1,0:T(8,128)(2,1)S(1)}, bf16[32,32,128]{2,1,0:T(8,128)(2,1)S(1)}, u32[]{:S(2)}, u32[]{:S(2)}) collective-permute-start(bf16[32,32,128]{2,1,0:T(8,128)(2,1)S(1)} %get-tuple-element.50), channel_id=1, source_target_pairs={{0,2},{1,3},{2,0},{3,1},{4,6},{5,7},{6,4},{7,5},{8,10},{9,11},{10,... | collective-permute-start | bytes 786440 | tf_op jit(solution)/shard_map/ppermute | solution.py:212
  9.3 2.5 %shard_map.110 = (bf16[32,32,128]{2,1,0:T(8,128)(2,1)S(1)}, bf16[32,32,128]{2,1,0:T(8,128)(2,1)S(1)}, bf16[32,32,128]{2,1,0:T(8,128)(2,1)S(1)}, bf16[32,32,128]{2,1,0:T(8,128)(2,1)S(1)}) custom-call(s32[2]{0:T(128)S(1)} %pad_add_fusion.me_ref, bf16[128,4096]{1,0:T(8,128)(2,1)S(1)} %copy-done.7, bf16[2,32,128,128]{3,2,1,0:T(8,128)(2,1)S(1)} %copy-done.2), custom_call_target="tpu_custom_call" | custom-call | flops 1073741824 | bytes 4194304 | tf_op jit(solution)/shard_map/pallas_call | solution.py:59
  12.0 1.9 collective-permute-start.4
  13.9 2.5 %shard_map.112 = (bf16[32,32,128]{2,1,0:T(8,128)(2,1)S(1)}, bf16[32,32,128]{2,1,0:T(8,128)(2,1)S(1)}, bf16[32,32,128]{2,1,0:T(8,128)(2,1)S(1)}, bf16[32,32,128]{2,1,0:T(8,128)(2,1)S(1)}) custom-call(s32[2]{0:T(128)S(1)} %pad_add_fusion.me_ref, bf16[128,4096]{1,0:T(8,128)(2,1)S(1)} %copy-done.6, bf16[2,32,128,128]{3,2,1,0:T(8,128)(2,1)S(1)} %copy-done.3), custom_call_target="tpu_custom_call" | custom-call | flops 1073741824 | bytes 4194304 | tf_op jit(solution)/shard_map/pallas_call | solution.py:59
  16.6 1.8 collective-permute-start.10
  18.4 2.4 %shard_map.113 = (bf16[32,32,128]{2,1,0:T(8,128)(2,1)S(1)}, bf16[32,32,128]{2,1,0:T(8,128)(2,1)S(1)}, bf16[32,32,128]{2,1,0:T(8,128)(2,1)S(1)}, bf16[32,32,128]{2,1,0:T(8,128)(2,1)S(1)}) custom-call(s32[2]{0:T(128)S(1)} %pad_add_fusion.me_ref, bf16[128,4096]{1,0:T(8,128)(2,1)S(1)} %copy-done.7, bf16[2,32,128,128]{3,2,1,0:T(8,128)(2,1)S(1)} %copy-done.2), custom_call_target="tpu_custom_call" | custom-call | flops 1073741824 | bytes 4194304 | tf_op jit(solution)/shard_map/pallas_call | solution.py:59
  21.5 1.9 collective-permute-start.11
  23.4 4.2 %collective-permute-done.4.rest_6_ = bf16[32,32,128]{2,1,0:T(8,128)(2,1)S(1)} collective-permute-done((bf16[32,32,128]{2,1,0:T(8,128)(2,1)S(1)}, bf16[32,32,128]{2,1,0:T(8,128)(2,1)S(1)}, u32[]{:S(2)}, u32[]{:S(2)}) %collective-permute-start.4) | collective-permute-done | bytes 262176 | tf_op jit(solution)/shard_map/ppermute | solution.py:212
  27.7 1.9 collective-permute-start.13
  29.6 3.1 %collective-permute-done.5.rest_7_ = bf16[32,32,128]{2,1,0:T(8,128)(2,1)S(1)} collective-permute-done((bf16[32,32,128]{2,1,0:T(8,128)(2,1)S(1)}, bf16[32,32,128]{2,1,0:T(8,128)(2,1)S(1)}, u32[]{:S(2)}, u32[]{:S(2)}) %collective-permute-start.5) | collective-permute-done | bytes 262176 | tf_op jit(solution)/shard_map/ppermute | solution.py:212
  32.8 1.9 collective-permute-start.14
  34.7 4.2 %collective-permute-done.10.rest_2_ = bf16[32,32,128]{2,1,0:T(8,128)(2,1)S(1)} collective-permute-done((bf16[32,32,128]{2,1,0:T(8,128)(2,1)S(1)}, bf16[32,32,128]{2,1,0:T(8,128)(2,1)S(1)}, u32[]{:S(2)}, u32[]{:S(2)}) %collective-permute-start.10) | collective-permute-done | bytes 262176 | tf_op jit(solution)/shard_map/ppermute | solution.py:212
  38.9 16.4 %shard_map.111 = (bf16[32,32,128]{2,1,0:T(8,128)(2,1)S(1)}, bf16[32,32,128]{2,1,0:T(8,128)(2,1)S(1)}, bf16[32,32,128]{2,1,0:T(8,128)(2,1)S(1)}, bf16[32,32,128]{...) custom-call(s32[2]{0:T(128)S(1)} %pad_add_fusion.me_ref, ...), custom_call_target="tpu_custom_call" | custom-call | flops 6442450944 | bytes 8388608 | tf_op jit(solution)/shard_map/pallas_call | solution.py:120
  55.9 2.0 collective-permute-start.19
  58.1 2.0 collective-permute-start.7
  60.1 16.2 %shard_map.114 = (bf16[32,32,128]{2,1,0:T(8,128)(2,1)S(1)}, bf16[32,32,128]{2,1,0:T(8,128)(2,1)S(1)}, bf16[32,32,128]{2,1,0:T(8,128)(2,1)S(1)}, bf16[32,32,128]{...) custom-call(s32[2]{0:T(128)S(1)} %pad_add_fusion.me_ref, ...), custom_call_target="tpu_custom_call" | custom-call | flops 6442450944 | bytes 8388608 | tf_op jit(solution)/shard_map/pallas_call | solution.py:120
  76.7 1.9 collective-permute-start.16
  78.6 1.5 collective-permute-start.30
  80.1 5.0 %collective-permute-done.8.rest_3_ = bf16[32,32,128]{2,1,0:T(8,128)(2,1)S(1)} collective-permute-done((bf16[32,32,128]{2,1,0:T(8,128)(2,1)S(1)}, bf16[32,32,128]{2,1,0:T(8,128)(2,1)S(1)}, u32[]{:S(2)}, u32[]{:S(2)}) %collective-permute-start.8) | collective-permute-done | bytes 262176 | tf_op jit(solution)/shard_map/ppermute | solution.py:212
  85.6 5.0 %collective-permute-done.16.rest_6_.rest_2_ = bf16[32,32,128]{2,1,0:T(8,128)(2,1)S(1)} collective-permute-done((bf16[32,32,128]{2,1,0:T(8,128)(2,1)S(1)}, bf16[32,32,128]{2,1,0:T(8,128)(2,1)S(1)}, u32[]{:S(2)}, u32[]{:S(2)}) %collective-permute-start.16) | collective-permute-done | bytes 262176 | tf_op jit(solution)/shard_map/ppermute | solution.py:212
  90.6 1.7 shard_map.116
  92.4 3.9 %collective-permute-done.17.rest_7_.rest_3_ = bf16[32,32,128]{2,1,0:T(8,128)(2,1)S(1)} collective-permute-done((bf16[32,32,128]{2,1,0:T(8,128)(2,1)S(1)}, bf16[32,32,128]{2,1,0:T(8,128)(2,1)S(1)}, u32[]{:S(2)}, u32[]{:S(2)}) %collective-permute-start.17) | collective-permute-done | bytes 262176 | tf_op jit(solution)/shard_map/ppermute | solution.py:212
  96.3 1.5 collective-permute-start.33
  98.3 3.6 %collective-permute-done.22.rest_14_.rest_6_ = bf16[32,32,128]{2,1,0:T(8,128)(2,1)S(1)} collective-permute-done((bf16[32,32,128]{2,1,0:T(8,128)(2,1)S(1)}, bf16[32,32,128]{2,1,0:T(8,128)(2,1)S(1)}, u32[]{:S(2)}, u32[]{:S(2)}) %collective-permute-start.22) | collective-permute-done | bytes 262176 | tf_op jit(solution)/shard_map/ppermute | solution.py:212
  101.8 5.6 %collective-permute-done.23.rest_15_.rest_7_ = bf16[32,32,128]{2,1,0:T(8,128)(2,1)S(1)} collective-permute-done((bf16[32,32,128]{2,1,0:T(8,128)(2,1)S(1)}, bf16[32,32,128]{2,1,0:T(8,128)(2,1)S(1)}, u32[]{:S(2)}, u32[]{:S(2)}) %collective-permute-start.23) | collective-permute-done | bytes 262176 | tf_op jit(solution)/shard_map/ppermute | solution.py:212
  107.5 1.7 shard_map.117
  109.2 1.6 collective-permute-start.27
  110.8 3.7 %shard_map.115 = (bf16[128,4096]{1,0:T(8,128)(2,1)}, bf16[128,4096]{1,0:T(8,128)(2,1)}) custom-call(s32[2]{0:T(128)S(1)} %pad_add_fusion.me_ref, bf16[2,32,128,128]{3,2,1,0:T(8,128)(2,1)S(1)} %copy-done.2, bf16[2,32,128,128]{3,2,1,0:T(8,128)(2,1)S(1)} %copy-done.4, bf16[32,32,128]{2,1,0:T(8,128)(2,1)S(1)} %get-tuple-element.56.rest_0_, ...), custom_call_target="tpu_custom_call" | custom-call | flops 4294967296 | bytes 10485760 | tf_op jit(solution)/shard_map/pallas_call | solution.py:197
  114.8 1.7 collective-permute-start.31
  116.5 10.7 %collective-permute-done.33 = bf16[4,2,32,16,128]{4,3,2,1,0:T(8,128)(2,1)} collective-permute-done((bf16[4,2,32,16,128]{4,3,2,1,0:T(8,128)(2,1)S(1)}, bf16[4,2,32,16,128]{4,3,2,1,0:T(8,128)(2,1)}, u32[]{:S(2)}, u32[]{:S(2)}) %collective-permute-start.33) | collective-permute-done | bytes 1048608 | tf_op jit(solution)/shard_map/ppermute | solution.py:212
  127.2 1.5 add_convert_fusion
  128.8 1.7 collective-permute-start.34
  130.5 19.1 %collective-permute-done.24 = bf16[4,2,32,16,128]{4,3,2,1,0:T(8,128)(2,1)S(1)} collective-permute-done((bf16[4,2,32,16,128]{4,3,2,1,0:T(8,128)(2,1)S(1)}, bf16[4,2,32,16,128]{4,3,2,1,0:T(8,128)(2,1)S(1)}, u32[]{:S(2)}, u32[]{:S(2)}) %collective-permute-start.24) | collective-permute-done | bytes 1048608 | tf_op jit(solution)/shard_map/ppermute | solution.py:212
  149.9 1.7 collective-permute-start.25
  151.6 19.2 %collective-permute-done.27 = bf16[4,2,32,16,128]{4,3,2,1,0:T(8,128)(2,1)S(1)} collective-permute-done((bf16[4,2,32,16,128]{4,3,2,1,0:T(8,128)(2,1)S(1)}, bf16[4,2,32,16,128]{4,3,2,1,0:T(8,128)(2,1)S(1)}, u32[]{:S(2)}, u32[]{:S(2)}) %collective-permute-start.27) | collective-permute-done | bytes 1048608 | tf_op jit(solution)/shard_map/ppermute | solution.py:212
  171.2 1.7 collective-permute-start.28
  173.1 2.8 %collective-permute-start.32 = (bf16[1,2,32,16,128]{4,3,2,1,0:T(8,128)(2,1)S(1)}, bf16[1,2,32,16,128]{4,3,2,1,0:T(8,128)(2,1)S(1)}, u32[]{:S(2)}, u32[]{:S(2)}) collective-permute-start(bf16[1,2,32,16,128]{4,3,2,1,0:T(8,128)(2,1)S(1)} %slice_bitcast_fusion.16), channel_id=1, source_target_pairs={{0,16},{4,20},{8,24},{12,28},{16,0},{20,4},{24,8},{28,12},{1,17},{... | collective-permute-start | bytes 786440 | tf_op jit(solution)/shard_map/ppermute | solution.py:212
  176.5 2.8 %collective-permute-start.26 = (bf16[1,2,32,16,128]{4,3,2,1,0:T(8,128)(2,1)S(1)}, bf16[1,2,32,16,128]{4,3,2,1,0:T(8,128)(2,1)S(1)}, u32[]{:S(2)}, u32[]{:S(2)}) collective-permute-start(bf16[1,2,32,16,128]{4,3,2,1,0:T(8,128)(2,1)S(1)} %slice_bitcast_fusion.22), channel_id=1, source_target_pairs={{0,16},{4,20},{8,24},{12,28},{16,0},{20,4},{24,8},{28,12},{1,17},{... | collective-permute-start | bytes 786440 | tf_op jit(solution)/shard_map/ppermute | solution.py:212
  179.3 15.5 %collective-permute-done.28 = bf16[2,2,32,16,128]{4,3,2,1,0:T(8,128)(2,1)S(1)} collective-permute-done((bf16[2,2,32,16,128]{4,3,2,1,0:T(8,128)(2,1)S(1)}, bf16[2,2,32,16,128]{4,3,2,1,0:T(8,128)(2,1)S(1)}, u32[]{:S(2)}, u32[]{:S(2)}) %collective-permute-start.28) | collective-permute-done | bytes 524320 | tf_op jit(solution)/shard_map/ppermute | solution.py:212
  195.0 0.9 collective-permute-start.29
  196.0 15.4 %collective-permute-done.35 = bf16[1,2,32,16,128]{4,3,2,1,0:T(8,128)(2,1)S(1)} collective-permute-done((bf16[1,2,32,16,128]{4,3,2,1,0:T(8,128)(2,1)S(1)}, bf16[1,2,32,16,128]{4,3,2,1,0:T(8,128)(2,1)S(1)}, u32[]{:S(2)}, u32[]{:S(2)}) %collective-permute-start.35) | collective-permute-done | bytes 262176 | tf_op jit(solution)/shard_map/ppermute | solution.py:212
  211.5 1.0 pad_maximum_fusion.1
  212.5 4.5 %collective-permute-done.26 = bf16[1,2,32,16,128]{4,3,2,1,0:T(8,128)(2,1)S(1)} collective-permute-done((bf16[1,2,32,16,128]{4,3,2,1,0:T(8,128)(2,1)S(1)}, bf16[1,2,32,16,128]{4,3,2,1,0:T(8,128)(2,1)S(1)}, u32[]{:S(2)}, u32[]{:S(2)}) %collective-permute-start.26) | collective-permute-done | bytes 262176 | tf_op jit(solution)/shard_map/ppermute | solution.py:212
  217.1 3.2 %collective-permute-done.29 = bf16[1,2,32,16,128]{4,3,2,1,0:T(8,128)(2,1)S(1)} collective-permute-done((bf16[1,2,32,16,128]{4,3,2,1,0:T(8,128)(2,1)S(1)}, bf16[1,2,32,16,128]{4,3,2,1,0:T(8,128)(2,1)S(1)}, u32[]{:S(2)}, u32[]{:S(2)}) %collective-permute-start.29) | collective-permute-done | bytes 262176 | tf_op jit(solution)/shard_map/ppermute | solution.py:212
  220.4 1.0 pad_maximum_fusion
  (76 shorter events, 6.2 us)
Async XLA Ops:
  0.6 8.7 %copy-start.2 = (bf16[2,32,128,128]{3,2,1,0:T(8,128)(2,1)S(1)}, bf16[2,32,128,128]{3,2,1,0:T(8,128)(2,1)}, u32[]{:S(2)}) copy-start(bf16[2,32,128,128]{3,2,1,0:T(8,128)(2,1)} %dl_ref.1) | copy-start | bytes 6291460
  0.7 1.7 copy-start.3
  2.4 1.2 copy-start.5
  3.7 5.7 %copy-start.7 = (bf16[128,4096]{1,0:T(8,128)(2,1)S(1)}, bf16[128,4096]{1,0:T(8,128)(2,1)}, u32[]{:S(2)}) copy-start(bf16[128,4096]{1,0:T(8,128)(2,1)} %g_ref.3) | copy-start | bytes 3145732
  6.2 7.8 %copy-start.6 = (bf16[128,4096]{1,0:T(8,128)(2,1)S(1)}, bf16[128,4096]{1,0:T(8,128)(2,1)}, u32[]{:S(2)}) copy-start(bf16[128,4096]{1,0:T(8,128)(2,1)} %x_ref.11) | copy-start | bytes 3145732
  6.2 10.3 %collective-permute-start = (bf16[32,32,128]{2,1,0:T(8,128)(2,1)S(1)}, bf16[32,32,128]{2,1,0:T(8,128)(2,1)S(1)}, u32[]{:S(2)}, u32[]{:S(2)}) collective-permute-start(bf16[32,32,128]{2,1,0:T(8,128)(2,1)S(1)} %get-tuple-element.49), channel_id=1, source_target_pairs={{0,1},{1,0},{2,3},{3,2},{4,5},{5,4},{6,7},{7,6},{8,9},{9,8},{10,11... | collective-permute-start | bytes 786440 | tf_op jit(solution)/shard_map/ppermute | solution.py:212
  6.7 9.8 %collective-permute-start.1 = (bf16[32,32,128]{2,1,0:T(8,128)(2,1)S(1)}, bf16[32,32,128]{2,1,0:T(8,128)(2,1)S(1)}, u32[]{:S(2)}, u32[]{:S(2)}) collective-permute-start(bf16[32,32,128]{2,1,0:T(8,128)(2,1)S(1)} %get-tuple-element.50), channel_id=1, source_target_pairs={{0,2},{1,3},{2,0},{3,1},{4,6},{5,7},{6,4},{7,5},{8,10},{9,11},{10,... | collective-permute-start | bytes 786440 | tf_op jit(solution)/shard_map/ppermute | solution.py:212
  9.3 12.3 %collective-permute-start.2 = (bf16[32,32,128]{2,1,0:T(8,128)(2,1)S(1)}, bf16[32,32,128]{2,1,0:T(8,128)(2,1)S(1)}, u32[]{:S(2)}, u32[]{:S(2)}) collective-permute-start(bf16[32,32,128]{2,1,0:T(8,128)(2,1)S(1)} %get-tuple-element.51), channel_id=1, source_target_pairs={{0,3},{1,2},{2,1},{3,0},{4,7},{5,6},{6,5},{7,4},{8,11},{9,10},{10,... | collective-permute-start | bytes 786440 | tf_op jit(solution)/shard_map/ppermute | solution.py:212
  11.8 11.6 %collective-permute-start.3 = (bf16[32,32,128]{2,1,0:T(8,128)(2,1)S(1)}, bf16[32,32,128]{2,1,0:T(8,128)(2,1)S(1)}, u32[]{:S(2)}, u32[]{:S(2)}) collective-permute-start(bf16[32,32,128]{2,1,0:T(8,128)(2,1)S(1)} %get-tuple-element.53), channel_id=1, source_target_pairs={{0,1},{1,0},{2,3},{3,2},{4,5},{5,4},{6,7},{7,6},{8,9},{9,8},{10,11... | collective-permute-start | bytes 786440 | tf_op jit(solution)/shard_map/ppermute | solution.py:212
  12.0 15.7 %collective-permute-start.4 = (bf16[32,32,128]{2,1,0:T(8,128)(2,1)S(1)}, bf16[32,32,128]{2,1,0:T(8,128)(2,1)S(1)}, u32[]{:S(2)}, u32[]{:S(2)}) collective-permute-start(bf16[32,32,128]{2,1,0:T(8,128)(2,1)S(1)} %get-tuple-element.54), channel_id=1, source_target_pairs={{0,2},{1,3},{2,0},{3,1},{4,6},{5,7},{6,4},{7,5},{8,10},{9,11},{10,... | collective-permute-start | bytes 786440 | tf_op jit(solution)/shard_map/ppermute | solution.py:212
  13.9 25.0 %copy-start.1 = (bf16[2,32,128,128]{3,2,1,0:T(8,128)(2,1)S(1)}, bf16[2,32,128,128]{3,2,1,0:T(8,128)(2,1)}, u32[]{:S(2)}) copy-start(bf16[2,32,128,128]{3,2,1,0:T(8,128)(2,1)} %df_ref.3) | copy-start | bytes 6291460
  16.4 22.5 %copy-start = (bf16[2,32,128,128]{3,2,1,0:T(8,128)(2,1)S(1)}, bf16[2,32,128,128]{3,2,1,0:T(8,128)(2,1)}, u32[]{:S(2)}) copy-start(bf16[2,32,128,128]{3,2,1,0:T(8,128)(2,1)} %ul_ref.3) | copy-start | bytes 6291460
  16.5 16.3 %collective-permute-start.5 = (bf16[32,32,128]{2,1,0:T(8,128)(2,1)S(1)}, bf16[32,32,128]{2,1,0:T(8,128)(2,1)S(1)}, u32[]{:S(2)}, u32[]{:S(2)}) collective-permute-start(bf16[32,32,128]{2,1,0:T(8,128)(2,1)S(1)} %get-tuple-element.55), channel_id=1, source_target_pairs={{0,3},{1,2},{2,1},{3,0},{4,7},{5,6},{6,5},{7,4},{8,11},{9,10},{10,... | collective-permute-start | bytes 786440 | tf_op jit(solution)/shard_map/ppermute | solution.py:212
  16.6 22.3 %collective-permute-start.10 = (bf16[32,32,128]{2,1,0:T(8,128)(2,1)S(1)}, bf16[32,32,128]{2,1,0:T(8,128)(2,1)S(1)}, u32[]{:S(2)}, u32[]{:S(2)}) collective-permute-start(bf16[32,32,128]{2,1,0:T(8,128)(2,1)S(1)} %get-tuple-element.62), channel_id=1, source_target_pairs={{0,2},{1,3},{2,0},{3,1},{4,6},{5,7},{6,4},{7,5},{8,10},{9,11},{10,... | collective-permute-start | bytes 786440 | tf_op jit(solution)/shard_map/ppermute | solution.py:212
  21.5 33.8 %collective-permute-start.11 = (bf16[32,32,128]{2,1,0:T(8,128)(2,1)S(1)}, bf16[32,32,128]{2,1,0:T(8,128)(2,1)S(1)}, u32[]{:S(2)}, u32[]{:S(2)}) collective-permute-start(bf16[32,32,128]{2,1,0:T(8,128)(2,1)S(1)} %get-tuple-element.63), channel_id=1, source_target_pairs={{0,3},{1,2},{2,1},{3,0},{4,7},{5,6},{6,5},{7,4},{8,11},{9,10},{10,... | collective-permute-start | bytes 786440 | tf_op jit(solution)/shard_map/ppermute | solution.py:212
  23.4 32.5 %collective-permute-start.12 = (bf16[32,32,128]{2,1,0:T(8,128)(2,1)S(1)}, bf16[32,32,128]{2,1,0:T(8,128)(2,1)S(1)}, u32[]{:S(2)}, u32[]{:S(2)}) collective-permute-start(bf16[32,32,128]{2,1,0:T(8,128)(2,1)S(1)} %get-tuple-element.65), channel_id=1, source_target_pairs={{0,1},{1,0},{2,3},{3,2},{4,5},{5,4},{6,7},{7,6},{8,9},{9,8},{10,11... | collective-permute-start | bytes 786440 | tf_op jit(solution)/shard_map/ppermute | solution.py:212
  27.7 30.3 %collective-permute-start.13 = (bf16[32,32,128]{2,1,0:T(8,128)(2,1)S(1)}, bf16[32,32,128]{2,1,0:T(8,128)(2,1)S(1)}, u32[]{:S(2)}, u32[]{:S(2)}) collective-permute-start(bf16[32,32,128]{2,1,0:T(8,128)(2,1)S(1)} %get-tuple-element.66), channel_id=1, source_target_pairs={{0,2},{1,3},{2,0},{3,1},{4,6},{5,7},{6,4},{7,5},{8,10},{9,11},{10,... | collective-permute-start | bytes 786440 | tf_op jit(solution)/shard_map/ppermute | solution.py:212
  32.8 25.2 %collective-permute-start.14 = (bf16[32,32,128]{2,1,0:T(8,128)(2,1)S(1)}, bf16[32,32,128]{2,1,0:T(8,128)(2,1)S(1)}, u32[]{:S(2)}, u32[]{:S(2)}) collective-permute-start(bf16[32,32,128]{2,1,0:T(8,128)(2,1)S(1)} %get-tuple-element.67), channel_id=1, source_target_pairs={{0,3},{1,2},{2,1},{3,0},{4,7},{5,6},{6,5},{7,4},{8,11},{9,10},{10,... | collective-permute-start | bytes 786440 | tf_op jit(solution)/shard_map/ppermute | solution.py:212
  38.9 19.2 %collective-permute-start.9 = (bf16[32,32,128]{2,1,0:T(8,128)(2,1)S(1)}, bf16[32,32,128]{2,1,0:T(8,128)(2,1)S(1)}, u32[]{:S(2)}, u32[]{:S(2)}) collective-permute-start(bf16[32,32,128]{2,1,0:T(8,128)(2,1)S(1)} %get-tuple-element.61), channel_id=1, source_target_pairs={{0,1},{1,0},{2,3},{3,2},{4,5},{5,4},{6,7},{7,6},{8,9},{9,8},{10,11... | collective-permute-start | bytes 786440 | tf_op jit(solution)/shard_map/ppermute | solution.py:212
  55.4 21.0 %collective-permute-start.18 = (bf16[32,32,128]{2,1,0:T(8,128)(2,1)S(1)}, bf16[32,32,128]{2,1,0:T(8,128)(2,1)S(1)}, u32[]{:S(2)}, u32[]{:S(2)}) collective-permute-start(bf16[32,32,128]{2,1,0:T(8,128)(2,1)S(1)} %get-tuple-element.73), channel_id=1, source_target_pairs={{0,1},{1,0},{2,3},{3,2},{4,5},{5,4},{6,7},{7,6},{8,9},{9,8},{10,11... | collective-permute-start | bytes 786440 | tf_op jit(solution)/shard_map/ppermute | solution.py:212
  55.9 20.5 %collective-permute-start.19 = (bf16[32,32,128]{2,1,0:T(8,128)(2,1)S(1)}, bf16[32,32,128]{2,1,0:T(8,128)(2,1)S(1)}, u32[]{:S(2)}, u32[]{:S(2)}) collective-permute-start(bf16[32,32,128]{2,1,0:T(8,128)(2,1)S(1)} %get-tuple-element.74), channel_id=1, source_target_pairs={{0,2},{1,3},{2,0},{3,1},{4,6},{5,7},{6,4},{7,5},{8,10},{9,11},{10,... | collective-permute-start | bytes 786440 | tf_op jit(solution)/shard_map/ppermute | solution.py:212
  57.9 18.7 %collective-permute-start.20 = (bf16[32,32,128]{2,1,0:T(8,128)(2,1)S(1)}, bf16[32,32,128]{2,1,0:T(8,128)(2,1)S(1)}, u32[]{:S(2)}, u32[]{:S(2)}) collective-permute-start(bf16[32,32,128]{2,1,0:T(8,128)(2,1)S(1)} %get-tuple-element.75), channel_id=1, source_target_pairs={{0,3},{1,2},{2,1},{3,0},{4,7},{5,6},{6,5},{7,4},{8,11},{9,10},{10,... | collective-permute-start | bytes 786440 | tf_op jit(solution)/shard_map/ppermute | solution.py:212
  57.9 20.6 %collective-permute-start.6 = (bf16[32,32,128]{2,1,0:T(8,128)(2,1)S(1)}, bf16[32,32,128]{2,1,0:T(8,128)(2,1)S(1)}, u32[]{:S(2)}, u32[]{:S(2)}) collective-permute-start(bf16[32,32,128]{2,1,0:T(8,128)(2,1)S(1)} %get-tuple-element.57), channel_id=1, source_target_pairs={{0,1},{1,0},{2,3},{3,2},{4,5},{5,4},{6,7},{7,6},{8,9},{9,8},{10,11... | collective-permute-start | bytes 786440 | tf_op jit(solution)/shard_map/ppermute | solution.py:212
  58.1 21.9 %collective-permute-start.7 = (bf16[32,32,128]{2,1,0:T(8,128)(2,1)S(1)}, bf16[32,32,128]{2,1,0:T(8,128)(2,1)S(1)}, u32[]{:S(2)}, u32[]{:S(2)}) collective-permute-start(bf16[32,32,128]{2,1,0:T(8,128)(2,1)S(1)} %get-tuple-element.58), channel_id=1, source_target_pairs={{0,2},{1,3},{2,0},{3,1},{4,6},{5,7},{6,4},{7,5},{8,10},{9,11},{10,... | collective-permute-start | bytes 786440 | tf_op jit(solution)/shard_map/ppermute | solution.py:212
  76.4 8.7 %collective-permute-start.8 = (bf16[32,32,128]{2,1,0:T(8,128)(2,1)S(1)}, bf16[32,32,128]{2,1,0:T(8,128)(2,1)S(1)}, u32[]{:S(2)}, u32[]{:S(2)}) collective-permute-start(bf16[32,32,128]{2,1,0:T(8,128)(2,1)S(1)} %get-tuple-element.59), channel_id=1, source_target_pairs={{0,3},{1,2},{2,1},{3,0},{4,7},{5,6},{6,5},{7,4},{8,11},{9,10},{10,... | collective-permute-start | bytes 786440 | tf_op jit(solution)/shard_map/ppermute | solution.py:212
  76.4 8.7 %collective-permute-start.15 = (bf16[32,32,128]{2,1,0:T(8,128)(2,1)S(1)}, bf16[32,32,128]{2,1,0:T(8,128)(2,1)S(1)}, u32[]{:S(2)}, u32[]{:S(2)}) collective-permute-start(bf16[32,32,128]{2,1,0:T(8,128)(2,1)S(1)} %get-tuple-element.69), channel_id=1, source_target_pairs={{0,1},{1,0},{2,3},{3,2},{4,5},{5,4},{6,7},{7,6},{8,9},{9,8},{10,11... | collective-permute-start | bytes 786440 | tf_op jit(solution)/shard_map/ppermute | solution.py:212
  76.7 13.9 %collective-permute-start.16 = (bf16[32,32,128]{2,1,0:T(8,128)(2,1)S(1)}, bf16[32,32,128]{2,1,0:T(8,128)(2,1)S(1)}, u32[]{:S(2)}, u32[]{:S(2)}) collective-permute-start(bf16[32,32,128]{2,1,0:T(8,128)(2,1)S(1)} %get-tuple-element.70), channel_id=1, source_target_pairs={{0,2},{1,3},{2,0},{3,1},{4,6},{5,7},{6,4},{7,5},{8,10},{9,11},{10,... | collective-permute-start | bytes 786440 | tf_op jit(solution)/shard_map/ppermute | solution.py:212
  78.6 35.9 %collective-permute-start.30 = (bf16[4,2,32,16,128]{4,3,2,1,0:T(8,128)(2,1)S(1)}, bf16[4,2,32,16,128]{4,3,2,1,0:T(8,128)(2,1)S(1)}, u32[]{:S(2)}, u32[]{:S(2)}) collective-permute-start(bf16[4,2,32,16,128]{4,3,2,1,0:T(8,128)(2,1)S(1)} %get-tuple-element.87), channel_id=1, source_target_pairs={{0,4},{4,0},{8,12},{12,8},{16,20},{20,16},{24,28},{28,24},{1,5},{5... | collective-permute-start | bytes 3145736 | tf_op jit(solution)/shard_map/ppermute | solution.py:212
  80.1 16.2 %collective-permute-start.17 = (bf16[32,32,128]{2,1,0:T(8,128)(2,1)S(1)}, bf16[32,32,128]{2,1,0:T(8,128)(2,1)S(1)}, u32[]{:S(2)}, u32[]{:S(2)}) collective-permute-start(bf16[32,32,128]{2,1,0:T(8,128)(2,1)S(1)} %get-tuple-element.71), channel_id=1, source_target_pairs={{0,3},{1,2},{2,1},{3,0},{4,7},{5,6},{6,5},{7,4},{8,11},{9,10},{10,... | collective-permute-start | bytes 786440 | tf_op jit(solution)/shard_map/ppermute | solution.py:212
  85.0 12.7 %collective-permute-start.21 = (bf16[32,32,128]{2,1,0:T(8,128)(2,1)S(1)}, bf16[32,32,128]{2,1,0:T(8,128)(2,1)S(1)}, u32[]{:S(2)}, u32[]{:S(2)}) collective-permute-start(bf16[32,32,128]{2,1,0:T(8,128)(2,1)S(1)} %get-tuple-element.77), channel_id=1, source_target_pairs={{0,1},{1,0},{2,3},{3,2},{4,5},{5,4},{6,7},{7,6},{8,9},{9,8},{10,11... | collective-permute-start | bytes 786440 | tf_op jit(solution)/shard_map/ppermute | solution.py:212
  85.1 16.7 %collective-permute-start.22 = (bf16[32,32,128]{2,1,0:T(8,128)(2,1)S(1)}, bf16[32,32,128]{2,1,0:T(8,128)(2,1)S(1)}, u32[]{:S(2)}, u32[]{:S(2)}) collective-permute-start(bf16[32,32,128]{2,1,0:T(8,128)(2,1)S(1)} %get-tuple-element.78), channel_id=1, source_target_pairs={{0,2},{1,3},{2,0},{3,1},{4,6},{5,7},{6,4},{7,5},{8,10},{9,11},{10,... | collective-permute-start | bytes 786440 | tf_op jit(solution)/shard_map/ppermute | solution.py:212
  90.6 16.9 %collective-permute-start.23 = (bf16[32,32,128]{2,1,0:T(8,128)(2,1)S(1)}, bf16[32,32,128]{2,1,0:T(8,128)(2,1)S(1)}, u32[]{:S(2)}, u32[]{:S(2)}) collective-permute-start(bf16[32,32,128]{2,1,0:T(8,128)(2,1)S(1)} %get-tuple-element.79), channel_id=1, source_target_pairs={{0,3},{1,2},{2,1},{3,0},{4,7},{5,6},{6,5},{7,4},{8,11},{9,10},{10,... | collective-permute-start | bytes 786440 | tf_op jit(solution)/shard_map/ppermute | solution.py:212
  96.3 30.9 %collective-permute-start.33 = (bf16[4,2,32,16,128]{4,3,2,1,0:T(8,128)(2,1)S(1)}, bf16[4,2,32,16,128]{4,3,2,1,0:T(8,128)(2,1)}, u32[]{:S(2)}, u32[]{:S(2)}) collective-permute-start(bf16[4,2,32,16,128]{4,3,2,1,0:T(8,128)(2,1)S(1)} %get-tuple-element.89), channel_id=1, source_target_pairs={{0,4},{4,0},{8,12},{12,8},{16,20},{20,16},{24,28},{28,24},{1,5},{5... | collective-permute-start | bytes 3145736 | tf_op jit(solution)/shard_map/ppermute | solution.py:212
  97.7 51.8 %collective-permute-start.24 = (bf16[4,2,32,16,128]{4,3,2,1,0:T(8,128)(2,1)S(1)}, bf16[4,2,32,16,128]{4,3,2,1,0:T(8,128)(2,1)S(1)}, u32[]{:S(2)}, u32[]{:S(2)}) collective-permute-start(bf16[4,2,32,16,128]{4,3,2,1,0:T(8,128)(2,1)S(1)} %get-tuple-element.83), channel_id=1, source_target_pairs={{0,4},{4,0},{8,12},{12,8},{16,20},{20,16},{24,28},{28,24},{1,5},{5... | collective-permute-start | bytes 3145736 | tf_op jit(solution)/shard_map/ppermute | solution.py:212
  107.5 3.3 %copy-start.4 = (bf16[2,32,128,128]{3,2,1,0:T(8,128)(2,1)S(1)}, bf16[2,32,128,128]{3,2,1,0:T(8,128)(2,1)}, u32[]{:S(2)}) copy-start(bf16[2,32,128,128]{3,2,1,0:T(8,128)(2,1)} %ur_ref.1) | copy-start | bytes 6291460
  109.2 61.6 %collective-permute-start.27 = (bf16[4,2,32,16,128]{4,3,2,1,0:T(8,128)(2,1)S(1)}, bf16[4,2,32,16,128]{4,3,2,1,0:T(8,128)(2,1)S(1)}, u32[]{:S(2)}, u32[]{:S(2)}) collective-permute-start(bf16[4,2,32,16,128]{4,3,2,1,0:T(8,128)(2,1)S(1)} %get-tuple-element.85), channel_id=1, source_target_pairs={{0,4},{4,0},{8,12},{12,8},{16,20},{20,16},{24,28},{28,24},{1,5},{5... | collective-permute-start | bytes 3145736 | tf_op jit(solution)/shard_map/ppermute | solution.py:212
  114.8 58.1 %collective-permute-start.31 = (bf16[2,2,32,16,128]{4,3,2,1,0:T(8,128)(2,1)S(1)}, bf16[2,2,32,16,128]{4,3,2,1,0:T(8,128)(2,1)S(1)}, u32[]{:S(2)}, u32[]{:S(2)}) collective-permute-start(bf16[2,2,32,16,128]{4,3,2,1,0:T(8,128)(2,1)S(1)} %slice_bitcast_fusion.2), channel_id=1, source_target_pairs={{0,8},{4,12},{8,0},{12,4},{16,24},{20,28},{24,16},{28,20},{1,9},{5... | collective-permute-start | bytes 1572872 | tf_op jit(solution)/shard_map/ppermute | solution.py:212
  128.8 47.1 %collective-permute-start.34 = (bf16[2,2,32,16,128]{4,3,2,1,0:T(8,128)(2,1)S(1)}, bf16[2,2,32,16,128]{4,3,2,1,0:T(8,128)(2,1)S(1)}, u32[]{:S(2)}, u32[]{:S(2)}) collective-permute-start(bf16[2,2,32,16,128]{4,3,2,1,0:T(8,128)(2,1)S(1)} %slice_bitcast_fusion), channel_id=1, source_target_pairs={{0,8},{4,12},{8,0},{12,4},{16,24},{20,28},{24,16},{28,20},{1,9},{5... | collective-permute-start | bytes 1572872 | tf_op jit(solution)/shard_map/ppermute | solution.py:212
  149.9 26.4 %collective-permute-start.25 = (bf16[2,2,32,16,128]{4,3,2,1,0:T(8,128)(2,1)S(1)}, bf16[2,2,32,16,128]{4,3,2,1,0:T(8,128)(2,1)S(1)}, u32[]{:S(2)}, u32[]{:S(2)}) collective-permute-start(bf16[2,2,32,16,128]{4,3,2,1,0:T(8,128)(2,1)S(1)} %slice_bitcast_fusion.6), channel_id=1, source_target_pairs={{0,8},{4,12},{8,0},{12,4},{16,24},{20,28},{24,16},{28,20},{1,9},{5... | collective-permute-start | bytes 1572872 | tf_op jit(solution)/shard_map/ppermute | solution.py:212
  171.2 23.6 %collective-permute-start.28 = (bf16[2,2,32,16,128]{4,3,2,1,0:T(8,128)(2,1)S(1)}, bf16[2,2,32,16,128]{4,3,2,1,0:T(8,128)(2,1)S(1)}, u32[]{:S(2)}, u32[]{:S(2)}) collective-permute-start(bf16[2,2,32,16,128]{4,3,2,1,0:T(8,128)(2,1)S(1)} %slice_bitcast_fusion.4), channel_id=1, source_target_pairs={{0,8},{4,12},{8,0},{12,4},{16,24},{20,28},{24,16},{28,20},{1,9},{5... | collective-permute-start | bytes 1572872 | tf_op jit(solution)/shard_map/ppermute | solution.py:212
  173.1 22.8 %collective-permute-start.32 = (bf16[1,2,32,16,128]{4,3,2,1,0:T(8,128)(2,1)S(1)}, bf16[1,2,32,16,128]{4,3,2,1,0:T(8,128)(2,1)S(1)}, u32[]{:S(2)}, u32[]{:S(2)}) collective-permute-start(bf16[1,2,32,16,128]{4,3,2,1,0:T(8,128)(2,1)S(1)} %slice_bitcast_fusion.16), channel_id=1, source_target_pairs={{0,16},{4,20},{8,24},{12,28},{16,0},{20,4},{24,8},{28,12},{1,17},{... | collective-permute-start | bytes 786440 | tf_op jit(solution)/shard_map/ppermute | solution.py:212
  176.0 35.3 %collective-permute-start.35 = (bf16[1,2,32,16,128]{4,3,2,1,0:T(8,128)(2,1)S(1)}, bf16[1,2,32,16,128]{4,3,2,1,0:T(8,128)(2,1)S(1)}, u32[]{:S(2)}, u32[]{:S(2)}) collective-permute-start(bf16[1,2,32,16,128]{4,3,2,1,0:T(8,128)(2,1)S(1)} %slice_bitcast_fusion.13), channel_id=1, source_target_pairs={{0,16},{4,20},{8,24},{12,28},{16,0},{20,4},{24,8},{28,12},{1,17},{... | collective-permute-start | bytes 786440 | tf_op jit(solution)/shard_map/ppermute | solution.py:212
  176.5 40.5 %collective-permute-start.26 = (bf16[1,2,32,16,128]{4,3,2,1,0:T(8,128)(2,1)S(1)}, bf16[1,2,32,16,128]{4,3,2,1,0:T(8,128)(2,1)S(1)}, u32[]{:S(2)}, u32[]{:S(2)}) collective-permute-start(bf16[1,2,32,16,128]{4,3,2,1,0:T(8,128)(2,1)S(1)} %slice_bitcast_fusion.22), channel_id=1, source_target_pairs={{0,16},{4,20},{8,24},{12,28},{16,0},{20,4},{24,8},{28,12},{1,17},{... | collective-permute-start | bytes 786440 | tf_op jit(solution)/shard_map/ppermute | solution.py:212
  195.0 25.3 %collective-permute-start.29 = (bf16[1,2,32,16,128]{4,3,2,1,0:T(8,128)(2,1)S(1)}, bf16[1,2,32,16,128]{4,3,2,1,0:T(8,128)(2,1)S(1)}, u32[]{:S(2)}, u32[]{:S(2)}) collective-permute-start(bf16[1,2,32,16,128]{4,3,2,1,0:T(8,128)(2,1)S(1)} %slice_bitcast_fusion.19), channel_id=1, source_target_pairs={{0,16},{4,20},{8,24},{12,28},{16,0},{20,4},{24,8},{28,12},{1,17},{... | collective-permute-start | bytes 786440 | tf_op jit(solution)/shard_map/ppermute | solution.py:212

commit v2 on v1

v2 whole, which is shorter than its diff:
```python
import functools

import jax
import jax.numpy as jnp
from jax import lax
from jax.experimental import pallas as pl
from jax.experimental.pallas import tpu as pltpu
from jax.sharding import PartitionSpec as P

gelu_root = 0.7978845608
gelu_cube = 0.044715
F32 = jnp.float32
BF16 = jnp.bfloat16


def mm(lhs, rhs, ldim, rdim):
    return lax.dot_general(lhs, rhs, (((ldim,), (rdim,)), ((), ())), preferred_element_type=F32)


def send_panel(outs, kind, scratch, me, blocks):
    span = blocks * blocks
    for k, out in enumerate(outs):
        start = pl.multiple_of((me ^ k) * span, span)
        rows = scratch[pl.ds(start, span), :]
        out[kind] = rows.reshape(out.shape[1:]).astype(BF16)


def gather_rows(parts, kind, scratch, slot, me, block, blocks):
    for k, part in enumerate(parts):
        start = pl.multiple_of((me ^ k) * blocks, blocks)
        scratch[slot, pl.ds(start, blocks), :] = part[kind, block].astype(F32)
    return scratch[slot].astype(BF16)


def hop_order(ways, kind):
    bits = [1 << b for b in range(ways.bit_length() - 1)]
    return [bits[1], bits[0]] + bits[2:] if kind and len(bits) > 1 else bits


def store_grad(outs, kind, block, value, scratch, slot, me, ways):
    rows = value.shape[0] // ways
    first, *later = hop_order(ways, kind)
    scratch[slot] = value
    for p in range(ways // 2):
        rel = sum(bit for t, bit in enumerate(later) if p >> t & 1)
        for out, target in ((outs[2 * kind], rel), (outs[2 * kind + 1], rel + first)):
            start = pl.multiple_of((me ^ target) * rows, rows)
            out[p, block] = scratch[slot, pl.ds(start, rows), :].astype(BF16)


def panels_kernel(ways, me_ref, x_ref, g_ref, ur_ref, dl_ref, *rest):
    outs, scr_r, scr_b = rest[:ways], rest[ways], rest[ways + 1]
    blocks, width = ur_ref.shape[1], ur_ref.shape[2]
    me = me_ref[0]
    for i in range(blocks):
        cols = slice(i * width, (i + 1) * width)
        scr_r[pl.ds(i, width, stride=blocks), :] = mm(ur_ref[0, i], x_ref[:, cols], 0, 1)
        scr_b[pl.ds(i, width, stride=blocks), :] = mm(dl_ref[0, i], g_ref[:, cols], 1, 1)
    send_panel(outs, 0, scr_r, me, blocks)
    send_panel(outs, 1, scr_b, me, blocks)


def full_spec(shape):
    return pl.BlockSpec(shape, lambda s: (0,) * len(shape))


def group_spec(w, q):
    return pl.BlockSpec((1,) + w.shape[1:], lambda s: (q, 0, 0, 0))


def limits(flops, mib):
    return dict(
        compiler_params=pltpu.CompilerParams(vmem_limit_bytes=40 * 2**20),
        cost_estimate=pl.CostEstimate(flops=flops * 8, bytes_accessed=mib * 2**20, transcendentals=0),
    )


def make_panels(me, x, g, ur, dl, q, ways):
    tok, blocks, width = x.shape[0], ur.shape[1], ur.shape[2]
    part = jax.ShapeDtypeStruct((2, blocks, blocks, tok), BF16)
    return pl.pallas_call(
        functools.partial(panels_kernel, ways),
        out_shape=[part] * ways,
        grid=(1,),
        in_specs=[
            pl.BlockSpec(memory_space=pltpu.SMEM),
            full_spec(x.shape),
            full_spec(g.shape),
            group_spec(ur, q),
            group_spec(dl, q),
        ],
        out_specs=[full_spec(part.shape)] * ways,
        scratch_shapes=[pltpu.VMEM((width * blocks, tok), F32)] * 2,
        **limits(4 * tok * blocks * width * width, 8),
    )(me, x, g, ur, dl)


UNROLL = 4


def middle_kernel(mp_ways, dp_ways, me_ref, ul_ref, df_ref, *rest):
    n = mp_ways
    first_in, outs, grads = rest[:n], rest[n : 2 * n], rest[2 * n : 2 * n + 4]
    scr_d, scr_u, asm_r, asm_b, gr1, gr2 = rest[2 * n + 4 :]
    blocks, width = ul_ref.shape[1], ul_ref.shape[2]
    me_mp, me_dp = me_ref[0], me_ref[1]

    def one(c, slot):
        ul, df = ul_ref[0, c], df_ref[0, c]
        cu = gather_rows(first_in, 0, asm_r, slot, me_mp, c, blocks)
        dg = gather_rows(first_in, 1, asm_b, slot, me_mp, c, blocks)
        pre = mm(ul, cu, 0, 0)
        sq = pre * pre
        th = jnp.tanh(gelu_root * (pre + gelu_cube * sq * pre))
        half = 0.5 * (1.0 + th)
        hidden = (pre * half).astype(BF16)
        slope = half + 0.5 * pre * (1.0 - th * th) * (gelu_root * (1.0 + 3.0 * gelu_cube * sq))
        scr_d[pl.ds(c, width, stride=blocks), :] = mm(df, hidden, 0, 0)
        pg = (mm(df, dg, 1, 0) * slope).astype(BF16)
        scr_u[pl.ds(c, width, stride=blocks), :] = mm(ul, pg, 1, 0)
        store_grad(grads, 0, c, mm(hidden, dg, 1, 1), gr1, slot, me_dp, dp_ways)
        store_grad(grads, 1, c, mm(cu, pg, 1, 1), gr2, slot, me_dp, dp_ways)

    def step(s, carry):
        for slot in range(UNROLL):
            one(s * UNROLL + slot, slot)
        return carry

    lax.fori_loop(0, blocks // UNROLL, step, 0)
    send_panel(outs, 0, scr_d, me_mp, blocks)
    send_panel(outs, 1, scr_u, me_mp, blocks)


def grad_halves(blocks, width, dp_ways):
    return jax.ShapeDtypeStruct((dp_ways // 2, blocks, width // dp_ways, width), BF16)


def make_middle(me, first_in, ul, df, q, dp_ways):
    n = len(first_in)
    part = jax.ShapeDtypeStruct(first_in[0].shape, BF16)
    blocks, width, tok = ul.shape[1], ul.shape[2], part.shape[3]
    half = grad_halves(blocks, width, dp_ways)
    res = pl.pallas_call(
        functools.partial(middle_kernel, n, dp_ways),
        out_shape=[part] * n + [half] * 4,
        grid=(1,),
        in_specs=[pl.BlockSpec(memory_space=pltpu.SMEM)] + [group_spec(ul, q)] * 2 + [full_spec(part.shape)] * n,
        out_specs=[full_spec(part.shape)] * n + [full_spec(half.shape)] * 4,
        scratch_shapes=[pltpu.VMEM((width * blocks, tok), F32)] * 2
        + [pltpu.VMEM((UNROLL, width, tok), F32)] * 2
        + [pltpu.VMEM((UNROLL, width, width), F32)] * 2,
        **limits(12 * tok * blocks * width * width, 8),
    )(me, ul, df, *first_in)
    return res[:n], res[n:]


def last_grads_kernel(mp_ways, dp_ways, me_ref, x_ref, g_ref, *rest):
    n = mp_ways
    second_in, grads = rest[:n], rest[n : n + 4]
    asm_d, asm_u, gr1, gr2 = rest[n + 4 :]
    blocks = second_in[0].shape[1]
    width = gr1.shape[1]
    me_mp, me_dp = me_ref[0], me_ref[1]
    for e in range(blocks):
        cols = slice(e * width, (e + 1) * width)
        slot = e % UNROLL
        cd = gather_rows(second_in, 0, asm_d, slot, me_mp, e, blocks)
        rg = gather_rows(second_in, 1, asm_u, slot, me_mp, e, blocks)
        store_grad(grads, 0, e, mm(cd, g_ref[:, cols], 1, 0), gr1, slot, me_dp, dp_ways)
        store_grad(grads, 1, e, mm(rg, x_ref[:, cols], 1, 0).T, gr2, slot, me_dp, dp_ways)


def make_last_grads(me, second_in, x, g, width, dp_ways):
    n = len(second_in)
    part = second_in[0]
    blocks, tok = part.shape[1], part.shape[3]
    half = grad_halves(blocks, width, dp_ways)
    return pl.pallas_call(
        functools.partial(last_grads_kernel, n, dp_ways),
        out_shape=[half] * 4,
        grid=(1,),
        in_specs=[pl.BlockSpec(memory_space=pltpu.SMEM)] + [full_spec(x.shape)] * 2 + [full_spec(part.shape)] * n,
        out_specs=[full_spec(half.shape)] * 4,
        scratch_shapes=[pltpu.VMEM((UNROLL, width, tok), F32)] * 2 + [pltpu.VMEM((UNROLL, width, width), F32)] * 2,
        **limits(4 * tok * blocks * width * width, 6),
    )(me, x, g, *second_in)


def outputs_kernel(mp_ways, me_ref, dl_ref, ur_ref, *rest):
    n = mp_ways
    groups = dl_ref.shape[0]
    second_in = rest[: groups * n]
    mixed, tgrad, asm_d, asm_u = rest[groups * n :]
    blocks, width = dl_ref.shape[1], dl_ref.shape[2]
    me_mp = me_ref[0]
    for e in range(blocks):
        cols = slice(e * width, (e + 1) * width)
        out_sum = grad_sum = None
        for q in range(groups):
            parts = second_in[q * n : (q + 1) * n]
            slot = (e * groups + q) % UNROLL
            cd = gather_rows(parts, 0, asm_d, slot, me_mp, e, blocks)
            rg = gather_rows(parts, 1, asm_u, slot, me_mp, e, blocks)
            one = mm(cd, dl_ref[q, e], 0, 0)
            two = mm(ur_ref[q, e], rg, 1, 0)
            out_sum = one if q == 0 else out_sum + one
            grad_sum = two if q == 0 else grad_sum + two
        mixed[:, cols] = out_sum.astype(BF16)
        tgrad[:, cols] = grad_sum.T.astype(BF16)


def make_outputs(me, second_in, dl, ur):
    n = len(second_in[0])
    part = second_in[0][0]
    groups, blocks, width, tok = dl.shape[0], dl.shape[1], dl.shape[2], part.shape[3]
    out = jax.ShapeDtypeStruct((tok, blocks * width), BF16)
    return pl.pallas_call(
        functools.partial(outputs_kernel, n),
        out_shape=[out] * 2,
        grid=(1,),
        in_specs=[pl.BlockSpec(memory_space=pltpu.SMEM)]
        + [full_spec(dl.shape)] * 2
        + [full_spec(part.shape)] * (n * groups),
        out_specs=[full_spec(out.shape)] * 2,
        scratch_shapes=[pltpu.VMEM((UNROLL, width, tok), F32)] * 2,
        **limits(8 * tok * blocks * width * width, 10),
    )(me, dl, ur, *[p for parts in second_in for p in parts])


def xor_permute(array, axis, k):
    return lax.ppermute(array, axis, [(i, i ^ k) for i in range(lax.axis_size(axis))])


def exchange(parts):
    return [p if k == 0 else xor_permute(p, "mp", k) for k, p in enumerate(parts)]


def halving_sums(halves, scale):
    ways = lax.axis_size("dp")
    pairs = [[halves[0], halves[1]], [halves[2], halves[3]]]
    orders = [hop_order(ways, kind) for kind in range(2)]
    sums = [None, None]
    for hop in range(len(orders[0])):
        for kind in range(2):
            keep, send = pairs[kind]
            got = xor_permute(send, "dp", orders[kind][hop])
            total = keep.astype(F32) + got.astype(F32)
            if total.shape[0] == 1:
                sums[kind] = total[0] * scale
                continue
            total = total.astype(BF16).reshape((total.shape[0] // 2, 2) + total.shape[1:])
            pairs[kind] = [total[:, 0], total[:, 1]]
    return sums


def body(tokens, cotangent, up_right, up_left, down_first_factor, down_left):
    groups, width = up_right.shape[0], up_right.shape[2]
    mp_ways, dp_ways = lax.axis_size("mp"), lax.axis_size("dp")
    scale = (dp_ways * tokens.shape[0]) ** (-0.5)
    me = jnp.stack([lax.axis_index("mp"), lax.axis_index("dp")]).astype(jnp.int32)
    firsts, seconds, mid_sums, last_sums = [], [], [], []
    for q in range(groups):
        firsts.append(exchange(make_panels(me, tokens, cotangent, up_right, down_left, q, mp_ways)))
    for q in range(groups):
        panels, halves = make_middle(me, firsts[q], up_left, down_first_factor, q, dp_ways)
        seconds.append(exchange(panels))
        mid_sums.append(halving_sums(halves, scale))
    for q in range(groups):
        halves = make_last_grads(me, seconds[q], tokens, cotangent, width, dp_ways)
        last_sums.append(halving_sums(halves, scale))
    mixed, tokens_grad = make_outputs(me, seconds, down_left, up_right)

    def pick(sums, kind):
        return jnp.stack([s[kind] for s in sums])

    return (mixed, tokens_grad, pick(last_sums, 1), pick(mid_sums, 1), pick(mid_sums, 0), pick(last_sums, 0))


def solution(mesh):
    weight = P(None, "mp", None, None)
    in_specs = (P("dp", "mp"), P("dp", "mp"), weight, weight, weight, weight)
    grad = P(None, "mp", "dp", None)
    out_specs = (P("dp", "mp"), P("dp", "mp"), grad, grad, grad, grad)
    return jax.shard_map(body, mesh=mesh, in_specs=in_specs, out_specs=out_specs, check_vma=False)
```

time: 222 us -> 199 us (0.90)
  waiting for transfers between devices: 123 us -> 107 us
  Pallas kernels: 49.8 us -> 39.4 us
  local copies, waits for them, and re-layouts: 3.34 us -> 6.26 us
    ppermute x36, waiting for transfers between devices: 123 us -> 107 us  [xor_permute(): lax.ppermute(array, axis, [(i, i ^ k) for i in range(lax.axis_size(axis))])]
    pallas_call x2, Pallas kernels: 32.7 us -> 21.9 us  [make_middle(): pl.pallas_call(functools.partial(middle_kernel, n, dp_ways), out_shape=[p...]
    unnamed x16 -> x18, local copies, waits for them, and re-layouts: 2.98 us -> 6.03 us
    pallas_call x4 -> x2, Pallas kernels: 9.88 us -> 10.1 us  [make_panels(): pl.pallas_call(functools.partial(panels_kernel, ways), out_shape=[part] *...]
  transfers between devices with their start and end apart: 36 -> 36, of which waited for: 16 -> 21; matrix products, arithmetic and copies ran while one was open for 2% -> 2% of each run, Pallas kernels for 21% -> 17%
where the time goes in v2:
time: 199 us
  waiting for transfers between devices  107 us (54%)
  starting transfers between devices  40 us (20%)
  Pallas kernels  39.4 us (20%)
  local copies, waits for them, and re-layouts  6.26 us (3%)
  other arithmetic  5.39 us (3%)
    ppermute x36, waiting for transfers between devices, xor_permute(): lax.ppermute(array, axis, [(i, i ^ k) for i in range(lax.axis_size(axis))])  107 us
    ppermute x36, starting transfers between devices, xor_permute(): lax.ppermute(array, axis, [(i, i ^ k) for i in range(lax.axis_size(axis))])  40 us
    pallas_call x2, Pallas kernels, make_middle(): pl.pallas_call(functools.partial(middle_kernel, n, dp_ways), out_shape=[p...  21.9 us
    pallas_call x2, Pallas kernels, make_panels(): pl.pallas_call(functools.partial(panels_kernel, ways), out_shape=[part] *...  10.1 us
    unnamed x18, local copies, waits for them, and re-layouts  6.03 us
  transfers between devices with their start and end apart: 36, of which 21 were waited for; matrix products, arithmetic and copies ran while one was open for 2% of the time, Pallas kernels for 17%

profile of v2, /device:TPU:0, one launch (start us, length us, event | category | flops | bytes accessed | tf_op | source)
XLA Modules:
  0.0 199.1 jit_solution(18316576459332629908)
XLA Ops:
  0.7 1.6 copy-done.2
  2.3 1.6 copy-done.4
  6.3 5.1 %shard_map.109 = (bf16[2,32,32,128]{3,2,1,0:T(8,128)(2,1)S(1)}, bf16[2,32,32,128]{3,2,1,0:T(8,128)(2,1)S(1)}, bf16[2,32,32,128]{3,2,1,0:T(8,128)(2,1)S(1)}, bf16[2,32,32,128]{3,2,1,0:T(8,128)(2,1)S(1)}) custom-call(s32[2]{0:T(128)S(1)} %pad_add_fusion.me_ref, bf16[128,4096]{1,0:T(8,128)(2,1)S(1)} %copy-done.6, bf16[128,4096]{1,0:T(8,128)(2,1)S(1)} %copy-done.8, ...), custom_call_target="tpu_custom_call" | custom-call | flops 2147483648 | bytes 8388608 | tf_op jit(solution)/shard_map/pallas_call | solution.py:81
  11.9 2.6 %collective-permute-start.1 = (bf16[2,32,32,128]{3,2,1,0:T(8,128)(2,1)S(1)}, bf16[2,32,32,128]{3,2,1,0:T(8,128)(2,1)S(1)}, u32[]{:S(2)}, u32[]{:S(2)}) collective-permute-start(bf16[2,32,32,128]{3,2,1,0:T(8,128)(2,1)S(1)} %get-tuple-element.42), channel_id=1, source_target_pairs={{0,2},{1,3},{2,0},{3,1},{4,6},{5,7},{6,4},{7,5},{8,10},{9,11},{10,... | collective-permute-start | bytes 1572872 | tf_op jit(solution)/shard_map/ppermute | solution.py:231
  14.6 5.1 %shard_map.111 = (bf16[2,32,32,128]{3,2,1,0:T(8,128)(2,1)S(1)}, bf16[2,32,32,128]{3,2,1,0:T(8,128)(2,1)S(1)}, bf16[2,32,32,128]{3,2,1,0:T(8,128)(2,1)S(1)}, bf16[2,32,32,128]{3,2,1,0:T(8,128)(2,1)S(1)}) custom-call(s32[2]{0:T(128)S(1)} %pad_add_fusion.me_ref, bf16[128,4096]{1,0:T(8,128)(2,1)S(1)} %copy-done.6, bf16[128,4096]{1,0:T(8,128)(2,1)S(1)} %copy-done.8, ...), custom_call_target="tpu_custom_call" | custom-call | flops 2147483648 | bytes 8388608 | tf_op jit(solution)/shard_map/pallas_call | solution.py:81
  19.9 1.9 collective-permute-start.7
  21.8 5.5 %collective-permute-done.1.rest_2_ = bf16[2,32,32,128]{3,2,1,0:T(8,128)(2,1)S(1)} collective-permute-done((bf16[2,32,32,128]{3,2,1,0:T(8,128)(2,1)S(1)}, bf16[2,32,32,128]{3,2,1,0:T(8,128)(2,1)S(1)}, u32[]{:S(2)}, u32[]{:S(2)}) %collective-permute-start.1) | collective-permute-done | bytes 524320 | tf_op jit(solution)/shard_map/ppermute | solution.py:231
  27.3 10.7 %collective-permute-done.2.rest_3_ = bf16[2,32,32,128]{3,2,1,0:T(8,128)(2,1)S(1)} collective-permute-done((bf16[2,32,32,128]{3,2,1,0:T(8,128)(2,1)S(1)}, bf16[2,32,32,128]{3,2,1,0:T(8,128)(2,1)S(1)}, u32[]{:S(2)}, u32[]{:S(2)}) %collective-permute-start.2) | collective-permute-done | bytes 524320 | tf_op jit(solution)/shard_map/ppermute | solution.py:231
  38.0 11.0 %shard_map.110 = (bf16[2,32,32,128]{3,2,1,0:T(8,128)(2,1)S(1)}, bf16[2,32,32,128]{3,2,1,0:T(8,128)(2,1)S(1)}, bf16[2,32,32,128]{3,2,1,0:T(8,128)(2,1)S(1)}, bf16...) custom-call(s32[2]{0:T(128)S(1)} %pad_add_fusion.me_ref, ...), custom_call_target="tpu_custom_call" | custom-call | flops 6442450944 | bytes 8388608 | tf_op jit(solution)/shard_map/pallas_call | solution.py:143
  49.5 2.0 collective-permute-start.4
  51.4 1.6 collective-permute-start.18
  53.1 7.4 %collective-permute-done.8.rest_3_ = bf16[2,32,32,128]{3,2,1,0:T(8,128)(2,1)S(1)} collective-permute-done((bf16[2,32,32,128]{3,2,1,0:T(8,128)(2,1)S(1)}, bf16[2,32,32,128]{3,2,1,0:T(8,128)(2,1)S(1)}, u32[]{:S(2)}, u32[]{:S(2)}) %collective-permute-start.8) | collective-permute-done | bytes 524320 | tf_op jit(solution)/shard_map/ppermute | solution.py:231
  60.5 1.6 collective-permute-start.24
  62.1 10.9 %shard_map.112 = (bf16[2,32,32,128]{3,2,1,0:T(8,128)(2,1)S(1)}, bf16[2,32,32,128]{3,2,1,0:T(8,128)(2,1)S(1)}, bf16[2,32,32,128]{3,2,1,0:T(8,128)(2,1)S(1)}, bf16...) custom-call(s32[2]{0:T(128)S(1)} %pad_add_fusion.me_ref, ...), custom_call_target="tpu_custom_call" | custom-call | flops 6442450944 | bytes 8388608 | tf_op jit(solution)/shard_map/pallas_call | solution.py:143
  73.9 1.3 collective-permute-done.24
  75.2 1.7 collective-permute-start.21
  77.0 1.6 collective-permute-start.10
  78.6 4.3 %collective-permute-done.5.rest_3_ = bf16[2,32,32,128]{3,2,1,0:T(8,128)(2,1)S(1)} collective-permute-done((bf16[2,32,32,128]{3,2,1,0:T(8,128)(2,1)S(1)}, bf16[2,32,32,128]{3,2,1,0:T(8,128)(2,1)S(1)}, u32[]{:S(2)}, u32[]{:S(2)}) %collective-permute-start.5) | collective-permute-done | bytes 524320 | tf_op jit(solution)/shard_map/ppermute | solution.py:231
  82.9 1.6 collective-permute-start.27
  84.5 1.8 shard_map.114
  86.4 2.7 %collective-permute-done.21 = bf16[4,32,16,128]{3,2,1,0:T(8,128)(2,1)S(1)} collective-permute-done((bf16[4,32,16,128]{3,2,1,0:T(8,128)(2,1)S(1)}, bf16[4,32,16,128]{3,2,1,0:T(8,128)(2,1)S(1)}, u32[]{:S(2)}, u32[]{:S(2)}) %collective-permute-start.21) | collective-permute-done | bytes 524320 | tf_op jit(solution)/shard_map/ppermute | solution.py:231
  89.1 1.7 collective-permute-start.19
  91.0 1.6 collective-permute-start.25
  92.6 2.1 %collective-permute-done.10.rest_6_.rest_2_ = bf16[2,32,32,128]{3,2,1,0:T(8,128)(2,1)S(1)} collective-permute-done((bf16[2,32,32,128]{3,2,1,0:T(8,128)(2,1)S(1)}, bf16[2,32,32,128]{3,2,1,0:T(8,128)(2,1)S(1)}, u32[]{:S(2)}, u32[]{:S(2)}) %collective-permute-start.10) | collective-permute-done | bytes 524320 | tf_op jit(solution)/shard_map/ppermute | solution.py:231
  94.7 2.0 %collective-permute-start.12 = (bf16[4,32,16,128]{3,2,1,0:T(8,128)(2,1)S(1)}, bf16[4,32,16,128]{3,2,1,0:T(8,128)(2,1)S(1)}, u32[]{:S(2)}, u32[]{:S(2)}) collective-permute-start(bf16[4,32,16,128]{3,2,1,0:T(8,128)(2,1)S(1)} %get-tuple-element.59), channel_id=1, source_target_pairs={{0,8},{4,12},{8,0},{12,4},{16,24},{20,28},{24,16},{28,20},{1,9},{5... | collective-permute-start | bytes 1572872 | tf_op jit(solution)/shard_map/ppermute | solution.py:231
  96.7 8.7 %collective-permute-done.11.rest_7_.rest_3_ = bf16[2,32,32,128]{3,2,1,0:T(8,128)(2,1)S(1)} collective-permute-done((bf16[2,32,32,128]{3,2,1,0:T(8,128)(2,1)S(1)}, bf16[2,32,32,128]{3,2,1,0:T(8,128)(2,1)S(1)}, u32[]{:S(2)}, u32[]{:S(2)}) %collective-permute-start.11) | collective-permute-done | bytes 524320 | tf_op jit(solution)/shard_map/ppermute | solution.py:231
  105.4 1.6 collective-permute-start.30
  107.0 1.8 shard_map.115
  109.2 3.7 %shard_map.113 = (bf16[128,4096]{1,0:T(8,128)(2,1)}, bf16[128,4096]{1,0:T(8,128)(2,1)}) custom-call(s32[2]{0:T(128)S(1)} %pad_add_fusion.me_ref, bf16[2,32,128,128]{3,2,1,0:T(8,128)(2,1)S(1)} %copy-done.3, bf16[2,32,128,128]{3,2,1,0:T(8,128)(2,1)S(1)} %copy-done.5, bf16[2,32,32,128]{3,2,1,0:T(8,128)(2,1)S(1)} %get-tuple-element.44.rest_0_, ...), custom_call_target="tpu_custom_call" | custom-call | flops 4294967296 | bytes 10485760 | tf_op jit(solution)/shard_map/pallas_call | solution.py:217
  112.9 1.6 collective-permute-start.15
  115.4 1.6 collective-permute-start.33
  117.0 8.7 %collective-permute-done.22 = bf16[2,32,16,128]{3,2,1,0:T(8,128)(2,1)S(1)} collective-permute-done((bf16[2,32,16,128]{3,2,1,0:T(8,128)(2,1)S(1)}, bf16[2,32,16,128]{3,2,1,0:T(8,128)(2,1)S(1)}, u32[]{:S(2)}, u32[]{:S(2)}) %collective-permute-start.22) | collective-permute-done | bytes 262176 | tf_op jit(solution)/shard_map/ppermute | solution.py:231
  125.8 1.6 collective-permute-start.28
  127.5 5.9 %collective-permute-done.28 = bf16[2,32,16,128]{3,2,1,0:T(8,128)(2,1)S(1)} collective-permute-done((bf16[2,32,16,128]{3,2,1,0:T(8,128)(2,1)S(1)}, bf16[2,32,16,128]{3,2,1,0:T(8,128)(2,1)S(1)}, u32[]{:S(2)}, u32[]{:S(2)}) %collective-permute-start.28) | collective-permute-done | bytes 262176 | tf_op jit(solution)/shard_map/ppermute | solution.py:231
  133.3 2.8 %collective-permute-start.20 = (bf16[1,32,16,128]{3,2,1,0:T(8,128)(2,1)S(1)}, bf16[1,32,16,128]{3,2,1,0:T(8,128)(2,1)S(1)}, u32[]{:S(2)}, u32[]{:S(2)}) collective-permute-start(bf16[1,32,16,128]{3,2,1,0:T(8,128)(2,1)S(1)} %slice_bitcast_fusion.26), channel_id=1, source_target_pairs={{0,16},{4,20},{8,24},{12,28},{16,0},{20,4},{24,8},{28,12},{1,17},{... | collective-permute-start | bytes 393224 | tf_op jit(solution)/shard_map/ppermute | solution.py:231
  136.2 4.9 %collective-permute-done.20 = bf16[1,32,16,128]{3,2,1,0:T(8,128)(2,1)S(1)} collective-permute-done((bf16[1,32,16,128]{3,2,1,0:T(8,128)(2,1)S(1)}, bf16[1,32,16,128]{3,2,1,0:T(8,128)(2,1)S(1)}, u32[]{:S(2)}, u32[]{:S(2)}) %collective-permute-start.20) | collective-permute-done | bytes 131104 | tf_op jit(solution)/shard_map/ppermute | solution.py:231
  142.1 7.0 %collective-permute-done.26 = bf16[1,32,16,128]{3,2,1,0:T(8,128)(2,1)S(1)} collective-permute-done((bf16[1,32,16,128]{3,2,1,0:T(8,128)(2,1)S(1)}, bf16[1,32,16,128]{3,2,1,0:T(8,128)(2,1)S(1)}, u32[]{:S(2)}, u32[]{:S(2)}) %collective-permute-start.26) | collective-permute-done | bytes 131104 | tf_op jit(solution)/shard_map/ppermute | solution.py:231
  149.2 9.5 %collective-permute-done.23 = bf16[1,32,16,128]{3,2,1,0:T(8,128)(2,1)S(1)} collective-permute-done((bf16[1,32,16,128]{3,2,1,0:T(8,128)(2,1)S(1)}, bf16[1,32,16,128]{3,2,1,0:T(8,128)(2,1)S(1)}, u32[]{:S(2)}, u32[]{:S(2)}) %collective-permute-start.23) | collective-permute-done | bytes 131104 | tf_op jit(solution)/shard_map/ppermute | solution.py:231
  159.5 5.7 %collective-permute-done.29 = bf16[1,32,16,128]{3,2,1,0:T(8,128)(2,1)S(1)} collective-permute-done((bf16[1,32,16,128]{3,2,1,0:T(8,128)(2,1)S(1)}, bf16[1,32,16,128]{3,2,1,0:T(8,128)(2,1)S(1)}, u32[]{:S(2)}, u32[]{:S(2)}) %collective-permute-start.29) | collective-permute-done | bytes 131104 | tf_op jit(solution)/shard_map/ppermute | solution.py:231
  166.8 2.1 %collective-permute-start.16 = (bf16[2,32,16,128]{3,2,1,0:T(8,128)(2,1)S(1)}, bf16[2,32,16,128]{3,2,1,0:T(8,128)(2,1)S(1)}, u32[]{:S(2)}, u32[]{:S(2)}) collective-permute-start(bf16[2,32,16,128]{3,2,1,0:T(8,128)(2,1)S(1)} %slice_bitcast_fusion.12), channel_id=1, source_target_pairs={{0,4},{4,0},{8,12},{12,8},{16,20},{20,16},{24,28},{28,24},{1,5},{5... | collective-permute-start | bytes 786440 | tf_op jit(solution)/shard_map/ppermute | solution.py:231
  169.0 2.1 %collective-permute-start.34 = (bf16[2,32,16,128]{3,2,1,0:T(8,128)(2,1)S(1)}, bf16[2,32,16,128]{3,2,1,0:T(8,128)(2,1)S(1)}, u32[]{:S(2)}, u32[]{:S(2)}) collective-permute-start(bf16[2,32,16,128]{3,2,1,0:T(8,128)(2,1)S(1)} %slice_bitcast_fusion), channel_id=1, source_target_pairs={{0,8},{4,12},{8,0},{12,4},{16,24},{20,28},{24,16},{28,20},{1,9},{5... | collective-permute-start | bytes 786440 | tf_op jit(solution)/shard_map/ppermute | solution.py:231
  171.1 3.1 %collective-permute-done.13 = bf16[2,32,16,128]{3,2,1,0:T(8,128)(2,1)S(1)} collective-permute-done((bf16[2,32,16,128]{3,2,1,0:T(8,128)(2,1)S(1)}, bf16[2,32,16,128]{3,2,1,0:T(8,128)(2,1)S(1)}, u32[]{:S(2)}, u32[]{:S(2)}) %collective-permute-start.13) | collective-permute-done | bytes 262176 | tf_op jit(solution)/shard_map/ppermute | solution.py:231
  174.4 4.0 %collective-permute-done.31 = bf16[2,32,16,128]{3,2,1,0:T(8,128)(2,1)S(1)} collective-permute-done((bf16[2,32,16,128]{3,2,1,0:T(8,128)(2,1)S(1)}, bf16[2,32,16,128]{3,2,1,0:T(8,128)(2,1)S(1)}, u32[]{:S(2)}, u32[]{:S(2)}) %collective-permute-start.31) | collective-permute-done | bytes 262176 | tf_op jit(solution)/shard_map/ppermute | solution.py:231
  178.7 3.0 %collective-permute-start.17 = (bf16[1,32,16,128]{3,2,1,0:T(8,128)(2,1)S(1)}, bf16[1,32,16,128]{3,2,1,0:T(8,128)(2,1)S(1)}, u32[]{:S(2)}, u32[]{:S(2)}) collective-permute-start(bf16[1,32,16,128]{3,2,1,0:T(8,128)(2,1)S(1)} %slice_bitcast_fusion.28), channel_id=1, source_target_pairs={{0,16},{4,20},{8,24},{12,28},{16,0},{20,4},{24,8},{28,12},{1,17},{... | collective-permute-start | bytes 393224 | tf_op jit(solution)/shard_map/ppermute | solution.py:231
  181.7 2.2 %collective-permute-done.34 = bf16[2,32,16,128]{3,2,1,0:T(8,128)(2,1)S(1)} collective-permute-done((bf16[2,32,16,128]{3,2,1,0:T(8,128)(2,1)S(1)}, bf16[2,32,16,128]{3,2,1,0:T(8,128)(2,1)S(1)}, u32[]{:S(2)}, u32[]{:S(2)}) %collective-permute-start.34) | collective-permute-done | bytes 262176 | tf_op jit(solution)/shard_map/ppermute | solution.py:231
  184.1 8.8 %collective-permute-done.14 = bf16[1,32,16,128]{3,2,1,0:T(8,128)(2,1)S(1)} collective-permute-done((bf16[1,32,16,128]{3,2,1,0:T(8,128)(2,1)S(1)}, bf16[1,32,16,128]{3,2,1,0:T(8,128)(2,1)S(1)}, u32[]{:S(2)}, u32[]{:S(2)}) %collective-permute-start.14) | collective-permute-done | bytes 131104 | tf_op jit(solution)/shard_map/ppermute | solution.py:231
  192.9 2.5 %collective-permute-done.32 = bf16[1,32,16,128]{3,2,1,0:T(8,128)(2,1)S(1)} collective-permute-done((bf16[1,32,16,128]{3,2,1,0:T(8,128)(2,1)S(1)}, bf16[1,32,16,128]{3,2,1,0:T(8,128)(2,1)S(1)}, u32[]{:S(2)}, u32[]{:S(2)}) %collective-permute-start.32) | collective-permute-done | bytes 131104 | tf_op jit(solution)/shard_map/ppermute | solution.py:231
  195.4 1.4 collective-permute-done.17
  (94 shorter events, 12.9 us)
Async XLA Ops:
  0.7 1.6 copy-start.2
  2.3 1.6 copy-start.4
  3.9 1.2 copy-start.6
  5.1 1.2 copy-start.8
  11.4 10.4 %collective-permute-start = (bf16[2,32,32,128]{3,2,1,0:T(8,128)(2,1)S(1)}, bf16[2,32,32,128]{3,2,1,0:T(8,128)(2,1)S(1)}, u32[]{:S(2)}, u32[]{:S(2)}) collective-permute-start(bf16[2,32,32,128]{3,2,1,0:T(8,128)(2,1)S(1)} %get-tuple-element.41), channel_id=1, source_target_pairs={{0,1},{1,0},{2,3},{3,2},{4,5},{5,4},{6,7},{7,6},{8,9},{9,8},{10,11... | collective-permute-start | bytes 1572872 | tf_op jit(solution)/shard_map/ppermute | solution.py:231
  11.9 15.3 %collective-permute-start.1 = (bf16[2,32,32,128]{3,2,1,0:T(8,128)(2,1)S(1)}, bf16[2,32,32,128]{3,2,1,0:T(8,128)(2,1)S(1)}, u32[]{:S(2)}, u32[]{:S(2)}) collective-permute-start(bf16[2,32,32,128]{3,2,1,0:T(8,128)(2,1)S(1)} %get-tuple-element.42), channel_id=1, source_target_pairs={{0,2},{1,3},{2,0},{3,1},{4,6},{5,7},{6,4},{7,5},{8,10},{9,11},{10,... | collective-permute-start | bytes 1572872 | tf_op jit(solution)/shard_map/ppermute | solution.py:231
  14.5 23.5 %copy-start = (bf16[2,32,128,128]{3,2,1,0:T(8,128)(2,1)S(1)}, bf16[2,32,128,128]{3,2,1,0:T(8,128)(2,1)}, u32[]{:S(2)}) copy-start(bf16[2,32,128,128]{3,2,1,0:T(8,128)(2,1)} %ul_ref.3) | copy-start | bytes 6291460
  14.5 23.5 %copy-start.1 = (bf16[2,32,128,128]{3,2,1,0:T(8,128)(2,1)S(1)}, bf16[2,32,128,128]{3,2,1,0:T(8,128)(2,1)}, u32[]{:S(2)}) copy-start(bf16[2,32,128,128]{3,2,1,0:T(8,128)(2,1)} %df_ref.3) | copy-start | bytes 6291460
  14.5 23.5 %collective-permute-start.2 = (bf16[2,32,32,128]{3,2,1,0:T(8,128)(2,1)S(1)}, bf16[2,32,32,128]{3,2,1,0:T(8,128)(2,1)S(1)}, u32[]{:S(2)}, u32[]{:S(2)}) collective-permute-start(bf16[2,32,32,128]{3,2,1,0:T(8,128)(2,1)S(1)} %get-tuple-element.43), channel_id=1, source_target_pairs={{0,3},{1,2},{2,1},{3,0},{4,7},{5,6},{6,5},{7,4},{8,11},{9,10},{10,... | collective-permute-start | bytes 1572872 | tf_op jit(solution)/shard_map/ppermute | solution.py:231
  19.6 31.8 %collective-permute-start.6 = (bf16[2,32,32,128]{3,2,1,0:T(8,128)(2,1)S(1)}, bf16[2,32,32,128]{3,2,1,0:T(8,128)(2,1)S(1)}, u32[]{:S(2)}, u32[]{:S(2)}) collective-permute-start(bf16[2,32,32,128]{3,2,1,0:T(8,128)(2,1)S(1)} %get-tuple-element.49), channel_id=1, source_target_pairs={{0,1},{1,0},{2,3},{3,2},{4,5},{5,4},{6,7},{7,6},{8,9},{9,8},{10,11... | collective-permute-start | bytes 1572872 | tf_op jit(solution)/shard_map/ppermute | solution.py:231
  19.9 31.6 %collective-permute-start.7 = (bf16[2,32,32,128]{3,2,1,0:T(8,128)(2,1)S(1)}, bf16[2,32,32,128]{3,2,1,0:T(8,128)(2,1)S(1)}, u32[]{:S(2)}, u32[]{:S(2)}) collective-permute-start(bf16[2,32,32,128]{3,2,1,0:T(8,128)(2,1)S(1)} %get-tuple-element.50), channel_id=1, source_target_pairs={{0,2},{1,3},{2,0},{3,1},{4,6},{5,7},{6,4},{7,5},{8,10},{9,11},{10,... | collective-permute-start | bytes 1572872 | tf_op jit(solution)/shard_map/ppermute | solution.py:231
  21.8 38.7 %collective-permute-start.8 = (bf16[2,32,32,128]{3,2,1,0:T(8,128)(2,1)S(1)}, bf16[2,32,32,128]{3,2,1,0:T(8,128)(2,1)S(1)}, u32[]{:S(2)}, u32[]{:S(2)}) collective-permute-start(bf16[2,32,32,128]{3,2,1,0:T(8,128)(2,1)S(1)} %get-tuple-element.51), channel_id=1, source_target_pairs={{0,3},{1,2},{2,1},{3,0},{4,7},{5,6},{6,5},{7,4},{8,11},{9,10},{10,... | collective-permute-start | bytes 1572872 | tf_op jit(solution)/shard_map/ppermute | solution.py:231
  49.0 28.0 %collective-permute-start.3 = (bf16[2,32,32,128]{3,2,1,0:T(8,128)(2,1)S(1)}, bf16[2,32,32,128]{3,2,1,0:T(8,128)(2,1)S(1)}, u32[]{:S(2)}, u32[]{:S(2)}) collective-permute-start(bf16[2,32,32,128]{3,2,1,0:T(8,128)(2,1)S(1)} %get-tuple-element.45), channel_id=1, source_target_pairs={{0,1},{1,0},{2,3},{3,2},{4,5},{5,4},{6,7},{7,6},{8,9},{9,8},{10,11... | collective-permute-start | bytes 1572872 | tf_op jit(solution)/shard_map/ppermute | solution.py:231
  49.5 29.2 %collective-permute-start.4 = (bf16[2,32,32,128]{3,2,1,0:T(8,128)(2,1)S(1)}, bf16[2,32,32,128]{3,2,1,0:T(8,128)(2,1)S(1)}, u32[]{:S(2)}, u32[]{:S(2)}) collective-permute-start(bf16[2,32,32,128]{3,2,1,0:T(8,128)(2,1)S(1)} %get-tuple-element.46), channel_id=1, source_target_pairs={{0,2},{1,3},{2,0},{3,1},{4,6},{5,7},{6,4},{7,5},{8,10},{9,11},{10,... | collective-permute-start | bytes 1572872 | tf_op jit(solution)/shard_map/ppermute | solution.py:231
  51.4 31.5 %collective-permute-start.5 = (bf16[2,32,32,128]{3,2,1,0:T(8,128)(2,1)S(1)}, bf16[2,32,32,128]{3,2,1,0:T(8,128)(2,1)S(1)}, u32[]{:S(2)}, u32[]{:S(2)}) collective-permute-start(bf16[2,32,32,128]{3,2,1,0:T(8,128)(2,1)S(1)} %get-tuple-element.47), channel_id=1, source_target_pairs={{0,3},{1,2},{2,1},{3,0},{4,7},{5,6},{6,5},{7,4},{8,11},{9,10},{10,... | collective-permute-start | bytes 1572872 | tf_op jit(solution)/shard_map/ppermute | solution.py:231
  51.4 21.5 %collective-permute-start.18 = (bf16[4,32,16,128]{3,2,1,0:T(8,128)(2,1)S(1)}, bf16[4,32,16,128]{3,2,1,0:T(8,128)(2,1)S(1)}, u32[]{:S(2)}, u32[]{:S(2)}) collective-permute-start(bf16[4,32,16,128]{3,2,1,0:T(8,128)(2,1)S(1)} %get-tuple-element.63), channel_id=1, source_target_pairs={{0,8},{4,12},{8,0},{12,4},{16,24},{20,28},{24,16},{28,20},{1,9},{5... | collective-permute-start | bytes 1572872 | tf_op jit(solution)/shard_map/ppermute | solution.py:231
  60.5 14.7 %collective-permute-start.24 = (bf16[4,32,16,128]{3,2,1,0:T(8,128)(2,1)S(1)}, bf16[4,32,16,128]{3,2,1,0:T(8,128)(2,1)S(1)}, u32[]{:S(2)}, u32[]{:S(2)}) collective-permute-start(bf16[4,32,16,128]{3,2,1,0:T(8,128)(2,1)S(1)} %get-tuple-element.67), channel_id=1, source_target_pairs={{0,4},{4,0},{8,12},{12,8},{16,20},{20,16},{24,28},{28,24},{1,5},{5... | collective-permute-start | bytes 1572872 | tf_op jit(solution)/shard_map/ppermute | solution.py:231
  72.9 11.6 %copy-start.7 = (bf16[128,4096]{1,0:T(8,128)(2,1)S(1)}, bf16[128,4096]{1,0:T(8,128)(2,1)}, u32[]{:S(2)}) copy-start(bf16[128,4096]{1,0:T(8,128)(2,1)} %x_ref.7) | copy-start | bytes 3145732
  72.9 18.0 %collective-permute-start.9 = (bf16[2,32,32,128]{3,2,1,0:T(8,128)(2,1)S(1)}, bf16[2,32,32,128]{3,2,1,0:T(8,128)(2,1)S(1)}, u32[]{:S(2)}, u32[]{:S(2)}) collective-permute-start(bf16[2,32,32,128]{3,2,1,0:T(8,128)(2,1)S(1)} %get-tuple-element.53), channel_id=1, source_target_pairs={{0,1},{1,0},{2,3},{3,2},{4,5},{5,4},{6,7},{7,6},{8,9},{9,8},{10,11... | collective-permute-start | bytes 1572872 | tf_op jit(solution)/shard_map/ppermute | solution.py:231
  75.2 14.0 %collective-permute-start.21 = (bf16[4,32,16,128]{3,2,1,0:T(8,128)(2,1)S(1)}, bf16[4,32,16,128]{3,2,1,0:T(8,128)(2,1)S(1)}, u32[]{:S(2)}, u32[]{:S(2)}) collective-permute-start(bf16[4,32,16,128]{3,2,1,0:T(8,128)(2,1)S(1)} %get-tuple-element.65), channel_id=1, source_target_pairs={{0,8},{4,12},{8,0},{12,4},{16,24},{20,28},{24,16},{28,20},{1,9},{5... | collective-permute-start | bytes 1572872 | tf_op jit(solution)/shard_map/ppermute | solution.py:231
  77.0 17.6 %collective-permute-start.10 = (bf16[2,32,32,128]{3,2,1,0:T(8,128)(2,1)S(1)}, bf16[2,32,32,128]{3,2,1,0:T(8,128)(2,1)S(1)}, u32[]{:S(2)}, u32[]{:S(2)}) collective-permute-start(bf16[2,32,32,128]{3,2,1,0:T(8,128)(2,1)S(1)} %get-tuple-element.54), channel_id=1, source_target_pairs={{0,2},{1,3},{2,0},{3,1},{4,6},{5,7},{6,4},{7,5},{8,10},{9,11},{10,... | collective-permute-start | bytes 1572872 | tf_op jit(solution)/shard_map/ppermute | solution.py:231
  78.6 26.8 %collective-permute-start.11 = (bf16[2,32,32,128]{3,2,1,0:T(8,128)(2,1)S(1)}, bf16[2,32,32,128]{3,2,1,0:T(8,128)(2,1)S(1)}, u32[]{:S(2)}, u32[]{:S(2)}) collective-permute-start(bf16[2,32,32,128]{3,2,1,0:T(8,128)(2,1)S(1)} %get-tuple-element.55), channel_id=1, source_target_pairs={{0,3},{1,2},{2,1},{3,0},{4,7},{5,6},{6,5},{7,4},{8,11},{9,10},{10,... | collective-permute-start | bytes 1572872 | tf_op jit(solution)/shard_map/ppermute | solution.py:231
  82.9 30.0 %collective-permute-start.27 = (bf16[4,32,16,128]{3,2,1,0:T(8,128)(2,1)S(1)}, bf16[4,32,16,128]{3,2,1,0:T(8,128)(2,1)S(1)}, u32[]{:S(2)}, u32[]{:S(2)}) collective-permute-start(bf16[4,32,16,128]{3,2,1,0:T(8,128)(2,1)S(1)} %get-tuple-element.69), channel_id=1, source_target_pairs={{0,4},{4,0},{8,12},{12,8},{16,20},{20,16},{24,28},{28,24},{1,5},{5... | collective-permute-start | bytes 1572872 | tf_op jit(solution)/shard_map/ppermute | solution.py:231
  89.1 25.6 %collective-permute-start.19 = (bf16[2,32,16,128]{3,2,1,0:T(8,128)(2,1)S(1)}, bf16[2,32,16,128]{3,2,1,0:T(8,128)(2,1)S(1)}, u32[]{:S(2)}, u32[]{:S(2)}) collective-permute-start(bf16[2,32,16,128]{3,2,1,0:T(8,128)(2,1)S(1)} %slice_bitcast_fusion.10), channel_id=1, source_target_pairs={{0,4},{4,0},{8,12},{12,8},{16,20},{20,16},{24,28},{28,24},{1,5},{5... | collective-permute-start | bytes 786440 | tf_op jit(solution)/shard_map/ppermute | solution.py:231
  91.0 24.4 %collective-permute-start.25 = (bf16[2,32,16,128]{3,2,1,0:T(8,128)(2,1)S(1)}, bf16[2,32,16,128]{3,2,1,0:T(8,128)(2,1)S(1)}, u32[]{:S(2)}, u32[]{:S(2)}) collective-permute-start(bf16[2,32,16,128]{3,2,1,0:T(8,128)(2,1)S(1)} %slice_bitcast_fusion.6), channel_id=1, source_target_pairs={{0,8},{4,12},{8,0},{12,4},{16,24},{20,28},{24,16},{28,20},{1,9},{5... | collective-permute-start | bytes 786440 | tf_op jit(solution)/shard_map/ppermute | solution.py:231
  94.7 71.4 %collective-permute-start.12 = (bf16[4,32,16,128]{3,2,1,0:T(8,128)(2,1)S(1)}, bf16[4,32,16,128]{3,2,1,0:T(8,128)(2,1)S(1)}, u32[]{:S(2)}, u32[]{:S(2)}) collective-permute-start(bf16[4,32,16,128]{3,2,1,0:T(8,128)(2,1)S(1)} %get-tuple-element.59), channel_id=1, source_target_pairs={{0,8},{4,12},{8,0},{12,4},{16,24},{20,28},{24,16},{28,20},{1,9},{5... | collective-permute-start | bytes 1572872 | tf_op jit(solution)/shard_map/ppermute | solution.py:231
  105.4 60.9 %collective-permute-start.30 = (bf16[4,32,16,128]{3,2,1,0:T(8,128)(2,1)S(1)}, bf16[4,32,16,128]{3,2,1,0:T(8,128)(2,1)S(1)}, u32[]{:S(2)}, u32[]{:S(2)}) collective-permute-start(bf16[4,32,16,128]{3,2,1,0:T(8,128)(2,1)S(1)} %get-tuple-element.71), channel_id=1, source_target_pairs={{0,4},{4,0},{8,12},{12,8},{16,20},{20,16},{24,28},{28,24},{1,5},{5... | collective-permute-start | bytes 1572872 | tf_op jit(solution)/shard_map/ppermute | solution.py:231
  107.0 1.8 copy-start.3
  107.0 2.2 %copy-start.5 = (bf16[2,32,128,128]{3,2,1,0:T(8,128)(2,1)S(1)}, bf16[2,32,128,128]{3,2,1,0:T(8,128)(2,1)}, u32[]{:S(2)}) copy-start(bf16[2,32,128,128]{3,2,1,0:T(8,128)(2,1)} %ur_ref.5) | copy-start | bytes 6291460
  112.9 53.7 %collective-permute-start.15 = (bf16[4,32,16,128]{3,2,1,0:T(8,128)(2,1)S(1)}, bf16[4,32,16,128]{3,2,1,0:T(8,128)(2,1)S(1)}, u32[]{:S(2)}, u32[]{:S(2)}) collective-permute-start(bf16[4,32,16,128]{3,2,1,0:T(8,128)(2,1)S(1)} %get-tuple-element.61), channel_id=1, source_target_pairs={{0,8},{4,12},{8,0},{12,4},{16,24},{20,28},{24,16},{28,20},{1,9},{5... | collective-permute-start | bytes 1572872 | tf_op jit(solution)/shard_map/ppermute | solution.py:231
  114.7 11.1 %collective-permute-start.22 = (bf16[2,32,16,128]{3,2,1,0:T(8,128)(2,1)S(1)}, bf16[2,32,16,128]{3,2,1,0:T(8,128)(2,1)S(1)}, u32[]{:S(2)}, u32[]{:S(2)}) collective-permute-start(bf16[2,32,16,128]{3,2,1,0:T(8,128)(2,1)S(1)} %slice_bitcast_fusion.8), channel_id=1, source_target_pairs={{0,4},{4,0},{8,12},{12,8},{16,20},{20,16},{24,28},{28,24},{1,5},{5... | collective-permute-start | bytes 786440 | tf_op jit(solution)/shard_map/ppermute | solution.py:231
  115.4 53.5 %collective-permute-start.33 = (bf16[4,32,16,128]{3,2,1,0:T(8,128)(2,1)S(1)}, bf16[4,32,16,128]{3,2,1,0:T(8,128)(2,1)S(1)}, u32[]{:S(2)}, u32[]{:S(2)}) collective-permute-start(bf16[4,32,16,128]{3,2,1,0:T(8,128)(2,1)S(1)} %get-tuple-element.73), channel_id=1, source_target_pairs={{0,4},{4,0},{8,12},{12,8},{16,20},{20,16},{24,28},{28,24},{1,5},{5... | collective-permute-start | bytes 1572872 | tf_op jit(solution)/shard_map/ppermute | solution.py:231
  125.8 7.6 %collective-permute-start.28 = (bf16[2,32,16,128]{3,2,1,0:T(8,128)(2,1)S(1)}, bf16[2,32,16,128]{3,2,1,0:T(8,128)(2,1)S(1)}, u32[]{:S(2)}, u32[]{:S(2)}) collective-permute-start(bf16[2,32,16,128]{3,2,1,0:T(8,128)(2,1)S(1)} %slice_bitcast_fusion.4), channel_id=1, source_target_pairs={{0,8},{4,12},{8,0},{12,4},{16,24},{20,28},{24,16},{28,20},{1,9},{5... | collective-permute-start | bytes 786440 | tf_op jit(solution)/shard_map/ppermute | solution.py:231
  133.3 7.8 %collective-permute-start.20 = (bf16[1,32,16,128]{3,2,1,0:T(8,128)(2,1)S(1)}, bf16[1,32,16,128]{3,2,1,0:T(8,128)(2,1)S(1)}, u32[]{:S(2)}, u32[]{:S(2)}) collective-permute-start(bf16[1,32,16,128]{3,2,1,0:T(8,128)(2,1)S(1)} %slice_bitcast_fusion.26), channel_id=1, source_target_pairs={{0,16},{4,20},{8,24},{12,28},{16,0},{20,4},{24,8},{28,12},{1,17},{... | collective-permute-start | bytes 393224 | tf_op jit(solution)/shard_map/ppermute | solution.py:231
  141.1 8.0 %collective-permute-start.26 = (bf16[1,32,16,128]{3,2,1,0:T(8,128)(2,1)S(1)}, bf16[1,32,16,128]{3,2,1,0:T(8,128)(2,1)S(1)}, u32[]{:S(2)}, u32[]{:S(2)}) collective-permute-start(bf16[1,32,16,128]{3,2,1,0:T(8,128)(2,1)S(1)} %slice_bitcast_fusion.22), channel_id=1, source_target_pairs={{0,16},{4,20},{8,24},{12,28},{16,0},{20,4},{24,8},{28,12},{1,17},{... | collective-permute-start | bytes 393224 | tf_op jit(solution)/shard_map/ppermute | solution.py:231
  149.1 9.5 %collective-permute-start.23 = (bf16[1,32,16,128]{3,2,1,0:T(8,128)(2,1)S(1)}, bf16[1,32,16,128]{3,2,1,0:T(8,128)(2,1)S(1)}, u32[]{:S(2)}, u32[]{:S(2)}) collective-permute-start(bf16[1,32,16,128]{3,2,1,0:T(8,128)(2,1)S(1)} %slice_bitcast_fusion.24), channel_id=1, source_target_pairs={{0,16},{4,20},{8,24},{12,28},{16,0},{20,4},{24,8},{28,12},{1,17},{... | collective-permute-start | bytes 393224 | tf_op jit(solution)/shard_map/ppermute | solution.py:231
  158.7 6.5 %collective-permute-start.29 = (bf16[1,32,16,128]{3,2,1,0:T(8,128)(2,1)S(1)}, bf16[1,32,16,128]{3,2,1,0:T(8,128)(2,1)S(1)}, u32[]{:S(2)}, u32[]{:S(2)}) collective-permute-start(bf16[1,32,16,128]{3,2,1,0:T(8,128)(2,1)S(1)} %slice_bitcast_fusion.20), channel_id=1, source_target_pairs={{0,16},{4,20},{8,24},{12,28},{16,0},{20,4},{24,8},{28,12},{1,17},{... | collective-permute-start | bytes 393224 | tf_op jit(solution)/shard_map/ppermute | solution.py:231
  166.2 8.0 %collective-permute-start.13 = (bf16[2,32,16,128]{3,2,1,0:T(8,128)(2,1)S(1)}, bf16[2,32,16,128]{3,2,1,0:T(8,128)(2,1)S(1)}, u32[]{:S(2)}, u32[]{:S(2)}) collective-permute-start(bf16[2,32,16,128]{3,2,1,0:T(8,128)(2,1)S(1)} %slice_bitcast_fusion.14), channel_id=1, source_target_pairs={{0,4},{4,0},{8,12},{12,8},{16,20},{20,16},{24,28},{28,24},{1,5},{5... | collective-permute-start | bytes 786440 | tf_op jit(solution)/shard_map/ppermute | solution.py:231
  166.5 11.9 %collective-permute-start.31 = (bf16[2,32,16,128]{3,2,1,0:T(8,128)(2,1)S(1)}, bf16[2,32,16,128]{3,2,1,0:T(8,128)(2,1)S(1)}, u32[]{:S(2)}, u32[]{:S(2)}) collective-permute-start(bf16[2,32,16,128]{3,2,1,0:T(8,128)(2,1)S(1)} %slice_bitcast_fusion.2), channel_id=1, source_target_pairs={{0,8},{4,12},{8,0},{12,4},{16,24},{20,28},{24,16},{28,20},{1,9},{5... | collective-permute-start | bytes 786440 | tf_op jit(solution)/shard_map/ppermute | solution.py:231
  166.8 11.8 %collective-permute-start.16 = (bf16[2,32,16,128]{3,2,1,0:T(8,128)(2,1)S(1)}, bf16[2,32,16,128]{3,2,1,0:T(8,128)(2,1)S(1)}, u32[]{:S(2)}, u32[]{:S(2)}) collective-permute-start(bf16[2,32,16,128]{3,2,1,0:T(8,128)(2,1)S(1)} %slice_bitcast_fusion.12), channel_id=1, source_target_pairs={{0,4},{4,0},{8,12},{12,8},{16,20},{20,16},{24,28},{28,24},{1,5},{5... | collective-permute-start | bytes 786440 | tf_op jit(solution)/shard_map/ppermute | solution.py:231
  169.0 14.9 %collective-permute-start.34 = (bf16[2,32,16,128]{3,2,1,0:T(8,128)(2,1)S(1)}, bf16[2,32,16,128]{3,2,1,0:T(8,128)(2,1)S(1)}, u32[]{:S(2)}, u32[]{:S(2)}) collective-permute-start(bf16[2,32,16,128]{3,2,1,0:T(8,128)(2,1)S(1)} %slice_bitcast_fusion), channel_id=1, source_target_pairs={{0,8},{4,12},{8,0},{12,4},{16,24},{20,28},{24,16},{28,20},{1,9},{5... | collective-permute-start | bytes 786440 | tf_op jit(solution)/shard_map/ppermute | solution.py:231
  174.3 18.5 %collective-permute-start.14 = (bf16[1,32,16,128]{3,2,1,0:T(8,128)(2,1)S(1)}, bf16[1,32,16,128]{3,2,1,0:T(8,128)(2,1)S(1)}, u32[]{:S(2)}, u32[]{:S(2)}) collective-permute-start(bf16[1,32,16,128]{3,2,1,0:T(8,128)(2,1)S(1)} %slice_bitcast_fusion.30), channel_id=1, source_target_pairs={{0,16},{4,20},{8,24},{12,28},{16,0},{20,4},{24,8},{28,12},{1,17},{... | collective-permute-start | bytes 393224 | tf_op jit(solution)/shard_map/ppermute | solution.py:231
  178.5 16.9 %collective-permute-start.32 = (bf16[1,32,16,128]{3,2,1,0:T(8,128)(2,1)S(1)}, bf16[1,32,16,128]{3,2,1,0:T(8,128)(2,1)S(1)}, u32[]{:S(2)}, u32[]{:S(2)}) collective-permute-start(bf16[1,32,16,128]{3,2,1,0:T(8,128)(2,1)S(1)} %slice_bitcast_fusion.18), channel_id=1, source_target_pairs={{0,16},{4,20},{8,24},{12,28},{16,0},{20,4},{24,8},{28,12},{1,17},{... | collective-permute-start | bytes 393224 | tf_op jit(solution)/shard_map/ppermute | solution.py:231
  178.7 18.1 %collective-permute-start.17 = (bf16[1,32,16,128]{3,2,1,0:T(8,128)(2,1)S(1)}, bf16[1,32,16,128]{3,2,1,0:T(8,128)(2,1)S(1)}, u32[]{:S(2)}, u32[]{:S(2)}) collective-permute-start(bf16[1,32,16,128]{3,2,1,0:T(8,128)(2,1)S(1)} %slice_bitcast_fusion.28), channel_id=1, source_target_pairs={{0,16},{4,20},{8,24},{12,28},{16,0},{20,4},{24,8},{28,12},{1,17},{... | collective-permute-start | bytes 393224 | tf_op jit(solution)/shard_map/ppermute | solution.py:231
  184.0 14.2 %collective-permute-start.35 = (bf16[1,32,16,128]{3,2,1,0:T(8,128)(2,1)S(1)}, bf16[1,32,16,128]{3,2,1,0:T(8,128)(2,1)S(1)}, u32[]{:S(2)}, u32[]{:S(2)}) collective-permute-start(bf16[1,32,16,128]{3,2,1,0:T(8,128)(2,1)S(1)} %slice_bitcast_fusion.16), channel_id=1, source_target_pairs={{0,16},{4,20},{8,24},{12,28},{16,0},{20,4},{24,8},{28,12},{1,17},{... | collective-permute-start | bytes 393224 | tf_op jit(solution)/shard_map/ppermute | solution.py:231

commit v3 on v2

--- a/solution.py
+++ b/solution.py
@@ -235,21 +235,23 @@
     return [p if k == 0 else xor_permute(p, "mp", k) for k, p in enumerate(parts)]
 
 
-def halving_sums(halves, scale):
+def halving_rounds(reductions, scale):
     ways = lax.axis_size("dp")
-    pairs = [[halves[0], halves[1]], [halves[2], halves[3]]]
     orders = [hop_order(ways, kind) for kind in range(2)]
-    sums = [None, None]
-    for hop in range(len(orders[0])):
-        for kind in range(2):
-            keep, send = pairs[kind]
-            got = xor_permute(send, "dp", orders[kind][hop])
-            total = keep.astype(F32) + got.astype(F32)
+    hops = len(orders[0])
+    pairs = [[[h[0], h[1]], [h[2], h[3]]] for h in reductions]
+    sums = [[None, None] for _ in reductions]
+    for turn in range(hops + len(reductions) - 1):
+        active = [(s, kind) for s in range(len(reductions)) if 0 <= turn - s < hops for kind in range(2)]
+        got = [xor_permute(pairs[s][kind][1], "dp", orders[kind][turn - s]) for s, kind in active]
+        got = lax.optimization_barrier(got)
+        for (s, kind), arrived in zip(active, got):
+            total = pairs[s][kind][0].astype(F32) + arrived.astype(F32)
             if total.shape[0] == 1:
-                sums[kind] = total[0] * scale
+                sums[s][kind] = total[0] * scale
                 continue
             total = total.astype(BF16).reshape((total.shape[0] // 2, 2) + total.shape[1:])
-            pairs[kind] = [total[:, 0], total[:, 1]]
+            pairs[s][kind] = [total[:, 0], total[:, 1]]
     return sums
 
 
@@ -258,16 +260,17 @@
     mp_ways, dp_ways = lax.axis_size("mp"), lax.axis_size("dp")
     scale = (dp_ways * tokens.shape[0]) ** (-0.5)
     me = jnp.stack([lax.axis_index("mp"), lax.axis_index("dp")]).astype(jnp.int32)
-    firsts, seconds, mid_sums, last_sums = [], [], [], []
+    firsts, seconds, reductions = [], [], []
     for q in range(groups):
         firsts.append(exchange(make_panels(me, tokens, cotangent, up_right, down_left, q, mp_ways)))
     for q in range(groups):
         panels, halves = make_middle(me, firsts[q], up_left, down_first_factor, q, dp_ways)
         seconds.append(exchange(panels))
-        mid_sums.append(halving_sums(halves, scale))
+        reductions.append(halves)
     for q in range(groups):
-        halves = make_last_grads(me, seconds[q], tokens, cotangent, width, dp_ways)
-        last_sums.append(halving_sums(halves, scale))
+        reductions.append(make_last_grads(me, seconds[q], tokens, cotangent, width, dp_ways))
+    sums = halving_rounds(reductions, scale)
+    mid_sums, last_sums = sums[:groups], sums[groups:]
     mixed, tokens_grad = make_outputs(me, seconds, down_left, up_right)
 
     def pick(sums, kind):

time: 199 us -> 189 us (0.950)
  waiting for transfers between devices: 107 us -> 87.6 us
  starting transfers between devices: 40 us -> 49.7 us
    ppermute x36, waiting for transfers between devices: 107 us -> 87.6 us  [xor_permute(): lax.ppermute(array, axis, [(i, i ^ k) for i in range(lax.axis_size(axis))])]
    ppermute x36, starting transfers between devices: 40 us -> 49.7 us  [xor_permute(): lax.ppermute(array, axis, [(i, i ^ k) for i in range(lax.axis_size(axis))])]
  transfers between devices with their start and end apart: 36 -> 36, of which waited for: 21 -> 18; matrix products, arithmetic and copies ran while one was open for 2% -> 2% of each run, Pallas kernels for 17% -> 18%
where the time goes in v3:
time: 189 us
  waiting for transfers between devices  87.6 us (46%)
  starting transfers between devices  49.7 us (26%)
  Pallas kernels  39.3 us (21%)
  local copies, waits for them, and re-layouts  5.88 us (3%)
  other arithmetic  5.38 us (3%)
    ppermute x36, waiting for transfers between devices, xor_permute(): lax.ppermute(array, axis, [(i, i ^ k) for i in range(lax.axis_size(axis))])  87.6 us
    ppermute x36, starting transfers between devices, xor_permute(): lax.ppermute(array, axis, [(i, i ^ k) for i in range(lax.axis_size(axis))])  49.7 us
    pallas_call x2, Pallas kernels, make_middle(): pl.pallas_call(functools.partial(middle_kernel, n, dp_ways), out_shape=[p...  21.9 us
    pallas_call x2, Pallas kernels, make_panels(): pl.pallas_call(functools.partial(panels_kernel, ways), out_shape=[part] *...  10.1 us
    unnamed x18, local copies, waits for them, and re-layouts  5.65 us
  transfers between devices with their start and end apart: 36, of which 18 were waited for; matrix products, arithmetic and copies ran while one was open for 2% of the time, Pallas kernels for 18%

profile of v3, /device:TPU:0, one launch (start us, length us, event | category | flops | bytes accessed | tf_op | source)
XLA Modules:
  0.0 188.9 jit_solution(1156659824346057818)
XLA Ops:
  0.7 1.6 copy-done.2
  2.3 1.6 copy-done.4
  3.9 1.2 copy-done.6
  5.1 1.2 copy-done.8
  6.3 5.1 %shard_map.109 = (bf16[2,32,32,128]{3,2,1,0:T(8,128)(2,1)S(1)}, bf16[2,32,32,128]{3,2,1,0:T(8,128)(2,1)S(1)}, bf16[2,32,32,128]{3,2,1,0:T(8,128)(2,1)S(1)}, bf16[2,32,32,128]{3,2,1,0:T(8,128)(2,1)S(1)}) custom-call(s32[2]{0:T(128)S(1)} %pad_add_fusion.me_ref, bf16[128,4096]{1,0:T(8,128)(2,1)S(1)} %copy-done.6, bf16[128,4096]{1,0:T(8,128)(2,1)S(1)} %copy-done.8, ...), custom_call_target="tpu_custom_call" | custom-call | flops 2147483648 | bytes 8388608 | tf_op jit(solution)/shard_map/pallas_call | solution.py:81
  11.9 2.6 %collective-permute-start.1 = (bf16[2,32,32,128]{3,2,1,0:T(8,128)(2,1)S(1)}, bf16[2,32,32,128]{3,2,1,0:T(8,128)(2,1)S(1)}, u32[]{:S(2)}, u32[]{:S(2)}) collective-permute-start(bf16[2,32,32,128]{3,2,1,0:T(8,128)(2,1)S(1)} %get-tuple-element.66), channel_id=1, source_target_pairs={{0,2},{1,3},{2,0},{3,1},{4,6},{5,7},{6,4},{7,5},{8,10},{9,11},{10,... | collective-permute-start | bytes 1572872 | tf_op jit(solution)/shard_map/ppermute | solution.py:231
  14.6 5.1 %shard_map.111 = (bf16[2,32,32,128]{3,2,1,0:T(8,128)(2,1)S(1)}, bf16[2,32,32,128]{3,2,1,0:T(8,128)(2,1)S(1)}, bf16[2,32,32,128]{3,2,1,0:T(8,128)(2,1)S(1)}, bf16[2,32,32,128]{3,2,1,0:T(8,128)(2,1)S(1)}) custom-call(s32[2]{0:T(128)S(1)} %pad_add_fusion.me_ref, bf16[128,4096]{1,0:T(8,128)(2,1)S(1)} %copy-done.6, bf16[128,4096]{1,0:T(8,128)(2,1)S(1)} %copy-done.8, ...), custom_call_target="tpu_custom_call" | custom-call | flops 2147483648 | bytes 8388608 | tf_op jit(solution)/shard_map/pallas_call | solution.py:81
  19.9 1.9 %collective-permute-start.7 = (bf16[2,32,32,128]{3,2,1,0:T(8,128)(2,1)S(1)}, bf16[2,32,32,128]{3,2,1,0:T(8,128)(2,1)S(1)}, u32[]{:S(2)}, u32[]{:S(2)}) collective-permute-start(bf16[2,32,32,128]{3,2,1,0:T(8,128)(2,1)S(1)} %get-tuple-element.74), channel_id=1, source_target_pairs={{0,2},{1,3},{2,0},{3,1},{4,6},{5,7},{6,4},{7,5},{8,10},{9,11},{10,... | collective-permute-start | bytes 1572872 | tf_op jit(solution)/shard_map/ppermute | solution.py:231
  21.8 5.5 %collective-permute-done.1.rest_2_ = bf16[2,32,32,128]{3,2,1,0:T(8,128)(2,1)S(1)} collective-permute-done((bf16[2,32,32,128]{3,2,1,0:T(8,128)(2,1)S(1)}, bf16[2,32,32,128]{3,2,1,0:T(8,128)(2,1)S(1)}, u32[]{:S(2)}, u32[]{:S(2)}) %collective-permute-start.1) | collective-permute-done | bytes 524320 | tf_op jit(solution)/shard_map/ppermute | solution.py:231
  27.3 10.7 %collective-permute-done.2.rest_3_ = bf16[2,32,32,128]{3,2,1,0:T(8,128)(2,1)S(1)} collective-permute-done((bf16[2,32,32,128]{3,2,1,0:T(8,128)(2,1)S(1)}, bf16[2,32,32,128]{3,2,1,0:T(8,128)(2,1)S(1)}, u32[]{:S(2)}, u32[]{:S(2)}) %collective-permute-start.2) | collective-permute-done | bytes 524320 | tf_op jit(solution)/shard_map/ppermute | solution.py:231
  38.0 11.0 %shard_map.110 = (bf16[2,32,32,128]{3,2,1,0:T(8,128)(2,1)S(1)}, bf16[2,32,32,128]{3,2,1,0:T(8,128)(2,1)S(1)}, bf16[2,32,32,128]{3,2,1,0:T(8,128)(2,1)S(1)}, bf16...) custom-call(s32[2]{0:T(128)S(1)} %pad_add_fusion.me_ref, ...), custom_call_target="tpu_custom_call" | custom-call | flops 6442450944 | bytes 8388608 | tf_op jit(solution)/shard_map/pallas_call | solution.py:143
  49.5 2.0 %collective-permute-start.4 = (bf16[2,32,32,128]{3,2,1,0:T(8,128)(2,1)S(1)}, bf16[2,32,32,128]{3,2,1,0:T(8,128)(2,1)S(1)}, u32[]{:S(2)}, u32[]{:S(2)}) collective-permute-start(bf16[2,32,32,128]{3,2,1,0:T(8,128)(2,1)S(1)} %get-tuple-element.70), channel_id=1, source_target_pairs={{0,2},{1,3},{2,0},{3,1},{4,6},{5,7},{6,4},{7,5},{8,10},{9,11},{10,... | collective-permute-start | bytes 1572872 | tf_op jit(solution)/shard_map/ppermute | solution.py:231
  51.4 1.6 collective-permute-start.12
  53.0 7.5 %collective-permute-done.8.rest_3_ = bf16[2,32,32,128]{3,2,1,0:T(8,128)(2,1)S(1)} collective-permute-done((bf16[2,32,32,128]{3,2,1,0:T(8,128)(2,1)S(1)}, bf16[2,32,32,128]{3,2,1,0:T(8,128)(2,1)S(1)}, u32[]{:S(2)}, u32[]{:S(2)}) %collective-permute-start.8) | collective-permute-done | bytes 524320 | tf_op jit(solution)/shard_map/ppermute | solution.py:231
  60.5 1.6 collective-permute-start.13
  62.1 10.9 %shard_map.112 = (bf16[2,32,32,128]{3,2,1,0:T(8,128)(2,1)S(1)}, bf16[2,32,32,128]{3,2,1,0:T(8,128)(2,1)S(1)}, bf16[2,32,32,128]{3,2,1,0:T(8,128)(2,1)S(1)}, bf16...) custom-call(s32[2]{0:T(128)S(1)} %pad_add_fusion.me_ref, ...), custom_call_target="tpu_custom_call" | custom-call | flops 6442450944 | bytes 8388608 | tf_op jit(solution)/shard_map/pallas_call | solution.py:143
  73.8 1.4 collective-permute-done.13
  75.2 1.6 collective-permute-start.10
  77.2 1.6 collective-permute-start.16
  78.8 4.1 %collective-permute-done.5.rest_3_ = bf16[2,32,32,128]{3,2,1,0:T(8,128)(2,1)S(1)} collective-permute-done((bf16[2,32,32,128]{3,2,1,0:T(8,128)(2,1)S(1)}, bf16[2,32,32,128]{3,2,1,0:T(8,128)(2,1)S(1)}, u32[]{:S(2)}, u32[]{:S(2)}) %collective-permute-start.5) | collective-permute-done | bytes 524320 | tf_op jit(solution)/shard_map/ppermute | solution.py:231
  82.9 1.6 collective-permute-start.17
  84.6 1.8 shard_map.114
  86.9 7.8 %collective-permute-done.10.rest_6_.rest_2_ = bf16[2,32,32,128]{3,2,1,0:T(8,128)(2,1)S(1)} collective-permute-done((bf16[2,32,32,128]{3,2,1,0:T(8,128)(2,1)S(1)}, bf16[2,32,32,128]{3,2,1,0:T(8,128)(2,1)S(1)}, u32[]{:S(2)}, u32[]{:S(2)}) %collective-permute-start.10) | collective-permute-done | bytes 524320 | tf_op jit(solution)/shard_map/ppermute | solution.py:231
  94.7 2.0 %collective-permute-start.15 = (bf16[2,32,16,128]{3,2,1,0:T(8,128)(2,1)S(1)}, bf16[2,32,16,128]{3,2,1,0:T(8,128)(2,1)S(1)}, u32[]{:S(2)}, u32[]{:S(2)}) collective-permute-start(bf16[2,32,16,128]{3,2,1,0:T(8,128)(2,1)S(1)} %slice_bitcast_fusion.13), channel_id=1, source_target_pairs={{0,4},{4,0},{8,12},{12,8},{16,20},{20,16},{24,28},{28,24},{1,5},{5... | collective-permute-start | bytes 786440 | tf_op jit(solution)/shard_map/ppermute | solution.py:231
  96.7 8.7 %collective-permute-done.11.rest_7_.rest_3_ = bf16[2,32,32,128]{3,2,1,0:T(8,128)(2,1)S(1)} collective-permute-done((bf16[2,32,32,128]{3,2,1,0:T(8,128)(2,1)S(1)}, bf16[2,32,32,128]{3,2,1,0:T(8,128)(2,1)S(1)}, u32[]{:S(2)}, u32[]{:S(2)}) %collective-permute-start.11) | collective-permute-done | bytes 524320 | tf_op jit(solution)/shard_map/ppermute | solution.py:231
  105.4 1.6 collective-permute-start.22
  107.0 3.7 %shard_map.113 = (bf16[128,4096]{1,0:T(8,128)(2,1)}, bf16[128,4096]{1,0:T(8,128)(2,1)}) custom-call(s32[2]{0:T(128)S(1)} %pad_add_fusion.me_ref, bf16[2,32,128,128]{3,2,1,0:T(8,128)(2,1)S(1)} %copy-done.3, bf16[2,32,128,128]{3,2,1,0:T(8,128)(2,1)S(1)} %copy-done.5, bf16[2,32,32,128]{3,2,1,0:T(8,128)(2,1)S(1)} %get-tuple-element.68.rest_0_, ...), custom_call_target="tpu_custom_call" | custom-call | flops 4294967296 | bytes 10485760 | tf_op jit(solution)/shard_map/pallas_call | solution.py:217
  110.7 1.6 collective-permute-start.23
  112.4 2.7 %collective-permute-start.18 = (bf16[1,32,16,128]{3,2,1,0:T(8,128)(2,1)S(1)}, bf16[1,32,16,128]{3,2,1,0:T(8,128)(2,1)S(1)}, u32[]{:S(2)}, u32[]{:S(2)}) collective-permute-start(bf16[1,32,16,128]{3,2,1,0:T(8,128)(2,1)S(1)} %slice_bitcast_fusion.31), channel_id=1, source_target_pairs={{0,16},{4,20},{8,24},{12,28},{16,0},{20,4},{24,8},{28,12},{1,17},{... | collective-permute-start | bytes 393224 | tf_op jit(solution)/shard_map/ppermute | solution.py:231
  116.5 10.8 %collective-permute-done.18 = bf16[1,32,16,128]{3,2,1,0:T(8,128)(2,1)S(1)} collective-permute-done((bf16[1,32,16,128]{3,2,1,0:T(8,128)(2,1)S(1)}, bf16[1,32,16,128]{3,2,1,0:T(8,128)(2,1)S(1)}, u32[]{:S(2)}, u32[]{:S(2)}) %collective-permute-start.18) | collective-permute-done | bytes 131104 | tf_op jit(solution)/shard_map/ppermute | solution.py:231
  127.4 3.4 %collective-permute-start.19 = (bf16[1,32,16,128]{3,2,1,0:T(8,128)(2,1)S(1)}, bf16[1,32,16,128]{3,2,1,0:T(8,128)(2,1)S(1)}, u32[]{:S(2)}, u32[]{:S(2)}) collective-permute-start(bf16[1,32,16,128]{3,2,1,0:T(8,128)(2,1)S(1)} %slice_bitcast_fusion.30), channel_id=1, source_target_pairs={{0,16},{4,20},{8,24},{12,28},{16,0},{20,4},{24,8},{28,12},{1,17},{... | collective-permute-start | bytes 393224 | tf_op jit(solution)/shard_map/ppermute | solution.py:231
  130.8 1.8 shard_map.115
  132.6 2.3 %collective-permute-done.19 = bf16[1,32,16,128]{3,2,1,0:T(8,128)(2,1)S(1)} collective-permute-done((bf16[1,32,16,128]{3,2,1,0:T(8,128)(2,1)S(1)}, bf16[1,32,16,128]{3,2,1,0:T(8,128)(2,1)S(1)}, u32[]{:S(2)}, u32[]{:S(2)}) %collective-permute-start.19) | collective-permute-done | bytes 131104 | tf_op jit(solution)/shard_map/ppermute | solution.py:231
  135.4 3.5 %collective-permute-start.29 = (bf16[4,32,16,128]{3,2,1,0:T(8,128)(2,1)S(1)}, bf16[4,32,16,128]{3,2,1,0:T(8,128)(2,1)S(1)}, u32[]{:S(2)}, u32[]{:S(2)}) collective-permute-start(bf16[4,32,16,128]{3,2,1,0:T(8,128)(2,1)S(1)} %get-tuple-element.105), channel_id=1, source_target_pairs={{0,8},{4,12},{8,0},{12,4},{16,24},{20,28},{24,16},{28,20},{1,9},{5... | collective-permute-start | bytes 1572872 | tf_op jit(solution)/shard_map/ppermute | solution.py:231
  139.3 2.0 %collective-permute-start.26 = (bf16[2,32,16,128]{3,2,1,0:T(8,128)(2,1)S(1)}, bf16[2,32,16,128]{3,2,1,0:T(8,128)(2,1)S(1)}, u32[]{:S(2)}, u32[]{:S(2)}) collective-permute-start(bf16[2,32,16,128]{3,2,1,0:T(8,128)(2,1)S(1)} %slice_bitcast_fusion.6), channel_id=1, source_target_pairs={{0,8},{4,12},{8,0},{12,4},{16,24},{20,28},{24,16},{28,20},{1,9},{5... | collective-permute-start | bytes 786440 | tf_op jit(solution)/shard_map/ppermute | solution.py:231
  141.4 1.6 collective-permute-start.27
  143.0 6.7 %collective-permute-done.28 = bf16[4,32,16,128]{3,2,1,0:T(8,128)(2,1)S(1)} collective-permute-done((bf16[4,32,16,128]{3,2,1,0:T(8,128)(2,1)S(1)}, bf16[4,32,16,128]{3,2,1,0:T(8,128)(2,1)S(1)}, u32[]{:S(2)}, u32[]{:S(2)}) %collective-permute-start.28) | collective-permute-done | bytes 524320 | tf_op jit(solution)/shard_map/ppermute | solution.py:231
  149.7 3.4 %collective-permute-start.25 = (bf16[1,32,16,128]{3,2,1,0:T(8,128)(2,1)S(1)}, bf16[1,32,16,128]{3,2,1,0:T(8,128)(2,1)S(1)}, u32[]{:S(2)}, u32[]{:S(2)}) collective-permute-start(bf16[1,32,16,128]{3,2,1,0:T(8,128)(2,1)S(1)} %slice_bitcast_fusion.28), channel_id=1, source_target_pairs={{0,16},{4,20},{8,24},{12,28},{16,0},{20,4},{24,8},{28,12},{1,17},{... | collective-permute-start | bytes 393224 | tf_op jit(solution)/shard_map/ppermute | solution.py:231
  153.2 4.1 %collective-permute-done.29 = bf16[4,32,16,128]{3,2,1,0:T(8,128)(2,1)S(1)} collective-permute-done((bf16[4,32,16,128]{3,2,1,0:T(8,128)(2,1)S(1)}, bf16[4,32,16,128]{3,2,1,0:T(8,128)(2,1)S(1)}, u32[]{:S(2)}, u32[]{:S(2)}) %collective-permute-start.29) | collective-permute-done | bytes 524320 | tf_op jit(solution)/shard_map/ppermute | solution.py:231
  157.3 3.0 %collective-permute-done.25 = bf16[1,32,16,128]{3,2,1,0:T(8,128)(2,1)S(1)} collective-permute-done((bf16[1,32,16,128]{3,2,1,0:T(8,128)(2,1)S(1)}, bf16[1,32,16,128]{3,2,1,0:T(8,128)(2,1)S(1)}, u32[]{:S(2)}, u32[]{:S(2)}) %collective-permute-start.25) | collective-permute-done | bytes 131104 | tf_op jit(solution)/shard_map/ppermute | solution.py:231
  161.2 2.7 %collective-permute-start.30 = (bf16[1,32,16,128]{3,2,1,0:T(8,128)(2,1)S(1)}, bf16[1,32,16,128]{3,2,1,0:T(8,128)(2,1)S(1)}, u32[]{:S(2)}, u32[]{:S(2)}) collective-permute-start(bf16[1,32,16,128]{3,2,1,0:T(8,128)(2,1)S(1)} %slice_bitcast_fusion.26), channel_id=1, source_target_pairs={{0,16},{4,20},{8,24},{12,28},{16,0},{20,4},{24,8},{28,12},{1,17},{... | collective-permute-start | bytes 393224 | tf_op jit(solution)/shard_map/ppermute | solution.py:231
  164.5 1.7 collective-permute-start.32
  166.4 1.6 collective-permute-start.33
  169.7 2.4 %collective-permute-done.30 = bf16[1,32,16,128]{3,2,1,0:T(8,128)(2,1)S(1)} collective-permute-done((bf16[1,32,16,128]{3,2,1,0:T(8,128)(2,1)S(1)}, bf16[1,32,16,128]{3,2,1,0:T(8,128)(2,1)S(1)}, u32[]{:S(2)}, u32[]{:S(2)}) %collective-permute-start.30) | collective-permute-done | bytes 131104 | tf_op jit(solution)/shard_map/ppermute | solution.py:231
  172.1 2.2 %collective-permute-done.31 = bf16[1,32,16,128]{3,2,1,0:T(8,128)(2,1)S(1)} collective-permute-done((bf16[1,32,16,128]{3,2,1,0:T(8,128)(2,1)S(1)}, bf16[1,32,16,128]{3,2,1,0:T(8,128)(2,1)S(1)}, u32[]{:S(2)}, u32[]{:S(2)}) %collective-permute-start.31) | collective-permute-done | bytes 131104 | tf_op jit(solution)/shard_map/ppermute | solution.py:231
  175.7 3.0 %collective-permute-start.35 = (bf16[1,32,16,128]{3,2,1,0:T(8,128)(2,1)S(1)}, bf16[1,32,16,128]{3,2,1,0:T(8,128)(2,1)S(1)}, u32[]{:S(2)}, u32[]{:S(2)}) collective-permute-start(bf16[1,32,16,128]{3,2,1,0:T(8,128)(2,1)S(1)} %slice_bitcast_fusion.22), channel_id=1, source_target_pairs={{0,16},{4,20},{8,24},{12,28},{16,0},{20,4},{24,8},{28,12},{1,17},{... | collective-permute-start | bytes 393224 | tf_op jit(solution)/shard_map/ppermute | solution.py:231
  178.8 6.4 %collective-permute-done.34 = bf16[1,32,16,128]{3,2,1,0:T(8,128)(2,1)S(1)} collective-permute-done((bf16[1,32,16,128]{3,2,1,0:T(8,128)(2,1)S(1)}, bf16[1,32,16,128]{3,2,1,0:T(8,128)(2,1)S(1)}, u32[]{:S(2)}, u32[]{:S(2)}) %collective-permute-start.34) | collective-permute-done | bytes 131104 | tf_op jit(solution)/shard_map/ppermute | solution.py:231
  185.2 2.0 %collective-permute-done.35 = bf16[1,32,16,128]{3,2,1,0:T(8,128)(2,1)S(1)} collective-permute-done((bf16[1,32,16,128]{3,2,1,0:T(8,128)(2,1)S(1)}, bf16[1,32,16,128]{3,2,1,0:T(8,128)(2,1)S(1)}, u32[]{:S(2)}, u32[]{:S(2)}) %collective-permute-start.35) | collective-permute-done | bytes 131104 | tf_op jit(solution)/shard_map/ppermute | solution.py:231
  (90 shorter events, 12.2 us)
Async XLA Ops:
  0.7 1.6 copy-start.2
  2.3 1.6 copy-start.4
  3.9 1.2 copy-start.6
  5.1 1.2 copy-start.8
  11.4 10.4 %collective-permute-start = (bf16[2,32,32,128]{3,2,1,0:T(8,128)(2,1)S(1)}, bf16[2,32,32,128]{3,2,1,0:T(8,128)(2,1)S(1)}, u32[]{:S(2)}, u32[]{:S(2)}) collective-permute-start(bf16[2,32,32,128]{3,2,1,0:T(8,128)(2,1)S(1)} %get-tuple-element.65), channel_id=1, source_target_pairs={{0,1},{1,0},{2,3},{3,2},{4,5},{5,4},{6,7},{7,6},{8,9},{9,8},{10,11... | collective-permute-start | bytes 1572872 | tf_op jit(solution)/shard_map/ppermute | solution.py:231
  11.9 15.3 %collective-permute-start.1 = (bf16[2,32,32,128]{3,2,1,0:T(8,128)(2,1)S(1)}, bf16[2,32,32,128]{3,2,1,0:T(8,128)(2,1)S(1)}, u32[]{:S(2)}, u32[]{:S(2)}) collective-permute-start(bf16[2,32,32,128]{3,2,1,0:T(8,128)(2,1)S(1)} %get-tuple-element.66), channel_id=1, source_target_pairs={{0,2},{1,3},{2,0},{3,1},{4,6},{5,7},{6,4},{7,5},{8,10},{9,11},{10,... | collective-permute-start | bytes 1572872 | tf_op jit(solution)/shard_map/ppermute | solution.py:231
  14.5 23.5 %copy-start = (bf16[2,32,128,128]{3,2,1,0:T(8,128)(2,1)S(1)}, bf16[2,32,128,128]{3,2,1,0:T(8,128)(2,1)}, u32[]{:S(2)}) copy-start(bf16[2,32,128,128]{3,2,1,0:T(8,128)(2,1)} %ul_ref.3) | copy-start | bytes 6291460
  14.5 23.5 %copy-start.1 = (bf16[2,32,128,128]{3,2,1,0:T(8,128)(2,1)S(1)}, bf16[2,32,128,128]{3,2,1,0:T(8,128)(2,1)}, u32[]{:S(2)}) copy-start(bf16[2,32,128,128]{3,2,1,0:T(8,128)(2,1)} %df_ref.3) | copy-start | bytes 6291460
  14.5 23.5 %collective-permute-start.2 = (bf16[2,32,32,128]{3,2,1,0:T(8,128)(2,1)S(1)}, bf16[2,32,32,128]{3,2,1,0:T(8,128)(2,1)S(1)}, u32[]{:S(2)}, u32[]{:S(2)}) collective-permute-start(bf16[2,32,32,128]{3,2,1,0:T(8,128)(2,1)S(1)} %get-tuple-element.67), channel_id=1, source_target_pairs={{0,3},{1,2},{2,1},{3,0},{4,7},{5,6},{6,5},{7,4},{8,11},{9,10},{10,... | collective-permute-start | bytes 1572872 | tf_op jit(solution)/shard_map/ppermute | solution.py:231
  19.6 31.8 %collective-permute-start.6 = (bf16[2,32,32,128]{3,2,1,0:T(8,128)(2,1)S(1)}, bf16[2,32,32,128]{3,2,1,0:T(8,128)(2,1)S(1)}, u32[]{:S(2)}, u32[]{:S(2)}) collective-permute-start(bf16[2,32,32,128]{3,2,1,0:T(8,128)(2,1)S(1)} %get-tuple-element.73), channel_id=1, source_target_pairs={{0,1},{1,0},{2,3},{3,2},{4,5},{5,4},{6,7},{7,6},{8,9},{9,8},{10,11... | collective-permute-start | bytes 1572872 | tf_op jit(solution)/shard_map/ppermute | solution.py:231
  19.9 31.6 %collective-permute-start.7 = (bf16[2,32,32,128]{3,2,1,0:T(8,128)(2,1)S(1)}, bf16[2,32,32,128]{3,2,1,0:T(8,128)(2,1)S(1)}, u32[]{:S(2)}, u32[]{:S(2)}) collective-permute-start(bf16[2,32,32,128]{3,2,1,0:T(8,128)(2,1)S(1)} %get-tuple-element.74), channel_id=1, source_target_pairs={{0,2},{1,3},{2,0},{3,1},{4,6},{5,7},{6,4},{7,5},{8,10},{9,11},{10,... | collective-permute-start | bytes 1572872 | tf_op jit(solution)/shard_map/ppermute | solution.py:231
  21.8 38.7 %collective-permute-start.8 = (bf16[2,32,32,128]{3,2,1,0:T(8,128)(2,1)S(1)}, bf16[2,32,32,128]{3,2,1,0:T(8,128)(2,1)S(1)}, u32[]{:S(2)}, u32[]{:S(2)}) collective-permute-start(bf16[2,32,32,128]{3,2,1,0:T(8,128)(2,1)S(1)} %get-tuple-element.75), channel_id=1, source_target_pairs={{0,3},{1,2},{2,1},{3,0},{4,7},{5,6},{6,5},{7,4},{8,11},{9,10},{10,... | collective-permute-start | bytes 1572872 | tf_op jit(solution)/shard_map/ppermute | solution.py:231
  49.0 28.0 %collective-permute-start.3 = (bf16[2,32,32,128]{3,2,1,0:T(8,128)(2,1)S(1)}, bf16[2,32,32,128]{3,2,1,0:T(8,128)(2,1)S(1)}, u32[]{:S(2)}, u32[]{:S(2)}) collective-permute-start(bf16[2,32,32,128]{3,2,1,0:T(8,128)(2,1)S(1)} %get-tuple-element.69), channel_id=1, source_target_pairs={{0,1},{1,0},{2,3},{3,2},{4,5},{5,4},{6,7},{7,6},{8,9},{9,8},{10,11... | collective-permute-start | bytes 1572872 | tf_op jit(solution)/shard_map/ppermute | solution.py:231
  49.5 27.8 %collective-permute-start.4 = (bf16[2,32,32,128]{3,2,1,0:T(8,128)(2,1)S(1)}, bf16[2,32,32,128]{3,2,1,0:T(8,128)(2,1)S(1)}, u32[]{:S(2)}, u32[]{:S(2)}) collective-permute-start(bf16[2,32,32,128]{3,2,1,0:T(8,128)(2,1)S(1)} %get-tuple-element.70), channel_id=1, source_target_pairs={{0,2},{1,3},{2,0},{3,1},{4,6},{5,7},{6,4},{7,5},{8,10},{9,11},{10,... | collective-permute-start | bytes 1572872 | tf_op jit(solution)/shard_map/ppermute | solution.py:231
  51.4 31.5 %collective-permute-start.5 = (bf16[2,32,32,128]{3,2,1,0:T(8,128)(2,1)S(1)}, bf16[2,32,32,128]{3,2,1,0:T(8,128)(2,1)S(1)}, u32[]{:S(2)}, u32[]{:S(2)}) collective-permute-start(bf16[2,32,32,128]{3,2,1,0:T(8,128)(2,1)S(1)} %get-tuple-element.71), channel_id=1, source_target_pairs={{0,3},{1,2},{2,1},{3,0},{4,7},{5,6},{6,5},{7,4},{8,11},{9,10},{10,... | collective-permute-start | bytes 1572872 | tf_op jit(solution)/shard_map/ppermute | solution.py:231
  51.4 21.5 %collective-permute-start.12 = (bf16[4,32,16,128]{3,2,1,0:T(8,128)(2,1)S(1)}, bf16[4,32,16,128]{3,2,1,0:T(8,128)(2,1)S(1)}, u32[]{:S(2)}, u32[]{:S(2)}) collective-permute-start(bf16[4,32,16,128]{3,2,1,0:T(8,128)(2,1)S(1)} %get-tuple-element.84), channel_id=1, source_target_pairs={{0,4},{4,0},{8,12},{12,8},{16,20},{20,16},{24,28},{28,24},{1,5},{5... | collective-permute-start | bytes 1572872 | tf_op jit(solution)/shard_map/ppermute | solution.py:231
  60.5 14.8 %collective-permute-start.13 = (bf16[4,32,16,128]{3,2,1,0:T(8,128)(2,1)S(1)}, bf16[4,32,16,128]{3,2,1,0:T(8,128)(2,1)S(1)}, u32[]{:S(2)}, u32[]{:S(2)}) collective-permute-start(bf16[4,32,16,128]{3,2,1,0:T(8,128)(2,1)S(1)} %get-tuple-element.85), channel_id=1, source_target_pairs={{0,8},{4,12},{8,0},{12,4},{16,24},{20,28},{24,16},{28,20},{1,9},{5... | collective-permute-start | bytes 1572872 | tf_op jit(solution)/shard_map/ppermute | solution.py:231
  73.0 13.4 %collective-permute-start.9 = (bf16[2,32,32,128]{3,2,1,0:T(8,128)(2,1)S(1)}, bf16[2,32,32,128]{3,2,1,0:T(8,128)(2,1)S(1)}, u32[]{:S(2)}, u32[]{:S(2)}) collective-permute-start(bf16[2,32,32,128]{3,2,1,0:T(8,128)(2,1)S(1)} %get-tuple-element.77), channel_id=1, source_target_pairs={{0,1},{1,0},{2,3},{3,2},{4,5},{5,4},{6,7},{7,6},{8,9},{9,8},{10,11... | collective-permute-start | bytes 1572872 | tf_op jit(solution)/shard_map/ppermute | solution.py:231
  75.2 19.5 %collective-permute-start.10 = (bf16[2,32,32,128]{3,2,1,0:T(8,128)(2,1)S(1)}, bf16[2,32,32,128]{3,2,1,0:T(8,128)(2,1)S(1)}, u32[]{:S(2)}, u32[]{:S(2)}) collective-permute-start(bf16[2,32,32,128]{3,2,1,0:T(8,128)(2,1)S(1)} %get-tuple-element.78), channel_id=1, source_target_pairs={{0,2},{1,3},{2,0},{3,1},{4,6},{5,7},{6,4},{7,5},{8,10},{9,11},{10,... | collective-permute-start | bytes 1572872 | tf_op jit(solution)/shard_map/ppermute | solution.py:231
  76.8 7.8 %copy-start.7 = (bf16[128,4096]{1,0:T(8,128)(2,1)S(1)}, bf16[128,4096]{1,0:T(8,128)(2,1)}, u32[]{:S(2)}) copy-start(bf16[128,4096]{1,0:T(8,128)(2,1)} %x_ref.7) | copy-start | bytes 3145732
  77.1 28.3 %collective-permute-start.11 = (bf16[2,32,32,128]{3,2,1,0:T(8,128)(2,1)S(1)}, bf16[2,32,32,128]{3,2,1,0:T(8,128)(2,1)S(1)}, u32[]{:S(2)}, u32[]{:S(2)}) collective-permute-start(bf16[2,32,32,128]{3,2,1,0:T(8,128)(2,1)S(1)} %get-tuple-element.79), channel_id=1, source_target_pairs={{0,3},{1,2},{2,1},{3,0},{4,7},{5,6},{6,5},{7,4},{8,11},{9,10},{10,... | collective-permute-start | bytes 1572872 | tf_op jit(solution)/shard_map/ppermute | solution.py:231
  77.2 33.5 %collective-permute-start.16 = (bf16[4,32,16,128]{3,2,1,0:T(8,128)(2,1)S(1)}, bf16[4,32,16,128]{3,2,1,0:T(8,128)(2,1)S(1)}, u32[]{:S(2)}, u32[]{:S(2)}) collective-permute-start(bf16[4,32,16,128]{3,2,1,0:T(8,128)(2,1)S(1)} %get-tuple-element.89), channel_id=1, source_target_pairs={{0,4},{4,0},{8,12},{12,8},{16,20},{20,16},{24,28},{28,24},{1,5},{5... | collective-permute-start | bytes 1572872 | tf_op jit(solution)/shard_map/ppermute | solution.py:231
  82.9 29.3 %collective-permute-start.17 = (bf16[4,32,16,128]{3,2,1,0:T(8,128)(2,1)S(1)}, bf16[4,32,16,128]{3,2,1,0:T(8,128)(2,1)S(1)}, u32[]{:S(2)}, u32[]{:S(2)}) collective-permute-start(bf16[4,32,16,128]{3,2,1,0:T(8,128)(2,1)S(1)} %get-tuple-element.90), channel_id=1, source_target_pairs={{0,8},{4,12},{8,0},{12,4},{16,24},{20,28},{24,16},{28,20},{1,9},{5... | collective-permute-start | bytes 1572872 | tf_op jit(solution)/shard_map/ppermute | solution.py:231
  84.6 22.4 %copy-start.3 = (bf16[2,32,128,128]{3,2,1,0:T(8,128)(2,1)S(1)}, bf16[2,32,128,128]{3,2,1,0:T(8,128)(2,1)}, u32[]{:S(2)}) copy-start(bf16[2,32,128,128]{3,2,1,0:T(8,128)(2,1)} %dl_ref.5) | copy-start | bytes 6291460
  84.6 22.4 %copy-start.5 = (bf16[2,32,128,128]{3,2,1,0:T(8,128)(2,1)S(1)}, bf16[2,32,128,128]{3,2,1,0:T(8,128)(2,1)}, u32[]{:S(2)}) copy-start(bf16[2,32,128,128]{3,2,1,0:T(8,128)(2,1)} %ur_ref.5) | copy-start | bytes 6291460
  86.4 25.8 %collective-permute-start.14 = (bf16[2,32,16,128]{3,2,1,0:T(8,128)(2,1)S(1)}, bf16[2,32,16,128]{3,2,1,0:T(8,128)(2,1)S(1)}, u32[]{:S(2)}, u32[]{:S(2)}) collective-permute-start(bf16[2,32,16,128]{3,2,1,0:T(8,128)(2,1)S(1)} %slice_bitcast_fusion.14), channel_id=1, source_target_pairs={{0,8},{4,12},{8,0},{12,4},{16,24},{20,28},{24,16},{28,20},{1,9},{5... | collective-permute-start | bytes 786440 | tf_op jit(solution)/shard_map/ppermute | solution.py:231
  94.7 17.6 %collective-permute-start.15 = (bf16[2,32,16,128]{3,2,1,0:T(8,128)(2,1)S(1)}, bf16[2,32,16,128]{3,2,1,0:T(8,128)(2,1)S(1)}, u32[]{:S(2)}, u32[]{:S(2)}) collective-permute-start(bf16[2,32,16,128]{3,2,1,0:T(8,128)(2,1)S(1)} %slice_bitcast_fusion.13), channel_id=1, source_target_pairs={{0,4},{4,0},{8,12},{12,8},{16,20},{20,16},{24,28},{28,24},{1,5},{5... | collective-permute-start | bytes 786440 | tf_op jit(solution)/shard_map/ppermute | solution.py:231
  105.4 30.0 %collective-permute-start.22 = (bf16[4,32,16,128]{3,2,1,0:T(8,128)(2,1)S(1)}, bf16[4,32,16,128]{3,2,1,0:T(8,128)(2,1)S(1)}, u32[]{:S(2)}, u32[]{:S(2)}) collective-permute-start(bf16[4,32,16,128]{3,2,1,0:T(8,128)(2,1)S(1)} %get-tuple-element.97), channel_id=1, source_target_pairs={{0,4},{4,0},{8,12},{12,8},{16,20},{20,16},{24,28},{28,24},{1,5},{5... | collective-permute-start | bytes 1572872 | tf_op jit(solution)/shard_map/ppermute | solution.py:231
  110.7 28.2 %collective-permute-start.23 = (bf16[4,32,16,128]{3,2,1,0:T(8,128)(2,1)S(1)}, bf16[4,32,16,128]{3,2,1,0:T(8,128)(2,1)S(1)}, u32[]{:S(2)}, u32[]{:S(2)}) collective-permute-start(bf16[4,32,16,128]{3,2,1,0:T(8,128)(2,1)S(1)} %get-tuple-element.98), channel_id=1, source_target_pairs={{0,8},{4,12},{8,0},{12,4},{16,24},{20,28},{24,16},{28,20},{1,9},{5... | collective-permute-start | bytes 1572872 | tf_op jit(solution)/shard_map/ppermute | solution.py:231
  112.4 15.0 %collective-permute-start.18 = (bf16[1,32,16,128]{3,2,1,0:T(8,128)(2,1)S(1)}, bf16[1,32,16,128]{3,2,1,0:T(8,128)(2,1)S(1)}, u32[]{:S(2)}, u32[]{:S(2)}) collective-permute-start(bf16[1,32,16,128]{3,2,1,0:T(8,128)(2,1)S(1)} %slice_bitcast_fusion.31), channel_id=1, source_target_pairs={{0,16},{4,20},{8,24},{12,28},{16,0},{20,4},{24,8},{28,12},{1,17},{... | collective-permute-start | bytes 393224 | tf_op jit(solution)/shard_map/ppermute | solution.py:231
  115.3 23.6 %collective-permute-start.20 = (bf16[2,32,16,128]{3,2,1,0:T(8,128)(2,1)S(1)}, bf16[2,32,16,128]{3,2,1,0:T(8,128)(2,1)S(1)}, u32[]{:S(2)}, u32[]{:S(2)}) collective-permute-start(bf16[2,32,16,128]{3,2,1,0:T(8,128)(2,1)S(1)} %slice_bitcast_fusion.11), channel_id=1, source_target_pairs={{0,8},{4,12},{8,0},{12,4},{16,24},{20,28},{24,16},{28,20},{1,9},{5... | collective-permute-start | bytes 786440 | tf_op jit(solution)/shard_map/ppermute | solution.py:231
  116.0 22.9 %collective-permute-start.21 = (bf16[2,32,16,128]{3,2,1,0:T(8,128)(2,1)S(1)}, bf16[2,32,16,128]{3,2,1,0:T(8,128)(2,1)S(1)}, u32[]{:S(2)}, u32[]{:S(2)}) collective-permute-start(bf16[2,32,16,128]{3,2,1,0:T(8,128)(2,1)S(1)} %slice_bitcast_fusion.10), channel_id=1, source_target_pairs={{0,4},{4,0},{8,12},{12,8},{16,20},{20,16},{24,28},{28,24},{1,5},{5... | collective-permute-start | bytes 786440 | tf_op jit(solution)/shard_map/ppermute | solution.py:231
  127.4 7.5 %collective-permute-start.19 = (bf16[1,32,16,128]{3,2,1,0:T(8,128)(2,1)S(1)}, bf16[1,32,16,128]{3,2,1,0:T(8,128)(2,1)S(1)}, u32[]{:S(2)}, u32[]{:S(2)}) collective-permute-start(bf16[1,32,16,128]{3,2,1,0:T(8,128)(2,1)S(1)} %slice_bitcast_fusion.30), channel_id=1, source_target_pairs={{0,16},{4,20},{8,24},{12,28},{16,0},{20,4},{24,8},{28,12},{1,17},{... | collective-permute-start | bytes 393224 | tf_op jit(solution)/shard_map/ppermute | solution.py:231
  134.9 14.9 %collective-permute-start.28 = (bf16[4,32,16,128]{3,2,1,0:T(8,128)(2,1)S(1)}, bf16[4,32,16,128]{3,2,1,0:T(8,128)(2,1)S(1)}, u32[]{:S(2)}, u32[]{:S(2)}) collective-permute-start(bf16[4,32,16,128]{3,2,1,0:T(8,128)(2,1)S(1)} %get-tuple-element.104), channel_id=1, source_target_pairs={{0,4},{4,0},{8,12},{12,8},{16,20},{20,16},{24,28},{28,24},{1,5},{5... | collective-permute-start | bytes 1572872 | tf_op jit(solution)/shard_map/ppermute | solution.py:231
  135.4 21.9 %collective-permute-start.29 = (bf16[4,32,16,128]{3,2,1,0:T(8,128)(2,1)S(1)}, bf16[4,32,16,128]{3,2,1,0:T(8,128)(2,1)S(1)}, u32[]{:S(2)}, u32[]{:S(2)}) collective-permute-start(bf16[4,32,16,128]{3,2,1,0:T(8,128)(2,1)S(1)} %get-tuple-element.105), channel_id=1, source_target_pairs={{0,8},{4,12},{8,0},{12,4},{16,24},{20,28},{24,16},{28,20},{1,9},{5... | collective-permute-start | bytes 1572872 | tf_op jit(solution)/shard_map/ppermute | solution.py:231
  139.0 18.3 %collective-permute-start.24 = (bf16[1,32,16,128]{3,2,1,0:T(8,128)(2,1)S(1)}, bf16[1,32,16,128]{3,2,1,0:T(8,128)(2,1)S(1)}, u32[]{:S(2)}, u32[]{:S(2)}) collective-permute-start(bf16[1,32,16,128]{3,2,1,0:T(8,128)(2,1)S(1)} %slice_bitcast_fusion.29), channel_id=1, source_target_pairs={{0,16},{4,20},{8,24},{12,28},{16,0},{20,4},{24,8},{28,12},{1,17},{... | collective-permute-start | bytes 393224 | tf_op jit(solution)/shard_map/ppermute | solution.py:231
  139.3 21.8 %collective-permute-start.26 = (bf16[2,32,16,128]{3,2,1,0:T(8,128)(2,1)S(1)}, bf16[2,32,16,128]{3,2,1,0:T(8,128)(2,1)S(1)}, u32[]{:S(2)}, u32[]{:S(2)}) collective-permute-start(bf16[2,32,16,128]{3,2,1,0:T(8,128)(2,1)S(1)} %slice_bitcast_fusion.6), channel_id=1, source_target_pairs={{0,8},{4,12},{8,0},{12,4},{16,24},{20,28},{24,16},{28,20},{1,9},{5... | collective-permute-start | bytes 786440 | tf_op jit(solution)/shard_map/ppermute | solution.py:231
  141.4 19.6 %collective-permute-start.27 = (bf16[2,32,16,128]{3,2,1,0:T(8,128)(2,1)S(1)}, bf16[2,32,16,128]{3,2,1,0:T(8,128)(2,1)S(1)}, u32[]{:S(2)}, u32[]{:S(2)}) collective-permute-start(bf16[2,32,16,128]{3,2,1,0:T(8,128)(2,1)S(1)} %slice_bitcast_fusion.5), channel_id=1, source_target_pairs={{0,4},{4,0},{8,12},{12,8},{16,20},{20,16},{24,28},{28,24},{1,5},{5... | collective-permute-start | bytes 786440 | tf_op jit(solution)/shard_map/ppermute | solution.py:231
  149.7 10.6 %collective-permute-start.25 = (bf16[1,32,16,128]{3,2,1,0:T(8,128)(2,1)S(1)}, bf16[1,32,16,128]{3,2,1,0:T(8,128)(2,1)S(1)}, u32[]{:S(2)}, u32[]{:S(2)}) collective-permute-start(bf16[1,32,16,128]{3,2,1,0:T(8,128)(2,1)S(1)} %slice_bitcast_fusion.28), channel_id=1, source_target_pairs={{0,16},{4,20},{8,24},{12,28},{16,0},{20,4},{24,8},{28,12},{1,17},{... | collective-permute-start | bytes 393224 | tf_op jit(solution)/shard_map/ppermute | solution.py:231
  161.2 10.9 %collective-permute-start.30 = (bf16[1,32,16,128]{3,2,1,0:T(8,128)(2,1)S(1)}, bf16[1,32,16,128]{3,2,1,0:T(8,128)(2,1)S(1)}, u32[]{:S(2)}, u32[]{:S(2)}) collective-permute-start(bf16[1,32,16,128]{3,2,1,0:T(8,128)(2,1)S(1)} %slice_bitcast_fusion.26), channel_id=1, source_target_pairs={{0,16},{4,20},{8,24},{12,28},{16,0},{20,4},{24,8},{28,12},{1,17},{... | collective-permute-start | bytes 393224 | tf_op jit(solution)/shard_map/ppermute | solution.py:231
  164.0 10.3 %collective-permute-start.31 = (bf16[1,32,16,128]{3,2,1,0:T(8,128)(2,1)S(1)}, bf16[1,32,16,128]{3,2,1,0:T(8,128)(2,1)S(1)}, u32[]{:S(2)}, u32[]{:S(2)}) collective-permute-start(bf16[1,32,16,128]{3,2,1,0:T(8,128)(2,1)S(1)} %slice_bitcast_fusion.25), channel_id=1, source_target_pairs={{0,16},{4,20},{8,24},{12,28},{16,0},{20,4},{24,8},{28,12},{1,17},{... | collective-permute-start | bytes 393224 | tf_op jit(solution)/shard_map/ppermute | solution.py:231
  164.5 11.0 %collective-permute-start.32 = (bf16[2,32,16,128]{3,2,1,0:T(8,128)(2,1)S(1)}, bf16[2,32,16,128]{3,2,1,0:T(8,128)(2,1)S(1)}, u32[]{:S(2)}, u32[]{:S(2)}) collective-permute-start(bf16[2,32,16,128]{3,2,1,0:T(8,128)(2,1)S(1)} %slice_bitcast_fusion.3), channel_id=1, source_target_pairs={{0,8},{4,12},{8,0},{12,4},{16,24},{20,28},{24,16},{28,20},{1,9},{5... | collective-permute-start | bytes 786440 | tf_op jit(solution)/shard_map/ppermute | solution.py:231
  166.4 9.1 %collective-permute-start.33 = (bf16[2,32,16,128]{3,2,1,0:T(8,128)(2,1)S(1)}, bf16[2,32,16,128]{3,2,1,0:T(8,128)(2,1)S(1)}, u32[]{:S(2)}, u32[]{:S(2)}) collective-permute-start(bf16[2,32,16,128]{3,2,1,0:T(8,128)(2,1)S(1)} %slice_bitcast_fusion.2), channel_id=1, source_target_pairs={{0,4},{4,0},{8,12},{12,8},{16,20},{20,16},{24,28},{28,24},{1,5},{5... | collective-permute-start | bytes 786440 | tf_op jit(solution)/shard_map/ppermute | solution.py:231
  175.6 9.6 %collective-permute-start.34 = (bf16[1,32,16,128]{3,2,1,0:T(8,128)(2,1)S(1)}, bf16[1,32,16,128]{3,2,1,0:T(8,128)(2,1)S(1)}, u32[]{:S(2)}, u32[]{:S(2)}) collective-permute-start(bf16[1,32,16,128]{3,2,1,0:T(8,128)(2,1)S(1)} %slice_bitcast_fusion.23), channel_id=1, source_target_pairs={{0,16},{4,20},{8,24},{12,28},{16,0},{20,4},{24,8},{28,12},{1,17},{... | collective-permute-start | bytes 393224 | tf_op jit(solution)/shard_map/ppermute | solution.py:231
  175.7 11.4 %collective-permute-start.35 = (bf16[1,32,16,128]{3,2,1,0:T(8,128)(2,1)S(1)}, bf16[1,32,16,128]{3,2,1,0:T(8,128)(2,1)S(1)}, u32[]{:S(2)}, u32[]{:S(2)}) collective-permute-start(bf16[1,32,16,128]{3,2,1,0:T(8,128)(2,1)S(1)} %slice_bitcast_fusion.22), channel_id=1, source_target_pairs={{0,16},{4,20},{8,24},{12,28},{16,0},{20,4},{24,8},{28,12},{1,17},{... | collective-permute-start | bytes 393224 | tf_op jit(solution)/shard_map/ppermute | solution.py:231

commit v4 on v3

--- a/solution.py
+++ b/solution.py
@@ -154,36 +154,42 @@
     return res[:n], res[n:]
 
 
-def last_grads_kernel(mp_ways, dp_ways, me_ref, x_ref, g_ref, *rest):
-    n = mp_ways
-    second_in, grads = rest[:n], rest[n : n + 4]
-    asm_d, asm_u, gr1, gr2 = rest[n + 4 :]
+def last_grads_kernel(groups, dp_ways, me_ref, x_ref, g_ref, *rest):
+    count = len(rest) - 8
+    n = count // groups
+    second_in, grads = rest[:count], rest[count : count + 4]
+    asm_d, asm_u, gr1, gr2 = rest[count + 4 :]
     blocks = second_in[0].shape[1]
     width = gr1.shape[1]
     me_mp, me_dp = me_ref[0], me_ref[1]
-    for e in range(blocks):
-        cols = slice(e * width, (e + 1) * width)
-        slot = e % UNROLL
-        cd = gather_rows(second_in, 0, asm_d, slot, me_mp, e, blocks)
-        rg = gather_rows(second_in, 1, asm_u, slot, me_mp, e, blocks)
-        store_grad(grads, 0, e, mm(cd, g_ref[:, cols], 1, 0), gr1, slot, me_dp, dp_ways)
-        store_grad(grads, 1, e, mm(rg, x_ref[:, cols], 1, 0).T, gr2, slot, me_dp, dp_ways)
-
-
-def make_last_grads(me, second_in, x, g, width, dp_ways):
-    n = len(second_in)
-    part = second_in[0]
+    for q in range(groups):
+        parts = second_in[q * n : (q + 1) * n]
+        for e in range(blocks):
+            cols = slice(e * width, (e + 1) * width)
+            slot = e % UNROLL
+            cd = gather_rows(parts, 0, asm_d, slot, me_mp, e, blocks)
+            rg = gather_rows(parts, 1, asm_u, slot, me_mp, e, blocks)
+            down = mm(cd, g_ref[:, cols], 1, 0)
+            right = mm(rg, x_ref[:, cols], 1, 0).T
+            store_grad(grads, 0, q * blocks + e, down, gr1, slot, me_dp, dp_ways)
+            store_grad(grads, 1, q * blocks + e, right, gr2, slot, me_dp, dp_ways)
+
+
+def make_last_grads(me, seconds, x, g, width, dp_ways):
+    groups = len(seconds)
+    parts = [p for second in seconds for p in second]
+    part = parts[0]
     blocks, tok = part.shape[1], part.shape[3]
-    half = grad_halves(blocks, width, dp_ways)
+    half = grad_halves(groups * blocks, width, dp_ways)
     return pl.pallas_call(
-        functools.partial(last_grads_kernel, n, dp_ways),
+        functools.partial(last_grads_kernel, groups, dp_ways),
         out_shape=[half] * 4,
         grid=(1,),
-        in_specs=[pl.BlockSpec(memory_space=pltpu.SMEM)] + [full_spec(x.shape)] * 2 + [full_spec(part.shape)] * n,
+        in_specs=[pl.BlockSpec(memory_space=pltpu.SMEM)] + [full_spec(x.shape)] * 2 + [full_spec(part.shape)] * len(parts),
         out_specs=[full_spec(half.shape)] * 4,
         scratch_shapes=[pltpu.VMEM((UNROLL, width, tok), F32)] * 2 + [pltpu.VMEM((UNROLL, width, width), F32)] * 2,
-        **limits(4 * tok * blocks * width * width, 6),
-    )(me, x, g, *second_in)
+        **limits(4 * groups * tok * blocks * width * width, 12),
+    )(me, x, g, *parts)
 
 
 def outputs_kernel(mp_ways, me_ref, dl_ref, ur_ref, *rest):
@@ -244,7 +250,9 @@
     for turn in range(hops + len(reductions) - 1):
         active = [(s, kind) for s in range(len(reductions)) if 0 <= turn - s < hops for kind in range(2)]
         got = [xor_permute(pairs[s][kind][1], "dp", orders[kind][turn - s]) for s, kind in active]
-        got = lax.optimization_barrier(got)
+        following = pairs[turn + 1] if turn + 1 < len(pairs) else []
+        got, following = lax.optimization_barrier((got, following))
+        pairs[turn + 1 : turn + 2] = [following] if following else []
         for (s, kind), arrived in zip(active, got):
             total = pairs[s][kind][0].astype(F32) + arrived.astype(F32)
             if total.shape[0] == 1:
@@ -267,16 +275,15 @@
         panels, halves = make_middle(me, firsts[q], up_left, down_first_factor, q, dp_ways)
         seconds.append(exchange(panels))
         reductions.append(halves)
-    for q in range(groups):
-        reductions.append(make_last_grads(me, seconds[q], tokens, cotangent, width, dp_ways))
+    reductions.append(make_last_grads(me, seconds, tokens, cotangent, width, dp_ways))
     sums = halving_rounds(reductions, scale)
-    mid_sums, last_sums = sums[:groups], sums[groups:]
+    mid_sums, last_sums = sums[:groups], [s.reshape((groups, -1) + s.shape[1:]) for s in sums[groups]]
     mixed, tokens_grad = make_outputs(me, seconds, down_left, up_right)
 
     def pick(sums, kind):
         return jnp.stack([s[kind] for s in sums])
 
-    return (mixed, tokens_grad, pick(last_sums, 1), pick(mid_sums, 1), pick(mid_sums, 0), pick(last_sums, 0))
+    return (mixed, tokens_grad, last_sums[1], pick(mid_sums, 1), pick(mid_sums, 0), last_sums[0])
 
 
 def solution(mesh):

time: 189 us -> 208 us (1.10)
  waiting for transfers between devices: 87.6 us -> 121 us
  starting transfers between devices: 49.7 us -> 36.7 us
    ppermute x36 -> x30, waiting for transfers between devices: 87.6 us -> 121 us  [xor_permute(): lax.ppermute(array, axis, [(i, i ^ k) for i in range(lax.axis_size(axis))])]
    ppermute x36 -> x30, starting transfers between devices: 49.7 us -> 36.7 us  [xor_permute(): lax.ppermute(array, axis, [(i, i ^ k) for i in range(lax.axis_size(axis))])]
  transfers between devices with their start and end apart: 36 -> 30, of which waited for: 18 -> 14; matrix products, arithmetic and copies ran while one was open for 2% -> 1% of each run, Pallas kernels for 18% -> 16%
where the time goes in v4:
time: 208 us
  waiting for transfers between devices  121 us (58%)
  Pallas kernels  38.7 us (19%)
  starting transfers between devices  36.7 us (18%)
  local copies, waits for them, and re-layouts  5.88 us (3%)
  other arithmetic  4.68 us (2%)
    ppermute x30, waiting for transfers between devices, xor_permute(): lax.ppermute(array, axis, [(i, i ^ k) for i in range(lax.axis_size(axis))])  121 us
    ppermute x30, starting transfers between devices, xor_permute(): lax.ppermute(array, axis, [(i, i ^ k) for i in range(lax.axis_size(axis))])  36.7 us
    pallas_call x2, Pallas kernels, make_middle(): pl.pallas_call(functools.partial(middle_kernel, n, dp_ways), out_shape=[p...  21.9 us
    pallas_call x2, Pallas kernels, make_panels(): pl.pallas_call(functools.partial(panels_kernel, ways), out_shape=[part] *...  10.1 us
    unnamed x18, local copies, waits for them, and re-layouts  5.65 us
  transfers between devices with their start and end apart: 30, of which 14 were waited for; matrix products, arithmetic and copies ran while one was open for 1% of the time, Pallas kernels for 16%

profile of v4, /device:TPU:0, one launch (start us, length us, event | category | flops | bytes accessed | tf_op | source)
XLA Modules:
  0.0 207.9 jit_solution(983511951469077911)
XLA Ops:
  0.7 1.6 copy-done.2
  2.3 1.6 copy-done.4
  3.9 1.2 copy-done.6
  5.1 1.2 copy-done.8
  6.3 5.1 %shard_map.109 = (bf16[2,32,32,128]{3,2,1,0:T(8,128)(2,1)S(1)}, bf16[2,32,32,128]{3,2,1,0:T(8,128)(2,1)S(1)}, bf16[2,32,32,128]{3,2,1,0:T(8,128)(2,1)S(1)}, bf16[2,32,32,128]{3,2,1,0:T(8,128)(2,1)S(1)}) custom-call(s32[2]{0:T(128)S(1)} %pad_add_fusion.me_ref, bf16[128,4096]{1,0:T(8,128)(2,1)S(1)} %copy-done.6, bf16[128,4096]{1,0:T(8,128)(2,1)S(1)} %copy-done.8, ...), custom_call_target="tpu_custom_call" | custom-call | flops 2147483648 | bytes 8388608 | tf_op jit(solution)/shard_map/pallas_call | solution.py:81
  11.9 2.6 %collective-permute-start.1 = (bf16[2,32,32,128]{3,2,1,0:T(8,128)(2,1)S(1)}, bf16[2,32,32,128]{3,2,1,0:T(8,128)(2,1)S(1)}, u32[]{:S(2)}, u32[]{:S(2)}) collective-permute-start(bf16[2,32,32,128]{3,2,1,0:T(8,128)(2,1)S(1)} %get-tuple-element.64), channel_id=1, source_target_pairs={{0,2},{1,3},{2,0},{3,1},{4,6},{5,7},{6,4},{7,5},{8,10},{9,11},{10,... | collective-permute-start | bytes 1572872 | tf_op jit(solution)/shard_map/ppermute | solution.py:237
  14.6 5.1 %shard_map.111 = (bf16[2,32,32,128]{3,2,1,0:T(8,128)(2,1)S(1)}, bf16[2,32,32,128]{3,2,1,0:T(8,128)(2,1)S(1)}, bf16[2,32,32,128]{3,2,1,0:T(8,128)(2,1)S(1)}, bf16[2,32,32,128]{3,2,1,0:T(8,128)(2,1)S(1)}) custom-call(s32[2]{0:T(128)S(1)} %pad_add_fusion.me_ref, bf16[128,4096]{1,0:T(8,128)(2,1)S(1)} %copy-done.6, bf16[128,4096]{1,0:T(8,128)(2,1)S(1)} %copy-done.8, ...), custom_call_target="tpu_custom_call" | custom-call | flops 2147483648 | bytes 8388608 | tf_op jit(solution)/shard_map/pallas_call | solution.py:81
  19.9 1.9 collective-permute-start.7
  21.8 5.5 %collective-permute-done.1.rest_2_ = bf16[2,32,32,128]{3,2,1,0:T(8,128)(2,1)S(1)} collective-permute-done((bf16[2,32,32,128]{3,2,1,0:T(8,128)(2,1)S(1)}, bf16[2,32,32,128]{3,2,1,0:T(8,128)(2,1)S(1)}, u32[]{:S(2)}, u32[]{:S(2)}) %collective-permute-start.1) | collective-permute-done | bytes 524320 | tf_op jit(solution)/shard_map/ppermute | solution.py:237
  27.3 10.7 %collective-permute-done.2.rest_3_ = bf16[2,32,32,128]{3,2,1,0:T(8,128)(2,1)S(1)} collective-permute-done((bf16[2,32,32,128]{3,2,1,0:T(8,128)(2,1)S(1)}, bf16[2,32,32,128]{3,2,1,0:T(8,128)(2,1)S(1)}, u32[]{:S(2)}, u32[]{:S(2)}) %collective-permute-start.2) | collective-permute-done | bytes 524320 | tf_op jit(solution)/shard_map/ppermute | solution.py:237
  38.0 11.0 %shard_map.110 = (bf16[2,32,32,128]{3,2,1,0:T(8,128)(2,1)S(1)}, bf16[2,32,32,128]{3,2,1,0:T(8,128)(2,1)S(1)}, bf16[2,32,32,128]{3,2,1,0:T(8,128)(2,1)S(1)}, bf16...) custom-call(s32[2]{0:T(128)S(1)} %pad_add_fusion.me_ref, ...), custom_call_target="tpu_custom_call" | custom-call | flops 6442450944 | bytes 8388608 | tf_op jit(solution)/shard_map/pallas_call | solution.py:143
  49.0 1.6 collective-permute-start.12
  50.7 1.6 collective-permute-start.13
  52.3 8.2 %collective-permute-done.8.rest_3_ = bf16[2,32,32,128]{3,2,1,0:T(8,128)(2,1)S(1)} collective-permute-done((bf16[2,32,32,128]{3,2,1,0:T(8,128)(2,1)S(1)}, bf16[2,32,32,128]{3,2,1,0:T(8,128)(2,1)S(1)}, u32[]{:S(2)}, u32[]{:S(2)}) %collective-permute-start.8) | collective-permute-done | bytes 524320 | tf_op jit(solution)/shard_map/ppermute | solution.py:237
  60.5 10.9 %shard_map.112 = (bf16[2,32,32,128]{3,2,1,0:T(8,128)(2,1)S(1)}, bf16[2,32,32,128]{3,2,1,0:T(8,128)(2,1)S(1)}, bf16[2,32,32,128]{3,2,1,0:T(8,128)(2,1)S(1)}, bf16...) custom-call(s32[2]{0:T(128)S(1)} %pad_add_fusion.me_ref, ...), custom_call_target="tpu_custom_call" | custom-call | flops 6442450944 | bytes 8388608 | tf_op jit(solution)/shard_map/pallas_call | solution.py:143
  71.3 1.6 collective-permute-start.10
  73.8 1.7 collective-permute-start.4
  75.6 10.6 %collective-permute-done.10.rest_6_ = bf16[2,32,32,128]{3,2,1,0:T(8,128)(2,1)S(1)} collective-permute-done((bf16[2,32,32,128]{3,2,1,0:T(8,128)(2,1)S(1)}, bf16[2,32,32,128]{3,2,1,0:T(8,128)(2,1)S(1)}, u32[]{:S(2)}, u32[]{:S(2)}) %collective-permute-start.10) | collective-permute-done | bytes 524320 | tf_op jit(solution)/shard_map/ppermute | solution.py:237
  86.1 0.7 collective-permute-start.5
  87.0 9.4 %collective-permute-done.11.rest_7_ = bf16[2,32,32,128]{3,2,1,0:T(8,128)(2,1)S(1)} collective-permute-done((bf16[2,32,32,128]{3,2,1,0:T(8,128)(2,1)S(1)}, bf16[2,32,32,128]{3,2,1,0:T(8,128)(2,1)S(1)}, u32[]{:S(2)}, u32[]{:S(2)}) %collective-permute-start.11) | collective-permute-done | bytes 524320 | tf_op jit(solution)/shard_map/ppermute | solution.py:237
  96.4 1.9 collective-permute-start.16
  98.3 1.6 collective-permute-start.17
  99.9 0.6 collective-permute-start.15
  100.5 8.1 %collective-permute-done.4.rest_2_ = bf16[2,32,32,128]{3,2,1,0:T(8,128)(2,1)S(1)} collective-permute-done((bf16[2,32,32,128]{3,2,1,0:T(8,128)(2,1)S(1)}, bf16[2,32,32,128]{3,2,1,0:T(8,128)(2,1)S(1)}, u32[]{:S(2)}, u32[]{:S(2)}) %collective-permute-start.4) | collective-permute-done | bytes 524320 | tf_op jit(solution)/shard_map/ppermute | solution.py:237
  108.6 1.6 collective-permute-start.14
  110.2 8.6 %collective-permute-done.5.rest_3_ = bf16[2,32,32,128]{3,2,1,0:T(8,128)(2,1)S(1)} collective-permute-done((bf16[2,32,32,128]{3,2,1,0:T(8,128)(2,1)S(1)}, bf16[2,32,32,128]{3,2,1,0:T(8,128)(2,1)S(1)}, u32[]{:S(2)}, u32[]{:S(2)}) %collective-permute-start.5) | collective-permute-done | bytes 524320 | tf_op jit(solution)/shard_map/ppermute | solution.py:237
  118.9 2.9 %shard_map.114 = (bf16[4,64,16,128]{3,2,1,0:T(8,128)(2,1)S(1)}, bf16[4,64,16,128]{3,2,1,0:T(8,128)(2,1)S(1)}, bf16[4,64,16,128]{3,2,1,0:T(8,128)(2,1)S(1)}, bf16[4,64,16,128]{3,2,1,0:T(8,128)(2,1)S(1)}) custom-call(s32[2]{0:T(128)S(1)} %pad_add_fusion.me_ref, bf16[128,4096]{1,0:T(8,128)(2,1)S(1)} %copy-done.7, bf16[128,4096]{1,0:T(8,128)(2,1)S(1)} %copy-done.8, ...), custom_call_target="tpu_custom_call" | custom-call | flops 4294967296 | bytes 12582912 | tf_op jit(solution)/shard_map/pallas_call | solution.py:184
  122.1 2.0 collective-permute-start.21
  124.2 1.6 collective-permute-start.20
  125.9 0.6 collective-permute-start.22
  126.6 3.1 %collective-permute-start.19 = (bf16[1,32,16,128]{3,2,1,0:T(8,128)(2,1)S(1)}, bf16[1,32,16,128]{3,2,1,0:T(8,128)(2,1)S(1)}, u32[]{:S(2)}, u32[]{:S(2)}) collective-permute-start(bf16[1,32,16,128]{3,2,1,0:T(8,128)(2,1)S(1)} %slice_bitcast_fusion.22), channel_id=1, source_target_pairs={{0,16},{4,20},{8,24},{12,28},{16,0},{20,4},{24,8},{28,12},{1,17},{... | collective-permute-start | bytes 393224 | tf_op jit(solution)/shard_map/ppermute | solution.py:237
  129.7 27.0 %collective-permute-done.19 = bf16[1,32,16,128]{3,2,1,0:T(8,128)(2,1)S(1)} collective-permute-done((bf16[1,32,16,128]{3,2,1,0:T(8,128)(2,1)S(1)}, bf16[1,32,16,128]{3,2,1,0:T(8,128)(2,1)S(1)}, u32[]{:S(2)}, u32[]{:S(2)}) %collective-permute-start.19) | collective-permute-done | bytes 131104 | tf_op jit(solution)/shard_map/ppermute | solution.py:237
  156.7 3.4 %collective-permute-start.18 = (bf16[1,32,16,128]{3,2,1,0:T(8,128)(2,1)S(1)}, bf16[1,32,16,128]{3,2,1,0:T(8,128)(2,1)S(1)}, u32[]{:S(2)}, u32[]{:S(2)}) collective-permute-start(bf16[1,32,16,128]{3,2,1,0:T(8,128)(2,1)S(1)} %slice_bitcast_fusion.23), channel_id=1, source_target_pairs={{0,16},{4,20},{8,24},{12,28},{16,0},{20,4},{24,8},{28,12},{1,17},{... | collective-permute-start | bytes 393224 | tf_op jit(solution)/shard_map/ppermute | solution.py:237
  160.1 3.7 %shard_map.113 = (bf16[128,4096]{1,0:T(8,128)(2,1)}, bf16[128,4096]{1,0:T(8,128)(2,1)}) custom-call(s32[2]{0:T(128)S(1)} %pad_add_fusion.me_ref, bf16[2,32,128,128]{3,2,1,0:T(8,128)(2,1)S(1)} %copy-done.3, bf16[2,32,128,128]{3,2,1,0:T(8,128)(2,1)S(1)} %copy-done.5, bf16[2,32,32,128]{3,2,1,0:T(8,128)(2,1)S(1)} %get-tuple-element.66.rest_0_, ...), custom_call_target="tpu_custom_call" | custom-call | flops 4294967296 | bytes 10485760 | tf_op jit(solution)/shard_map/pallas_call | solution.py:223
  163.8 2.1 collective-permute-done.18
  166.2 0.6 collective-permute-start.27
  167.6 2.5 %collective-permute-start.25 = (bf16[1,32,16,128]{3,2,1,0:T(8,128)(2,1)S(1)}, bf16[1,32,16,128]{3,2,1,0:T(8,128)(2,1)S(1)}, u32[]{:S(2)}, u32[]{:S(2)}) collective-permute-start(bf16[1,32,16,128]{3,2,1,0:T(8,128)(2,1)S(1)} %slice_bitcast_fusion.20), channel_id=1, source_target_pairs={{0,16},{4,20},{8,24},{12,28},{16,0},{20,4},{24,8},{28,12},{1,17},{... | collective-permute-start | bytes 393224 | tf_op jit(solution)/shard_map/ppermute | solution.py:237
  170.2 0.6 collective-permute-start.24
  170.8 9.8 %collective-permute-done.25 = bf16[1,32,16,128]{3,2,1,0:T(8,128)(2,1)S(1)} collective-permute-done((bf16[1,32,16,128]{3,2,1,0:T(8,128)(2,1)S(1)}, bf16[1,32,16,128]{3,2,1,0:T(8,128)(2,1)S(1)}, u32[]{:S(2)}, u32[]{:S(2)}) %collective-permute-start.25) | collective-permute-done | bytes 131104 | tf_op jit(solution)/shard_map/ppermute | solution.py:237
  180.6 1.4 collective-permute-done.24
  182.0 1.0 collective-permute-done.26
  183.2 2.5 %collective-permute-start.29 = (bf16[1,64,16,128]{3,2,1,0:T(8,128)(2,1)S(1)}, bf16[1,64,16,128]{3,2,1,0:T(8,128)(2,1)S(1)}, u32[]{:S(2)}, u32[]{:S(2)}) collective-permute-start(bf16[1,64,16,128]{3,2,1,0:T(8,128)(2,1)S(1)} %slice_bitcast_fusion.5), channel_id=1, source_target_pairs={{0,16},{4,20},{8,24},{12,28},{16,0},{20,4},{24,8},{28,12},{1,17},{... | collective-permute-start | bytes 786440 | tf_op jit(solution)/shard_map/ppermute | solution.py:237
  185.8 0.6 collective-permute-start.28
  186.5 0.8 pad_maximum_fusion.1
  187.3 0.8 pad_maximum_fusion
  188.1 14.9 %collective-permute-done.29 = bf16[1,64,16,128]{3,2,1,0:T(8,128)(2,1)S(1)} collective-permute-done((bf16[1,64,16,128]{3,2,1,0:T(8,128)(2,1)S(1)}, bf16[1,64,16,128]{3,2,1,0:T(8,128)(2,1)S(1)}, u32[]{:S(2)}, u32[]{:S(2)}) %collective-permute-start.29) | collective-permute-done | bytes 262176 | tf_op jit(solution)/shard_map/ppermute | solution.py:237
  203.0 3.8 %collective-permute-done.28 = bf16[1,64,16,128]{3,2,1,0:T(8,128)(2,1)S(1)} collective-permute-done((bf16[1,64,16,128]{3,2,1,0:T(8,128)(2,1)S(1)}, bf16[1,64,16,128]{3,2,1,0:T(8,128)(2,1)S(1)}, u32[]{:S(2)}, u32[]{:S(2)}) %collective-permute-start.28) | collective-permute-done | bytes 262176 | tf_op jit(solution)/shard_map/ppermute | solution.py:237
  206.8 1.1 fusion.4
  (66 shorter events, 4.3 us)
Async XLA Ops:
  0.7 1.6 copy-start.2
  2.3 1.6 copy-start.4
  3.9 1.2 copy-start.6
  5.1 1.2 copy-start.8
  11.4 10.4 %collective-permute-start = (bf16[2,32,32,128]{3,2,1,0:T(8,128)(2,1)S(1)}, bf16[2,32,32,128]{3,2,1,0:T(8,128)(2,1)S(1)}, u32[]{:S(2)}, u32[]{:S(2)}) collective-permute-start(bf16[2,32,32,128]{3,2,1,0:T(8,128)(2,1)S(1)} %get-tuple-element.63), channel_id=1, source_target_pairs={{0,1},{1,0},{2,3},{3,2},{4,5},{5,4},{6,7},{7,6},{8,9},{9,8},{10,11... | collective-permute-start | bytes 1572872 | tf_op jit(solution)/shard_map/ppermute | solution.py:237
  11.9 15.3 %collective-permute-start.1 = (bf16[2,32,32,128]{3,2,1,0:T(8,128)(2,1)S(1)}, bf16[2,32,32,128]{3,2,1,0:T(8,128)(2,1)S(1)}, u32[]{:S(2)}, u32[]{:S(2)}) collective-permute-start(bf16[2,32,32,128]{3,2,1,0:T(8,128)(2,1)S(1)} %get-tuple-element.64), channel_id=1, source_target_pairs={{0,2},{1,3},{2,0},{3,1},{4,6},{5,7},{6,4},{7,5},{8,10},{9,11},{10,... | collective-permute-start | bytes 1572872 | tf_op jit(solution)/shard_map/ppermute | solution.py:237
  14.5 23.5 %copy-start = (bf16[2,32,128,128]{3,2,1,0:T(8,128)(2,1)S(1)}, bf16[2,32,128,128]{3,2,1,0:T(8,128)(2,1)}, u32[]{:S(2)}) copy-start(bf16[2,32,128,128]{3,2,1,0:T(8,128)(2,1)} %ul_ref.3) | copy-start | bytes 6291460
  14.5 23.5 %copy-start.1 = (bf16[2,32,128,128]{3,2,1,0:T(8,128)(2,1)S(1)}, bf16[2,32,128,128]{3,2,1,0:T(8,128)(2,1)}, u32[]{:S(2)}) copy-start(bf16[2,32,128,128]{3,2,1,0:T(8,128)(2,1)} %df_ref.3) | copy-start | bytes 6291460
  14.5 23.5 %collective-permute-start.2 = (bf16[2,32,32,128]{3,2,1,0:T(8,128)(2,1)S(1)}, bf16[2,32,32,128]{3,2,1,0:T(8,128)(2,1)S(1)}, u32[]{:S(2)}, u32[]{:S(2)}) collective-permute-start(bf16[2,32,32,128]{3,2,1,0:T(8,128)(2,1)S(1)} %get-tuple-element.65), channel_id=1, source_target_pairs={{0,3},{1,2},{2,1},{3,0},{4,7},{5,6},{6,5},{7,4},{8,11},{9,10},{10,... | collective-permute-start | bytes 1572872 | tf_op jit(solution)/shard_map/ppermute | solution.py:237
  19.6 32.6 %collective-permute-start.6 = (bf16[2,32,32,128]{3,2,1,0:T(8,128)(2,1)S(1)}, bf16[2,32,32,128]{3,2,1,0:T(8,128)(2,1)S(1)}, u32[]{:S(2)}, u32[]{:S(2)}) collective-permute-start(bf16[2,32,32,128]{3,2,1,0:T(8,128)(2,1)S(1)} %get-tuple-element.71), channel_id=1, source_target_pairs={{0,1},{1,0},{2,3},{3,2},{4,5},{5,4},{6,7},{7,6},{8,9},{9,8},{10,11... | collective-permute-start | bytes 1572872 | tf_op jit(solution)/shard_map/ppermute | solution.py:237
  19.9 32.4 %collective-permute-start.7 = (bf16[2,32,32,128]{3,2,1,0:T(8,128)(2,1)S(1)}, bf16[2,32,32,128]{3,2,1,0:T(8,128)(2,1)S(1)}, u32[]{:S(2)}, u32[]{:S(2)}) collective-permute-start(bf16[2,32,32,128]{3,2,1,0:T(8,128)(2,1)S(1)} %get-tuple-element.72), channel_id=1, source_target_pairs={{0,2},{1,3},{2,0},{3,1},{4,6},{5,7},{6,4},{7,5},{8,10},{9,11},{10,... | collective-permute-start | bytes 1572872 | tf_op jit(solution)/shard_map/ppermute | solution.py:237
  21.8 38.7 %collective-permute-start.8 = (bf16[2,32,32,128]{3,2,1,0:T(8,128)(2,1)S(1)}, bf16[2,32,32,128]{3,2,1,0:T(8,128)(2,1)S(1)}, u32[]{:S(2)}, u32[]{:S(2)}) collective-permute-start(bf16[2,32,32,128]{3,2,1,0:T(8,128)(2,1)S(1)} %get-tuple-element.73), channel_id=1, source_target_pairs={{0,3},{1,2},{2,1},{3,0},{4,7},{5,6},{6,5},{7,4},{8,11},{9,10},{10,... | collective-permute-start | bytes 1572872 | tf_op jit(solution)/shard_map/ppermute | solution.py:237
  49.0 24.5 %collective-permute-start.12 = (bf16[4,32,16,128]{3,2,1,0:T(8,128)(2,1)S(1)}, bf16[4,32,16,128]{3,2,1,0:T(8,128)(2,1)S(1)}, u32[]{:S(2)}, u32[]{:S(2)}) collective-permute-start(bf16[4,32,16,128]{3,2,1,0:T(8,128)(2,1)S(1)} %get-tuple-element.81), channel_id=1, source_target_pairs={{0,4},{4,0},{8,12},{12,8},{16,20},{20,16},{24,28},{28,24},{1,5},{5... | collective-permute-start | bytes 1572872 | tf_op jit(solution)/shard_map/ppermute | solution.py:237
  50.7 23.1 %collective-permute-start.13 = (bf16[4,32,16,128]{3,2,1,0:T(8,128)(2,1)S(1)}, bf16[4,32,16,128]{3,2,1,0:T(8,128)(2,1)S(1)}, u32[]{:S(2)}, u32[]{:S(2)}) collective-permute-start(bf16[4,32,16,128]{3,2,1,0:T(8,128)(2,1)S(1)} %get-tuple-element.82), channel_id=1, source_target_pairs={{0,8},{4,12},{8,0},{12,4},{16,24},{20,28},{24,16},{28,20},{1,9},{5... | collective-permute-start | bytes 1572872 | tf_op jit(solution)/shard_map/ppermute | solution.py:237
  71.3 14.8 %collective-permute-start.10 = (bf16[2,32,32,128]{3,2,1,0:T(8,128)(2,1)S(1)}, bf16[2,32,32,128]{3,2,1,0:T(8,128)(2,1)S(1)}, u32[]{:S(2)}, u32[]{:S(2)}) collective-permute-start(bf16[2,32,32,128]{3,2,1,0:T(8,128)(2,1)S(1)} %get-tuple-element.76), channel_id=1, source_target_pairs={{0,2},{1,3},{2,0},{3,1},{4,6},{5,7},{6,4},{7,5},{8,10},{9,11},{10,... | collective-permute-start | bytes 1572872 | tf_op jit(solution)/shard_map/ppermute | solution.py:237
  73.0 23.5 %collective-permute-start.11 = (bf16[2,32,32,128]{3,2,1,0:T(8,128)(2,1)S(1)}, bf16[2,32,32,128]{3,2,1,0:T(8,128)(2,1)S(1)}, u32[]{:S(2)}, u32[]{:S(2)}) collective-permute-start(bf16[2,32,32,128]{3,2,1,0:T(8,128)(2,1)S(1)} %get-tuple-element.77), channel_id=1, source_target_pairs={{0,3},{1,2},{2,1},{3,0},{4,7},{5,6},{6,5},{7,4},{8,11},{9,10},{10,... | collective-permute-start | bytes 1572872 | tf_op jit(solution)/shard_map/ppermute | solution.py:237
  73.2 25.1 %collective-permute-start.9 = (bf16[2,32,32,128]{3,2,1,0:T(8,128)(2,1)S(1)}, bf16[2,32,32,128]{3,2,1,0:T(8,128)(2,1)S(1)}, u32[]{:S(2)}, u32[]{:S(2)}) collective-permute-start(bf16[2,32,32,128]{3,2,1,0:T(8,128)(2,1)S(1)} %get-tuple-element.75), channel_id=1, source_target_pairs={{0,1},{1,0},{2,3},{3,2},{4,5},{5,4},{6,7},{7,6},{8,9},{9,8},{10,11... | collective-permute-start | bytes 1572872 | tf_op jit(solution)/shard_map/ppermute | solution.py:237
  73.6 26.3 %collective-permute-start.3 = (bf16[2,32,32,128]{3,2,1,0:T(8,128)(2,1)S(1)}, bf16[2,32,32,128]{3,2,1,0:T(8,128)(2,1)S(1)}, u32[]{:S(2)}, u32[]{:S(2)}) collective-permute-start(bf16[2,32,32,128]{3,2,1,0:T(8,128)(2,1)S(1)} %get-tuple-element.67), channel_id=1, source_target_pairs={{0,1},{1,0},{2,3},{3,2},{4,5},{5,4},{6,7},{7,6},{8,9},{9,8},{10,11... | collective-permute-start | bytes 1572872 | tf_op jit(solution)/shard_map/ppermute | solution.py:237
  73.8 34.9 %collective-permute-start.4 = (bf16[2,32,32,128]{3,2,1,0:T(8,128)(2,1)S(1)}, bf16[2,32,32,128]{3,2,1,0:T(8,128)(2,1)S(1)}, u32[]{:S(2)}, u32[]{:S(2)}) collective-permute-start(bf16[2,32,32,128]{3,2,1,0:T(8,128)(2,1)S(1)} %get-tuple-element.68), channel_id=1, source_target_pairs={{0,2},{1,3},{2,0},{3,1},{4,6},{5,7},{6,4},{7,5},{8,10},{9,11},{10,... | collective-permute-start | bytes 1572872 | tf_op jit(solution)/shard_map/ppermute | solution.py:237
  75.4 43.4 %copy-start.7 = (bf16[128,4096]{1,0:T(8,128)(2,1)S(1)}, bf16[128,4096]{1,0:T(8,128)(2,1)}, u32[]{:S(2)}) copy-start(bf16[128,4096]{1,0:T(8,128)(2,1)} %x_ref.5) | copy-start | bytes 3145732
  86.1 32.7 %collective-permute-start.5 = (bf16[2,32,32,128]{3,2,1,0:T(8,128)(2,1)S(1)}, bf16[2,32,32,128]{3,2,1,0:T(8,128)(2,1)S(1)}, u32[]{:S(2)}, u32[]{:S(2)}) collective-permute-start(bf16[2,32,32,128]{3,2,1,0:T(8,128)(2,1)S(1)} %get-tuple-element.69), channel_id=1, source_target_pairs={{0,3},{1,2},{2,1},{3,0},{4,7},{5,6},{6,5},{7,4},{8,11},{9,10},{10,... | collective-permute-start | bytes 1572872 | tf_op jit(solution)/shard_map/ppermute | solution.py:237
  96.4 25.4 %collective-permute-start.16 = (bf16[4,32,16,128]{3,2,1,0:T(8,128)(2,1)S(1)}, bf16[4,32,16,128]{3,2,1,0:T(8,128)(2,1)S(1)}, u32[]{:S(2)}, u32[]{:S(2)}) collective-permute-start(bf16[4,32,16,128]{3,2,1,0:T(8,128)(2,1)S(1)} %get-tuple-element.90), channel_id=1, source_target_pairs={{0,4},{4,0},{8,12},{12,8},{16,20},{20,16},{24,28},{28,24},{1,5},{5... | collective-permute-start | bytes 1572872 | tf_op jit(solution)/shard_map/ppermute | solution.py:237
  98.3 23.5 %collective-permute-start.17 = (bf16[4,32,16,128]{3,2,1,0:T(8,128)(2,1)S(1)}, bf16[4,32,16,128]{3,2,1,0:T(8,128)(2,1)S(1)}, u32[]{:S(2)}, u32[]{:S(2)}) collective-permute-start(bf16[4,32,16,128]{3,2,1,0:T(8,128)(2,1)S(1)} %get-tuple-element.91), channel_id=1, source_target_pairs={{0,8},{4,12},{8,0},{12,4},{16,24},{20,28},{24,16},{28,20},{1,9},{5... | collective-permute-start | bytes 1572872 | tf_op jit(solution)/shard_map/ppermute | solution.py:237
  99.9 21.9 %collective-permute-start.15 = (bf16[2,32,16,128]{3,2,1,0:T(8,128)(2,1)S(1)}, bf16[2,32,16,128]{3,2,1,0:T(8,128)(2,1)S(1)}, u32[]{:S(2)}, u32[]{:S(2)}) collective-permute-start(bf16[2,32,16,128]{3,2,1,0:T(8,128)(2,1)S(1)} %slice_bitcast_fusion.14), channel_id=1, source_target_pairs={{0,4},{4,0},{8,12},{12,8},{16,20},{20,16},{24,28},{28,24},{1,5},{5... | collective-permute-start | bytes 786440 | tf_op jit(solution)/shard_map/ppermute | solution.py:237
  108.6 13.2 %collective-permute-start.14 = (bf16[2,32,16,128]{3,2,1,0:T(8,128)(2,1)S(1)}, bf16[2,32,16,128]{3,2,1,0:T(8,128)(2,1)S(1)}, u32[]{:S(2)}, u32[]{:S(2)}) collective-permute-start(bf16[2,32,16,128]{3,2,1,0:T(8,128)(2,1)S(1)} %slice_bitcast_fusion.15), channel_id=1, source_target_pairs={{0,8},{4,12},{8,0},{12,4},{16,24},{20,28},{24,16},{28,20},{1,9},{5... | collective-permute-start | bytes 786440 | tf_op jit(solution)/shard_map/ppermute | solution.py:237
  122.0 38.1 %copy-start.3 = (bf16[2,32,128,128]{3,2,1,0:T(8,128)(2,1)S(1)}, bf16[2,32,128,128]{3,2,1,0:T(8,128)(2,1)}, u32[]{:S(2)}) copy-start(bf16[2,32,128,128]{3,2,1,0:T(8,128)(2,1)} %dl_ref.5) | copy-start | bytes 6291460
  122.0 38.1 %copy-start.5 = (bf16[2,32,128,128]{3,2,1,0:T(8,128)(2,1)S(1)}, bf16[2,32,128,128]{3,2,1,0:T(8,128)(2,1)}, u32[]{:S(2)}) copy-start(bf16[2,32,128,128]{3,2,1,0:T(8,128)(2,1)} %ur_ref.5) | copy-start | bytes 6291460
  122.1 43.8 %collective-permute-start.21 = (bf16[2,32,16,128]{3,2,1,0:T(8,128)(2,1)S(1)}, bf16[2,32,16,128]{3,2,1,0:T(8,128)(2,1)S(1)}, u32[]{:S(2)}, u32[]{:S(2)}) collective-permute-start(bf16[2,32,16,128]{3,2,1,0:T(8,128)(2,1)S(1)} %slice_bitcast_fusion.10), channel_id=1, source_target_pairs={{0,4},{4,0},{8,12},{12,8},{16,20},{20,16},{24,28},{28,24},{1,5},{5... | collective-permute-start | bytes 786440 | tf_op jit(solution)/shard_map/ppermute | solution.py:237
  124.2 41.6 %collective-permute-start.20 = (bf16[2,32,16,128]{3,2,1,0:T(8,128)(2,1)S(1)}, bf16[2,32,16,128]{3,2,1,0:T(8,128)(2,1)S(1)}, u32[]{:S(2)}, u32[]{:S(2)}) collective-permute-start(bf16[2,32,16,128]{3,2,1,0:T(8,128)(2,1)S(1)} %slice_bitcast_fusion.11), channel_id=1, source_target_pairs={{0,8},{4,12},{8,0},{12,4},{16,24},{20,28},{24,16},{28,20},{1,9},{5... | collective-permute-start | bytes 786440 | tf_op jit(solution)/shard_map/ppermute | solution.py:237
  125.9 39.9 %collective-permute-start.22 = (bf16[4,64,16,128]{3,2,1,0:T(8,128)(2,1)S(1)}, bf16[4,64,16,128]{3,2,1,0:T(8,128)(2,1)S(1)}, u32[]{:S(2)}, u32[]{:S(2)}) collective-permute-start(bf16[4,64,16,128]{3,2,1,0:T(8,128)(2,1)S(1)} %get-tuple-element.103), channel_id=1, source_target_pairs={{0,4},{4,0},{8,12},{12,8},{16,20},{20,16},{24,28},{28,24},{1,5},{5... | collective-permute-start | bytes 3145736 | tf_op jit(solution)/shard_map/ppermute | solution.py:237
  126.5 39.4 %collective-permute-start.23 = (bf16[4,64,16,128]{3,2,1,0:T(8,128)(2,1)S(1)}, bf16[4,64,16,128]{3,2,1,0:T(8,128)(2,1)S(1)}, u32[]{:S(2)}, u32[]{:S(2)}) collective-permute-start(bf16[4,64,16,128]{3,2,1,0:T(8,128)(2,1)S(1)} %get-tuple-element.104), channel_id=1, source_target_pairs={{0,8},{4,12},{8,0},{12,4},{16,24},{20,28},{24,16},{28,20},{1,9},{5... | collective-permute-start | bytes 3145736 | tf_op jit(solution)/shard_map/ppermute | solution.py:237
  126.6 30.1 %collective-permute-start.19 = (bf16[1,32,16,128]{3,2,1,0:T(8,128)(2,1)S(1)}, bf16[1,32,16,128]{3,2,1,0:T(8,128)(2,1)S(1)}, u32[]{:S(2)}, u32[]{:S(2)}) collective-permute-start(bf16[1,32,16,128]{3,2,1,0:T(8,128)(2,1)S(1)} %slice_bitcast_fusion.22), channel_id=1, source_target_pairs={{0,16},{4,20},{8,24},{12,28},{16,0},{20,4},{24,8},{28,12},{1,17},{... | collective-permute-start | bytes 393224 | tf_op jit(solution)/shard_map/ppermute | solution.py:237
  156.7 9.1 %collective-permute-start.18 = (bf16[1,32,16,128]{3,2,1,0:T(8,128)(2,1)S(1)}, bf16[1,32,16,128]{3,2,1,0:T(8,128)(2,1)S(1)}, u32[]{:S(2)}, u32[]{:S(2)}) collective-permute-start(bf16[1,32,16,128]{3,2,1,0:T(8,128)(2,1)S(1)} %slice_bitcast_fusion.23), channel_id=1, source_target_pairs={{0,16},{4,20},{8,24},{12,28},{16,0},{20,4},{24,8},{28,12},{1,17},{... | collective-permute-start | bytes 393224 | tf_op jit(solution)/shard_map/ppermute | solution.py:237
  166.2 15.8 %collective-permute-start.27 = (bf16[2,64,16,128]{3,2,1,0:T(8,128)(2,1)S(1)}, bf16[2,64,16,128]{3,2,1,0:T(8,128)(2,1)S(1)}, u32[]{:S(2)}, u32[]{:S(2)}) collective-permute-start(bf16[2,64,16,128]{3,2,1,0:T(8,128)(2,1)S(1)} %slice_bitcast_fusion.1), channel_id=1, source_target_pairs={{0,4},{4,0},{8,12},{12,8},{16,20},{20,16},{24,28},{28,24},{1,5},{5... | collective-permute-start | bytes 1572872 | tf_op jit(solution)/shard_map/ppermute | solution.py:237
  167.1 15.9 %collective-permute-start.26 = (bf16[2,64,16,128]{3,2,1,0:T(8,128)(2,1)S(1)}, bf16[2,64,16,128]{3,2,1,0:T(8,128)(2,1)S(1)}, u32[]{:S(2)}, u32[]{:S(2)}) collective-permute-start(bf16[2,64,16,128]{3,2,1,0:T(8,128)(2,1)S(1)} %slice_bitcast_fusion.2), channel_id=1, source_target_pairs={{0,8},{4,12},{8,0},{12,4},{16,24},{20,28},{24,16},{28,20},{1,9},{5... | collective-permute-start | bytes 1572872 | tf_op jit(solution)/shard_map/ppermute | solution.py:237
  167.6 13.0 %collective-permute-start.25 = (bf16[1,32,16,128]{3,2,1,0:T(8,128)(2,1)S(1)}, bf16[1,32,16,128]{3,2,1,0:T(8,128)(2,1)S(1)}, u32[]{:S(2)}, u32[]{:S(2)}) collective-permute-start(bf16[1,32,16,128]{3,2,1,0:T(8,128)(2,1)S(1)} %slice_bitcast_fusion.20), channel_id=1, source_target_pairs={{0,16},{4,20},{8,24},{12,28},{16,0},{20,4},{24,8},{28,12},{1,17},{... | collective-permute-start | bytes 393224 | tf_op jit(solution)/shard_map/ppermute | solution.py:237
  170.2 11.9 %collective-permute-start.24 = (bf16[1,32,16,128]{3,2,1,0:T(8,128)(2,1)S(1)}, bf16[1,32,16,128]{3,2,1,0:T(8,128)(2,1)S(1)}, u32[]{:S(2)}, u32[]{:S(2)}) collective-permute-start(bf16[1,32,16,128]{3,2,1,0:T(8,128)(2,1)S(1)} %slice_bitcast_fusion.21), channel_id=1, source_target_pairs={{0,16},{4,20},{8,24},{12,28},{16,0},{20,4},{24,8},{28,12},{1,17},{... | collective-permute-start | bytes 393224 | tf_op jit(solution)/shard_map/ppermute | solution.py:237
  183.2 19.8 %collective-permute-start.29 = (bf16[1,64,16,128]{3,2,1,0:T(8,128)(2,1)S(1)}, bf16[1,64,16,128]{3,2,1,0:T(8,128)(2,1)S(1)}, u32[]{:S(2)}, u32[]{:S(2)}) collective-permute-start(bf16[1,64,16,128]{3,2,1,0:T(8,128)(2,1)S(1)} %slice_bitcast_fusion.5), channel_id=1, source_target_pairs={{0,16},{4,20},{8,24},{12,28},{16,0},{20,4},{24,8},{28,12},{1,17},{... | collective-permute-start | bytes 786440 | tf_op jit(solution)/shard_map/ppermute | solution.py:237
  185.8 20.9 %collective-permute-start.28 = (bf16[1,64,16,128]{3,2,1,0:T(8,128)(2,1)S(1)}, bf16[1,64,16,128]{3,2,1,0:T(8,128)(2,1)S(1)}, u32[]{:S(2)}, u32[]{:S(2)}) collective-permute-start(bf16[1,64,16,128]{3,2,1,0:T(8,128)(2,1)S(1)} %slice_bitcast_fusion.6), channel_id=1, source_target_pairs={{0,16},{4,20},{8,24},{12,28},{16,0},{20,4},{24,8},{28,12},{1,17},{... | collective-permute-start | bytes 786440 | tf_op jit(solution)/shard_map/ppermute | solution.py:237
